TPU v7x, 32 devices: a whole 2x2x4 slice. The times are simulated.
32 devices in a mesh: dp: 2 (over core), row: 4 (over y, x), col: 4 (over z).
Axes of the slice: x: 2, y: 2, z: 4, core: 2. Of those that a mesh axis runs over, the one named last changes fastest.
Arguments:
- tokens: bfloat16 [4096, 2048], P(('dp', 'row'), 'col'), may hold values from -6 to 6
- mixer_norm: float32 [2048], P('col'), may hold values from 0.1 to 1.9
- in_value: float32 [2048, 4096], P('col', 'row'), may hold values from -0.125 to 0.125
- in_gate: float32 [2048, 4096], P('col', 'row'), may hold values from -0.125 to 0.125
- conv_weight: float32 [4096, 4], P(('row', 'col')), may hold values from -3 to 3
- conv_bias: float32 [4096], P(('row', 'col')), may hold values from -4 to 4
- state_proj: float32 [4096, 160], P(('row', 'col')), may hold values from -0.25 to 0.25
- step_proj: float32 [128, 4096], P(None, ('row', 'col')), may hold values from -0.5 to 0.5
- step_bias: float32 [4096], P(('row', 'col')), may hold values from -5 to -2
- decay_log: float32 [4096, 16], P(('row', 'col')), may hold values from 0 to 2.8
- skip_gain: float32 [4096], P(('row', 'col')), may hold values from 0.5 to 1.5
- mixer_out: float32 [4096, 2048], P('row', 'col'), may hold values from -0.1875 to 0.1875
- feed_norm: float32 [2048], P('col'), may hold values from 0.1 to 1.9
- feed_gate: float32 [2048, 8192], P('col', 'row'), may hold values from -0.125 to 0.125
- feed_up: float32 [2048, 8192], P('col', 'row'), may hold values from -0.125 to 0.125
- feed_down: float32 [8192, 2048], P('row', 'col'), may hold values from -0.09375 to 0.09375
- out_grad: bfloat16 [4096, 2048], P(('dp', 'row'), 'col'), may hold values from -6 to 6
Outputs:
- output: bfloat16 [4096, 2048], P(('dp', 'row'), 'col')
- tokens_grad: float32 [4096, 2048], P(('dp', 'row'), 'col')
- mixer_norm_grad: float32 [2048], P('col')
- in_value_grad: float32 [2048, 4096], P('col', 'row')
- in_gate_grad: float32 [2048, 4096], P('col', 'row')
- conv_weight_grad: float32 [4096, 4], P(('row', 'col'))
- conv_bias_grad: float32 [4096], P(('row', 'col'))
- state_proj_grad: float32 [4096, 160], P(('row', 'col'))
- step_proj_grad: float32 [128, 4096], P(None, ('row', 'col'))
- step_bias_grad: float32 [4096], P(('row', 'col'))
- decay_log_grad: float32 [4096, 16], P(('row', 'col'))
- skip_gain_grad: float32 [4096], P(('row', 'col'))
- mixer_out_grad: float32 [4096, 2048], P('row', 'col')
- feed_norm_grad: float32 [2048], P('col')
- feed_gate_grad: float32 [2048, 8192], P('col', 'row')
- feed_up_grad: float32 [2048, 8192], P('col', 'row')
- feed_down_grad: float32 [8192, 2048], P('row', 'col')
All inputs are finite; a program needn't handle non-finite values.
Results may differ from a plain program's by a relative error of at most 0.02.
The roundings to bfloat16 on the way count: a program that leaves them out, or rounds other values in their place, can miss the bound.
Values may be sent and summed in bfloat16 or wider, within the bound.
No kernel may reach another device: no remote copies, remote signals or barrier semaphores. Data moves between devices by JAX's collectives and lax.ppermute only.
A program may use at most 384 MiB of HBM per device.

v0:
```python
import jax
import jax.numpy as jnp
from jax import lax
from jax.sharding import PartitionSpec as P

STATE = 16
CONV = 4
DT_RANK = 128
SEQ_LEN = 2048
SCAN_BLOCK = 16


epsilon = 1e-05
contract_first = (((0,), (0,)), ((), ()))
contract_cross = (((0,), (1,)), ((), ()))
contract_last = (((1,), (1,)), ((), ()))
contract_inner = (((1,), (0,)), ((), ()))


def for_sending(shard):

    def short(part):
        return part.astype(jnp.bfloat16) if part.dtype == jnp.float32 else part

    return jax.tree.map(short, shard)


def sigmoid_linear(values):
    return values * jax.nn.sigmoid(values)


def sigmoid_slope(values):
    logistic = jax.nn.sigmoid(values)
    return logistic * (1.0 + values * (1.0 - logistic))


def product(multiplicand, multiplier, dims):
    return lax.dot_general(multiplicand, multiplier, dims, preferred_element_type=jnp.float32)


def feature_total(values):
    return lax.psum(values, "col")


def token_block(values):
    return lax.all_gather(values, "row", axis=0, tiled=True)


def channel_block(items):
    return jax.tree.map(
        lambda part, own: part.astype(own.dtype),
        lax.all_gather(for_sending(items), "col", axis=0, tiled=True),
        items,
    )


def row_total(term_fn, row_count):
    return lax.psum_scatter(
        term_fn(jnp.int32(0), row_count * lax.axis_size("row")),
        "row",
        scatter_dimension=0,
        tiled=True,
    )


def projection_total(values):
    return lax.psum(values, ("row", "col"))


def norm_forward(values, weights):
    feature_count = values.shape[1] * lax.axis_size("col")
    squares = feature_total(jnp.sum(values * values, axis=1))
    inverse = lax.rsqrt(squares / feature_count + epsilon)
    scaled = values * inverse[:, None]
    return (scaled, inverse, (scaled * weights[None, :]).astype(jnp.bfloat16))


def norm_backward(upstream, scaled, inverse, weights):
    feature_count = scaled.shape[1] * lax.axis_size("col")
    weighted = upstream * weights[None, :]
    inner_mean = feature_total(jnp.sum(weighted * scaled, axis=1)) / feature_count
    return (
        inverse[:, None] * (weighted - scaled * inner_mean[:, None]),
        jnp.sum(upstream * scaled, axis=0),
    )


def project_out(blocks, weight_low, row_count):

    def partial_term(offset, amount):
        return product(blocks, weight_low, contract_first)

    return row_total(partial_term, row_count)


def conv_forward(values, weights, biases, sequences):
    channels = values.shape[0]
    grouped = values.reshape(channels, sequences, SEQ_LEN)
    padded = jnp.pad(grouped, ((0, 0), (0, 0), (CONV - 1, 0)))
    summed = jnp.zeros(grouped.shape, jnp.float32) + biases[:, None, None]
    for offset in range(CONV):
        summed = (
            summed + padded[:, :, offset : offset + SEQ_LEN] * weights[:, offset][:, None, None]
        )
    return (padded, summed.reshape(values.shape))


def conv_backward(upstream, padded, weights, sequences):
    channels = upstream.shape[0]
    grouped = upstream.reshape(channels, sequences, SEQ_LEN)
    grad_bias = jnp.sum(grouped, axis=(1, 2))
    grad_weight = jnp.stack(
        [
            jnp.sum(grouped * padded[:, :, offset : offset + SEQ_LEN], axis=(1, 2))
            for offset in range(CONV)
        ],
        axis=1,
    )
    trailing = jnp.pad(grouped, ((0, 0), (0, 0), (0, CONV - 1)))
    summed = jnp.zeros(grouped.shape, jnp.float32)
    for offset in range(CONV):
        start_at = CONV - 1 - offset
        summed = (
            summed
            + trailing[:, :, start_at : start_at + SEQ_LEN] * weights[:, offset][:, None, None]
        )
    return (summed.reshape(upstream.shape), grad_weight, grad_bias)


def by_step(values, block_len):
    leading = values.shape[:-1]
    blocked = values.reshape(leading + (values.shape[-1] // block_len, block_len))
    return jnp.moveaxis(blocked, -1, 0)


def from_steps(values):
    shifted = jnp.moveaxis(values, 0, -1)
    return shifted.reshape(shifted.shape[:-2] + (shifted.shape[-2] * shifted.shape[-1],))


def link_blocks(earlier, latter):
    return (earlier[0] * latter[0], latter[0] * earlier[1] + latter[1])


def block_entries(decays, states, sequences):
    full_shape = states.shape
    split_shape = full_shape[:2] + (sequences, full_shape[2] // sequences)
    _, reached = lax.associative_scan(
        link_blocks, (decays.reshape(split_shape), states.reshape(split_shape)), axis=3
    )
    zeroes = jnp.zeros(split_shape[:3] + (1,), jnp.float32)
    return jnp.concatenate([zeroes, reached[..., :-1]], axis=3).reshape(full_shape)


def scan_inputs(step_size, conv_act, in_coef, out_coef, decay_rate):
    block_len = SCAN_BLOCK
    return (
        decay_rate.T[:, :, None],
        by_step(step_size, block_len),
        by_step(step_size * conv_act, block_len),
        by_step(in_coef, block_len),
        by_step(out_coef, block_len),
    )


def advance(prepared, position, memory):
    decay_rates, step_blocks, drive_blocks, in_blocks, _ = prepared
    factor = jnp.exp(step_blocks[position][None] * decay_rates)
    return factor * memory + drive_blocks[position][None] * in_blocks[position][:, None, :]


def entry_states(prepared, sequences):
    decay_rates, step_blocks = (prepared[0], prepared[1])
    state_shape = (decay_rates.shape[0], decay_rates.shape[1], step_blocks.shape[2])
    local_state = lax.fori_loop(
        0,
        SCAN_BLOCK,
        lambda position, memory: advance(prepared, position, memory),
        jnp.zeros(state_shape, jnp.float32),
    )
    decays = jnp.exp(jnp.sum(step_blocks, axis=0)[None] * decay_rates)
    return block_entries(decays, local_state, sequences)


def scan_forward(prepared, entries):
    out_blocks = prepared[4]

    def emit_output(memory, position):
        memory = advance(prepared, position, memory)
        return (memory, jnp.sum(out_blocks[position][:, None, :] * memory, axis=0))

    _, outputs = lax.scan(emit_output, entries, jnp.arange(SCAN_BLOCK))
    return from_steps(outputs)


def scan_backward(prepared, entries, step_size, conv_act, upstream, sequences):
    decay_rates, step_blocks, drive_blocks, in_blocks, out_blocks = prepared
    block_len = SCAN_BLOCK

    def emit_state(memory, position):
        memory = advance(prepared, position, memory)
        return (memory, memory)

    _, states = lax.scan(emit_state, entries, jnp.arange(block_len))
    previous = jnp.concatenate([entries[None], states[:-1]], axis=0)
    channels = step_size.shape[0]
    grouped = step_size.reshape(channels, sequences, SEQ_LEN)
    next_step = jnp.concatenate(
        [grouped[:, :, 1:], jnp.zeros((channels, sequences, 1), jnp.float32)], axis=2
    ).reshape(step_size.shape)
    keepers = jnp.concatenate(
        [jnp.ones((sequences, SEQ_LEN - 1), jnp.float32), jnp.zeros((sequences, 1), jnp.float32)],
        axis=1,
    )
    next_steps = by_step(next_step, block_len)
    keep_steps = by_step(keepers, block_len)
    act_steps = by_step(conv_act, block_len)
    grad_steps = by_step(upstream, block_len)

    def recede(position, memory):
        factor = jnp.exp(next_steps[position][None] * decay_rates) * keep_steps[position][None]
        return factor * memory + out_blocks[position][:, None, :] * grad_steps[position][None]

    state_shape = states.shape[1:]
    local_grad = lax.fori_loop(
        0,
        block_len,
        lambda iteration, memory: recede(block_len - 1 - iteration, memory),
        jnp.zeros(state_shape, jnp.float32),
    )
    decays = (
        jnp.exp(jnp.sum(next_steps, axis=0)[None] * decay_rates)
        * jnp.prod(keep_steps, axis=0)[None]
    )
    incoming = block_entries(decays[..., ::-1], local_grad[..., ::-1], sequences)[..., ::-1]

    def gather_grads(memory, position):
        memory = recede(position, memory)
        factor = jnp.exp(step_blocks[position][None] * decay_rates)
        earlier_state = previous[position]
        grad_step = jnp.sum(
            memory
            * (
                decay_rates * factor * earlier_state
                + in_blocks[position][:, None, :] * act_steps[position][None]
            ),
            axis=0,
        )
        grad_rate = jnp.sum(memory * factor * earlier_state * step_blocks[position][None], axis=2)
        grad_in = jnp.sum(memory * drive_blocks[position][None], axis=1)
        grad_act = jnp.sum(memory * in_blocks[position][:, None, :], axis=0) * step_blocks[position]
        grad_out = jnp.sum(grad_steps[position][None] * states[position], axis=1)
        return (memory, (grad_step, grad_rate, grad_in, grad_act, grad_out))

    _, (grad_step, grad_rate, grad_in, grad_act, grad_out) = lax.scan(
        gather_grads, incoming, jnp.arange(block_len), reverse=True
    )
    return (
        from_steps(grad_step),
        jnp.sum(grad_rate, axis=0).T,
        from_steps(grad_in),
        from_steps(grad_act),
        from_steps(grad_out),
    )


def body(
    tokens,
    mixer_norm,
    in_value,
    in_gate,
    conv_weight,
    conv_bias,
    state_proj,
    step_proj,
    step_bias,
    decay_log,
    skip_gain,
    mixer_out,
    feed_norm,
    feed_gate,
    feed_up,
    feed_down,
    out_grad,
):
    value_low = in_value.astype(jnp.bfloat16)
    gate_in_low = in_gate.astype(jnp.bfloat16)
    state_low = state_proj.astype(jnp.bfloat16)
    step_weight = step_proj.astype(jnp.bfloat16)
    mixer_low = mixer_out.astype(jnp.bfloat16)
    feed_gate_low = feed_gate.astype(jnp.bfloat16)
    feed_up_low = feed_up.astype(jnp.bfloat16)
    feed_down_low = feed_down.astype(jnp.bfloat16)
    row_count = tokens.shape[0]
    inputs = tokens.astype(jnp.float32)
    scaled_first, inverse_first, normed_first = norm_forward(inputs, mixer_norm)
    normed_all = token_block(normed_first)
    sequences = normed_all.shape[0] // SEQ_LEN
    mixer_in, gate_in = (
        lax.psum_scatter(
            product(value_low, normed_all, contract_cross), "col", scatter_dimension=0, tiled=True
        ),
        lax.psum_scatter(
            product(gate_in_low, normed_all, contract_cross), "col", scatter_dimension=0, tiled=True
        ),
    )
    padded, conv_out = conv_forward(mixer_in, conv_weight, conv_bias, sequences)
    conv_act = sigmoid_linear(conv_out).astype(jnp.bfloat16)
    projected = projection_total(product(state_low, conv_act, contract_first))
    step_low = projected[:DT_RANK].astype(jnp.bfloat16)
    in_coef = projected[DT_RANK : DT_RANK + STATE]
    out_coef = projected[DT_RANK + STATE :]
    step_pre = product(step_weight, step_low, contract_first) + step_bias[:, None]
    step_size = jax.nn.softplus(step_pre)
    decay_rate = -jnp.exp(decay_log)
    act_float = conv_act.astype(jnp.float32)
    prepared = scan_inputs(step_size, act_float, in_coef, out_coef, decay_rate)
    entries = entry_states(prepared, sequences)
    scan_out = scan_forward(prepared, entries) + skip_gain[:, None] * act_float
    gate_act = sigmoid_linear(gate_in)
    gated = (scan_out * gate_act).astype(jnp.bfloat16)
    (gated_all,) = channel_block((gated,))
    middle = inputs + project_out(gated_all, mixer_low, row_count)
    scaled_second, inverse_second, normed_second = norm_forward(middle, feed_norm)
    normed_feed = token_block(normed_second)
    gate_pre, up_pre = (
        lax.psum_scatter(
            product(feed_gate_low, normed_feed, contract_cross).astype(jnp.bfloat16),
            "col",
            scatter_dimension=0,
            tiled=True,
        ).astype(jnp.float32),
        lax.psum_scatter(
            product(feed_up_low, normed_feed, contract_cross).astype(jnp.bfloat16),
            "col",
            scatter_dimension=0,
            tiled=True,
        ).astype(jnp.float32),
    )
    gate_swish = sigmoid_linear(gate_pre)
    hidden = (gate_swish * up_pre).astype(jnp.bfloat16)
    (hidden_all,) = channel_block((hidden,))
    output = (middle + project_out(hidden_all, feed_down_low, row_count)).astype(jnp.bfloat16)
    grad_all = token_block(out_grad)
    feed_down_grad = product(hidden_all, grad_all, contract_inner)
    row_block = feed_down_low
    hidden_back = lax.psum_scatter(
        product(row_block, grad_all, contract_last).astype(jnp.bfloat16),
        "col",
        scatter_dimension=0,
        tiled=True,
    ).astype(jnp.float32)
    gate_back = (hidden_back * up_pre * sigmoid_slope(gate_pre)).astype(jnp.bfloat16)
    up_back = (hidden_back * gate_swish).astype(jnp.bfloat16)
    gate_back_all, up_back_all = channel_block((gate_back, up_back))
    feed_gate_grad = product(normed_feed, gate_back_all, contract_cross)
    feed_up_grad = product(normed_feed, up_back_all, contract_cross)

    def feed_term(offset, amount):
        return product(gate_back_all, feed_gate_low, contract_cross) + product(
            up_back_all, feed_up_low, contract_cross
        )

    normed_back = row_total(feed_term, row_count)
    middle_norm, feed_norm_part = norm_backward(
        normed_back, scaled_second, inverse_second, feed_norm
    )
    middle_back = out_grad.astype(jnp.float32) + middle_norm
    middle_all = token_block(middle_back.astype(jnp.bfloat16))
    mixer_out_grad = product(gated_all, middle_all, contract_inner)
    row_block = mixer_low
    gated_back = lax.psum_scatter(
        product(row_block, middle_all, contract_last).astype(jnp.bfloat16),
        "col",
        scatter_dimension=0,
        tiled=True,
    ).astype(jnp.float32)
    scan_back = gated_back * gate_act
    gate_in_back = (gated_back * scan_out * sigmoid_slope(gate_in)).astype(jnp.bfloat16)
    entries_back = entry_states(prepared, sequences)
    step_back, decay_back, in_back, act_scan, out_back = scan_backward(
        prepared, entries_back, step_size, act_float, scan_back, sequences
    )
    skip_gain_grad = jnp.sum(scan_back * act_float, axis=1)
    act_scan = act_scan + skip_gain[:, None] * scan_back
    pre_back = step_back * jax.nn.sigmoid(step_pre)
    step_bias_grad = jnp.sum(pre_back, axis=1)
    pre_low = pre_back.astype(jnp.bfloat16)
    step_proj_grad = product(step_low, pre_low, contract_last)
    rank_back = product(step_weight, pre_low, contract_inner)
    proj_back = projection_total(jnp.concatenate([rank_back, in_back, out_back], axis=0)).astype(
        jnp.bfloat16
    )
    state_proj_grad = product(conv_act, proj_back, contract_last)
    act_back = act_scan + product(state_low, proj_back, contract_inner)
    conv_back = act_back * sigmoid_slope(conv_out)
    mixer_back, conv_weight_grad, conv_bias_grad = conv_backward(
        conv_back, padded, conv_weight, sequences
    )
    mixer_back_all, gate_in_back_all = channel_block(
        (mixer_back.astype(jnp.bfloat16), gate_in_back)
    )
    in_value_grad = product(normed_all, mixer_back_all, contract_cross)
    in_gate_grad = product(normed_all, gate_in_back_all, contract_cross)

    def mixer_term(offset, amount):
        return product(mixer_back_all, value_low, contract_cross) + product(
            gate_in_back_all, gate_in_low, contract_cross
        )

    normed_first_back = row_total(mixer_term, row_count)
    input_norm, mixer_norm_part = norm_backward(
        normed_first_back, scaled_first, inverse_first, mixer_norm
    )
    tokens_grad = middle_back + input_norm
    decay_log_grad = decay_back * decay_rate
    summed = lax.psum(
        (
            in_value_grad,
            in_gate_grad,
            conv_weight_grad,
            conv_bias_grad,
            state_proj_grad,
            step_proj_grad,
            step_bias_grad,
            decay_log_grad,
            skip_gain_grad,
            mixer_out_grad,
            feed_gate_grad,
            feed_up_grad,
            feed_down_grad,
        ),
        "dp",
    )
    gain_sums = lax.psum((mixer_norm_part, feed_norm_part), ("dp", "row"))
    return (
        output,
        tokens_grad,
        gain_sums[0],
        summed[0],
        summed[1],
        summed[2],
        summed[3],
        summed[4],
        summed[5],
        summed[6],
        summed[7],
        summed[8],
        summed[9],
        gain_sums[1],
        summed[10],
        summed[11],
        summed[12],
    )


def solution(mesh):
    return jax.shard_map(
        body,
        mesh=mesh,
        in_specs=(
            P(("dp", "row"), "col"),
            P("col"),
            P("col", "row"),
            P("col", "row"),
            P(("row", "col"), None),
            P(("row", "col")),
            P(("row", "col"), None),
            P(None, ("row", "col")),
            P(("row", "col")),
            P(("row", "col"), None),
            P(("row", "col")),
            P("row", "col"),
            P("col"),
            P("col", "row"),
            P("col", "row"),
            P("row", "col"),
            P(("dp", "row"), "col"),
        ),
        out_specs=(
            P(("dp", "row"), "col"),
            P(("dp", "row"), "col"),
            P("col"),
            P("col", "row"),
            P("col", "row"),
            P(("row", "col"), None),
            P(("row", "col")),
            P(("row", "col"), None),
            P(None, ("row", "col")),
            P(("row", "col")),
            P(("row", "col"), None),
            P(("row", "col")),
            P("row", "col"),
            P("col"),
            P("col", "row"),
            P("col", "row"),
            P("row", "col"),
        ),
        check_vma=False,
    )
```

profile of v0, /device:TPU:1, one launch (start us, length us, event | category | flops | bytes accessed | tf_op | source)
XLA Modules:
  0.0 2913.4 jit_solution(3945711383540398377)
XLA Ops:
  8.6 10.8 psum.147
  22.1 35.7 %all-gather.12.cloned.1.call-done = bf16[2048,512]{1,0:T(8,128)(2,1)} async-done(((bf16[512,512]{1,0:T(8,128)(2,1)}), bf16[2048,512]{1,0:T(8,128)(2,1)}) %all-gather.12.cloned.1.call-update) | async-done | bytes 2097168 | tf_op jit(solution)/shard_map/all_gather | solution.py:46
  65.8 143.8 %reduce-scatter.11.cloned.1.call-done = f32[256,2048]{0,1:T(8,128)} async-done(((f32[1024,2048]{0,1:T(8,128)}), f32[256,2048]{0,1:T(8,128)}) %reduce-scatter.11.cloned.1.call-update) | async-done | bytes 2097168 | tf_op jit(solution)/shard_map/reduce_scatter | solution.py:300
  225.6 106.0 %all-reduce.40.cloned.1.call-done = f32[160,2048]{1,0:T(8,128)} async-done(((f32[160,2048]{1,0:T(8,128)}), f32[160,2048]{1,0:T(8,128)}) %all-reduce.40.cloned.1.call-update) | async-done | bytes 1310736 | tf_op jit(solution)/shard_map/psum | solution.py:67
  351.0 40.6 %while.86 = (s32[]{:T(128)}, f32[16,256,128]{2,1,0:T(8,128)S(1)}, f32[16,256,128]{2,1,0:T(8,128)}, f32[16,256,1]{1,0,2:T(8,128)S(1)}, f32[16,256,128]{2,1,0:T(8,...) while((s32[]{:T(128)}, f32[16,256,128]{2,1,0:T(8,128)S(1)}, f32[16,256,128]{2,1,0:T(8,128)}, ...), condition=%wide.region_5.6_spmd.clone, body=%wide.region_4.5_spmd.clone.sunk | while | flops 2621443 | bytes 5021799 | solution.py:175
  420.5 8.7 pad.121
  440.9 15.6 pad.122
  456.5 15.6 pad.123
  474.9 30.4 %pad.242 = f32[16,256,1,128]{1,0,3,2:T(8,128)} pad(f32[16,256,1,64]{1,0,3,2:T(8,128)} %add.555, f32[]{:T(128)} %constant.182.clone.1), padding=0_0_0x0_0_0x0_0_0x1_0_1 | pad | bytes 3145732
  508.7 30.4 %pad.176 = f32[16,256,1,127]{1,0,3,2:T(8,128)} pad(f32[16,256,1,64]{1,0,3,2:T(8,128)} %pad_maximum_fusion.2, f32[]{:T(128)} %constant.182.clone.1), padding=0_0_0x0_0_0x0_0_0x0_0_1 | pad | bytes 3129348 | tf_op jit(solution)/shard_map/slice | solution.py:152
  551.4 92.1 %while.83 = (s32[]{:T(128)}, f32[16,256,128]{2,1,0:T(8,128)S(1)}, f32[16,256,128]{2,1,0:T(8,128)}, s32[16]{0:T(128)S(1)}, f32[16,256,128]{2,1,0:T(8,128)}, /*ind...) while((s32[]{:T(128)}, f32[16,256,128]{2,1,0:T(8,128)S(1)}, ...), condition=%wide.region_9.10_spmd, body=%wide.region_7.9_spmd.sunk | while | flops 3112965 | bytes 5440171 | solution.py:192
  650.3 80.3 %all-gather.14.cloned.1.call-done = bf16[1024,2048]{0,1:T(8,128)(2,1)} async-done(((bf16[256,2048]{0,1:T(8,128)(2,1)}), bf16[1024,2048]{0,1:T(8,128)(2,1)}) %all-gather.14.cloned.1.call-update) | async-done | bytes 4194320 | tf_op jit(solution)/shard_map/all_gather | solution.py:52
  738.7 50.1 %reduce-scatter.15.cloned.1.call-done = f32[512,512]{1,0:T(8,128)} async-done(((f32[2048,512]{1,0:T(8,128)}), f32[512,512]{1,0:T(8,128)}) %reduce-scatter.15.cloned.1.call-update) | async-done | bytes 1048592 | tf_op jit(solution)/shard_map/reduce_scatter | solution.py:58
  790.2 9.7 psum.149
  801.0 25.0 all-gather.20.cloned.1.call-done
  826.0 10.8 convolution_convert_fusion
  836.8 26.9 all-gather.16.cloned.1.call-done
  863.7 10.9 convert_bitcast_fusion.1
  874.9 10.7 convert_bitcast_fusion
  885.7 124.8 %reduce-scatter.23.cloned.1.call-done = bf16[512,2048]{0,1:T(8,128)(2,1)} async-done(((bf16[2048,2048]{0,1:T(8,128)(2,1)}), bf16[512,2048]{0,1:T(8,128)(2,1)}) %reduce-scatter.23.cloned.1.call-update) | async-done | bytes 2097168 | tf_op jit(solution)/shard_map/reduce_scatter | solution.py:347
  1010.4 147.4 %reduce-scatter.17.cloned.1.call-done = bf16[512,2048]{0,1:T(8,128)(2,1)} async-done(((bf16[2048,2048]{0,1:T(8,128)(2,1)}), bf16[512,2048]{0,1:T(8,128)(2,1)}) %reduce-scatter.17.cloned.1.call-update) | async-done | bytes 2097168 | tf_op jit(solution)/shard_map/reduce_scatter | solution.py:327
  1157.9 147.6 %reduce-scatter.19.cloned.1.call-done = bf16[512,2048]{0,1:T(8,128)(2,1)} async-done(((bf16[2048,2048]{0,1:T(8,128)(2,1)}), bf16[512,2048]{0,1:T(8,128)(2,1)}) %reduce-scatter.19.cloned.1.call-update) | async-done | bytes 2097168 | tf_op jit(solution)/shard_map/reduce_scatter | solution.py:333
  1313.5 150.1 %all-gather.22.cloned.1.call-done = bf16[2048,2048]{0,1:T(8,128)(2,1)} async-done(((bf16[512,2048]{0,1:T(8,128)(2,1)}), bf16[2048,2048]{0,1:T(8,128)(2,1)}) %all-gather.22.cloned.1.call-update) | async-done | bytes 8388624 | tf_op jit(solution)/shard_map/all_gather | solution.py:52
  1463.6 11.1 fusion.58
  1474.8 138.3 %all-gather.24.cloned.1.call-done = bf16[2048,2048]{0,1:T(8,128)(2,1)} async-done(((bf16[512,2048]{0,1:T(8,128)(2,1)}), bf16[2048,2048]{0,1:T(8,128)(2,1)}) %all-gather.24.cloned.1.call-update) | async-done | bytes 8388624 | tf_op jit(solution)/shard_map/all_gather | solution.py:52
  1613.0 12.4 convolution_add_fusion
  1625.6 50.8 %reduce-scatter.25.cloned.1.call-done = f32[512,512]{1,0:T(8,128)} async-done(((f32[2048,512]{1,0:T(8,128)}), f32[512,512]{1,0:T(8,128)}) %reduce-scatter.25.cloned.1.call-update) | async-done | bytes 1048592 | tf_op jit(solution)/shard_map/reduce_scatter | solution.py:58
  1678.6 9.6 psum.150
  1694.4 30.7 %all-gather.26.cloned.1.call-done = bf16[2048,512]{1,0:T(8,128)(2,1)} async-done(((bf16[512,512]{1,0:T(8,128)(2,1)}), bf16[2048,512]{1,0:T(8,128)(2,1)}) %all-gather.26.cloned.1.call-update) | async-done | bytes 2097168 | tf_op jit(solution)/shard_map/all_gather | solution.py:46
  1733.3 97.4 %while.84 = (s32[]{:T(128)}, f32[16,256,128]{2,1,0:T(8,128)S(1)}, f32[16,16,256,128]{3,2,1,0:T(8,128)}, s32[16]{0:T(128)S(1)}, f32[16,256,128]{2,1,0:T(8,128)}, ...) while((s32[]{:T(128)}, f32[16,256,128]{2,1,0:T(8,128)S(1)}, ...), condition=%wide.region_26.27_spmd, body=%wide.region_25.26_spmd.sunk | while | flops 2097157 | bytes 7119523 | solution.py:204
  1830.8 22.0 slice.548
  1863.6 22.2 pad_maximum_fusion
  1894.2 51.0 %while.87 = (s32[]{:T(128)}, f32[16,256,128]{2,1,0:T(8,128)S(1)}, f32[16,256,128]{2,1,0:T(8,128)}, f32[16,256,1]{1,0,2:T(8,128)S(1)}, f32[16,16,128]{2,1,0:T(8,1...) while((s32[]{:T(128)}, f32[16,256,128]{2,1,0:T(8,128)S(1)}, ...), condition=%wide.region_23.24_spmd.clone, body=%wide.region_22.23_spmd.clone.sunk | while | flops 3145735 | bytes 5023409 | solution.py:225
  1982.9 8.8 pad.135
  2001.8 15.6 pad.136
  2017.4 15.7 pad.137
  2038.8 23.1 pad.243
  2064.2 30.4 %pad.178 = f32[16,256,1,127]{1,0,3,2:T(8,128)} pad(f32[16,256,1,64]{1,0,3,2:T(8,128)} %pad_maximum_fusion.3, f32[]{:T(128)} %constant.182.clone.1), padding=0_0_0x0_0_0x0_0_0x0_0_1 | pad | bytes 3129348 | tf_op jit(solution)/shard_map/slice | solution.py:152
  2104.3 246.7 %while.85 = (s32[]{:T(128)}, f32[16,256,128]{2,1,0:T(8,128)S(1)}, f32[16,256,128]{2,1,0:T(8,128)}, f32[16,16,256]{2,1,0:T(8,128)}, f32[16,16,128]{2,1,0:T(8,128)...) while((s32[]{:T(128)}, f32[16,256,128]{2,1,0:T(8,128)S(1)}, ...), condition=%wide.region_33.34_spmd, body=%wide.region_27.0_spmd.sunk | while | flops 11493382 | bytes 11437883 | solution.py:255
  2371.0 89.2 %all-reduce.43 = bf16[160,2048]{1,0:T(8,128)(2,1)} all-reduce(f32[160,2048]{1,0:T(8,128)} %pad_maximum_fusion.1), channel_id=1, replica_groups=mesh['dp'=2,'row'=4,'col'=4] {'row','col'}, use_global_device_ids=true, to_apply=%region_34.35 | all-reduce | flops 327680 | bytes 1966080 | tf_op jit(solution)/shard_map/psum | solution.py:67
  2474.6 82.6 %all-gather.30.cloned.1.call-done = bf16[1024,1,2048]{0,2,1:T(8,128)(2,1)} async-done(((bf16[256,1,2048]{0,2,1:T(8,128)(2,1)}), bf16[1024,1,2048]{0,2,1:T(8,128)(2,1)}) %all-gather.30.cloned.1.call-update) | async-done | bytes 4194320 | tf_op jit(solution)/shard_map/all_gather | solution.py:52
  2565.7 141.0 %all-gather.18.cloned.1.call-done = bf16[2048,2048]{0,1:T(8,128)(2,1)} async-done(((bf16[512,2048]{0,1:T(8,128)(2,1)}), bf16[2048,2048]{0,1:T(8,128)(2,1)}) %all-gather.18.cloned.1.call-update) | async-done | bytes 8388624 | tf_op jit(solution)/shard_map/all_gather | solution.py:52
  2706.7 11.1 fusion.54
  2719.4 9.9 fusion.111
  2729.3 9.7 fusion.112
  2765.3 15.3 all-reduce.33
  2787.7 29.8 %reduce-scatter.21.cloned.1.call-done = f32[512,512]{1,0:T(8,128)} async-done(((f32[2048,512]{1,0:T(8,128)}), f32[512,512]{1,0:T(8,128)}) %reduce-scatter.21.cloned.1.call-update) | async-done | bytes 1048592 | tf_op jit(solution)/shard_map/reduce_scatter | solution.py:58
  2820.7 67.1 %all-reduce.42.cloned.1.call-done = (f32[512,1024]{1,0:T(8,128)}, f32[512,1024]{1,0:T(8,128)}, f32[256,160]{0,1:T(8,128)}, f32[128,256]{1,0:T(8,128)}, f32[1024,...) async-done(((f32[512,1024]{1,0:T(8,128)}, f32[512,1024]{1,0:T(8,128)}, f32[256,160]{0,1:T(8,128)}, f32[128,256]{1,0:T(8,128)}, ...) | async-done | bytes 19169296 | tf_op jit(solution)/shard_map/psum | solution.py:417
  (898 shorter events, 764.8 us)
Async XLA Ops:
  7.2 50.6 %copy-start.48 = (f32[512,1024]{1,0:T(8,128)S(1)}, f32[512,1024]{1,0:T(8,128)}, u32[]{:S(2)}) copy-start(f32[512,1024]{1,0:T(8,128)} %param.29) | copy-start | bytes 6291460
  7.2 50.6 %all-gather.12.cloned.1.call-start = ((), (), s32[]{:S(2)}) async-start(), calls=%async_computation.10 | async-start | bytes 2621440 | tf_op jit(solution)/shard_map/all_gather | solution.py:46
  22.0 187.5 %reduce-scatter.11.cloned.1.call-start = ((), (), s32[]{:S(2)}) async-start(), calls=%async_computation.11 | async-start | bytes 10485760 | tf_op jit(solution)/shard_map/reduce_scatter | solution.py:300
  65.1 144.5 %copy-start.96 = (f32[256]{0:T(256)S(1)}, f32[256]{0:T(256)}, u32[]{:S(2)}) copy-start(f32[256]{0:T(256)} %param.32) | copy-start | bytes 3076
  65.1 266.6 %all-reduce.40.cloned.1.call-start = ((), (), s32[]{:S(2)}) async-start(), calls=%async_computation.12 | async-start | bytes 2621440 | tf_op jit(solution)/shard_map/psum | solution.py:67
  65.7 150.0 %copy-start.83 = (f32[256,1]{0,1:T(1,128)}, f32[256,1]{0,1:T(1,128)S(1)}, u32[]{:S(2)}) copy-start(f32[256,1]{0,1:T(1,128)S(1)} %get-tuple-element.1176) | copy-start | bytes 3076
  65.7 150.0 %copy-start.85 = (f32[256,1]{0,1:T(1,128)}, f32[256,1]{0,1:T(1,128)S(1)}, u32[]{:S(2)}) copy-start(f32[256,1]{0,1:T(1,128)S(1)} %get-tuple-element.1177) | copy-start | bytes 3076
  65.8 150.0 %copy-start.87 = (f32[256,1]{0,1:T(1,128)}, f32[256,1]{0,1:T(1,128)S(1)}, u32[]{:S(2)}) copy-start(f32[256,1]{0,1:T(1,128)S(1)} %get-tuple-element.1178) | copy-start | bytes 3076
  65.8 149.9 %copy-start.89 = (f32[256,1]{0,1:T(1,128)}, f32[256,1]{0,1:T(1,128)S(1)}, u32[]{:S(2)}) copy-start(f32[256,1]{0,1:T(1,128)S(1)} %get-tuple-element.1179) | copy-start | bytes 3076
  217.3 428.5 %reduce-scatter.13.cloned.1.call-start = ((), (), s32[]{:S(2)}) async-start(), calls=%async_computation.13 | async-start | bytes 10485760 | tf_op jit(solution)/shard_map/reduce_scatter | solution.py:303
  217.4 176.3 %copy-start.66 = (f32[16,256]{1,0:T(8,128)}, f32[16,256]{1,0:T(8,128)S(1)}, u32[]{:S(2)}) copy-start(f32[16,256]{1,0:T(8,128)S(1)} %get-tuple-element.1174) | copy-start | bytes 49156
  225.3 106.3 %copy-start.56 = (f32[128,256]{1,0:T(8,128)S(1)}, f32[128,256]{1,0:T(8,128)}, u32[]{:S(2)}) copy-start(f32[128,256]{1,0:T(8,128)} %param.34) | copy-start | bytes 393220
  225.3 106.3 %copy-start.97 = (f32[256]{0:T(256)S(1)}, f32[256]{0:T(256)}, u32[]{:S(2)}) copy-start(f32[256]{0:T(256)} %param.35) | copy-start | bytes 3076
  225.4 505.3 %all-gather.14.cloned.1.call-start = ((), (), s32[]{:S(2)}) async-start(), calls=%async_computation.14 | async-start | bytes 5242880 | tf_op jit(solution)/shard_map/all_gather | solution.py:52
  414.0 16.5 copy-start.73
  507.6 31.4 %copy-start.27 = (f32[16,256,1,128]{1,0,3,2:T(8,128)S(1)}, f32[16,256,1,128]{1,0,3,2:T(8,128)}, u32[]{:S(2)}) copy-start(f32[16,256,1,128]{1,0,3,2:T(8,128)} %pad.242) | copy-start | bytes 6291460
  649.8 139.0 %reduce-scatter.15.cloned.1.call-start = ((), (), s32[]{:S(2)}) async-start(), calls=%async_computation.15 | async-start | bytes 5242880 | tf_op jit(solution)/shard_map/reduce_scatter | solution.py:58
  737.8 50.9 %copy-start.13 = (bf16[512,512]{1,0:T(8,128)(2,1)S(1)}, bf16[512,512]{1,0:T(8,128)(2,1)}, u32[]{:S(2)}) copy-start(bf16[512,512]{1,0:T(8,128)(2,1)} %param.27) | copy-start | bytes 1572868
  737.9 62.1 %copy-start.78 = (f32[512]{0:T(512)S(1)}, f32[512]{0:T(512)}, u32[]{:S(2)}) copy-start(f32[512]{0:T(512)} %param.39) | copy-start | bytes 6148
  737.9 88.1 %all-gather.20.cloned.1.call-start = ((), (), s32[]{:S(2)}) async-start(), calls=%async_computation.21 | async-start | bytes 2621440 | tf_op jit(solution)/shard_map/all_gather | solution.py:46
  738.6 125.1 %all-gather.16.cloned.1.call-start = ((), (), s32[]{:S(2)}) async-start(), calls=%async_computation.16 | async-start | bytes 2621440 | tf_op jit(solution)/shard_map/all_gather | solution.py:46
  790.2 898.0 %copy-start.4 = (f32[512,512]{1,0:T(8,128)}, f32[512,512]{1,0:T(8,128)S(1)}, u32[]{:S(2)}) copy-start(f32[512,512]{1,0:T(8,128)S(1)} %get-tuple-element.1108) | copy-start | bytes 3145732
  799.9 888.3 %copy-start.74 = (f32[512]{0:T(512)}, f32[512]{0:T(512)S(1)}, u32[]{:S(2)}) copy-start(f32[512]{0:T(512)S(1)} %add_rsqrt_fusion) | copy-start | bytes 6148
  800.9 209.5 %reduce-scatter.23.cloned.1.call-start = ((), (), s32[]{:S(2)}) async-start(), calls=%async_computation.22 | async-start | bytes 10485760 | tf_op jit(solution)/shard_map/reduce_scatter | solution.py:347
  836.8 321.1 %reduce-scatter.17.cloned.1.call-start = ((), (), s32[]{:S(2)}) async-start(), calls=%async_computation.17 | async-start | bytes 10485760 | tf_op jit(solution)/shard_map/reduce_scatter | solution.py:327
  874.7 430.8 %reduce-scatter.19.cloned.1.call-start = ((), (), s32[]{:S(2)}) async-start(), calls=%async_computation.18 | async-start | bytes 10485760 | tf_op jit(solution)/shard_map/reduce_scatter | solution.py:333
  885.6 578.0 %all-gather.22.cloned.1.call-start = ((), (), s32[]{:S(2)}) async-start(), calls=%async_computation.23 | async-start | bytes 10485760 | tf_op jit(solution)/shard_map/all_gather | solution.py:52
  1312.7 300.3 %all-gather.24.cloned.1.call-start = ((), (), s32[]{:S(2)}) async-start(), calls=%async_computation.24 | async-start | bytes 10485760 | tf_op jit(solution)/shard_map/all_gather | solution.py:52
  1313.5 362.9 %reduce-scatter.25.cloned.1.call-start = ((), (), s32[]{:S(2)}) async-start(), calls=%async_computation.25 | async-start | bytes 5242880 | tf_op jit(solution)/shard_map/reduce_scatter | solution.py:58
  1625.5 99.6 %all-gather.26.cloned.1.call-start = ((), (), s32[]{:S(2)}) async-start(), calls=%async_computation.26 | async-start | bytes 2621440 | tf_op jit(solution)/shard_map/all_gather | solution.py:46
  1690.4 195.3 %reduce-scatter.27.cloned.1.call-start = ((), (), s32[]{:S(2)}) async-start(), calls=%async_computation.27 | async-start | bytes 5242880 | tf_op jit(solution)/shard_map/reduce_scatter | solution.py:372
  1731.8 735.7 %all-gather.28.cloned.1.call-start = ((), (), s32[]{:S(2)}) async-start(), calls=%async_computation.28 | async-start | bytes 5242880 | tf_op jit(solution)/shard_map/all_gather | solution.py:52
  1830.8 22.0 copy-start.24
  1863.5 22.2 copy-start.8
  2100.3 456.9 %all-gather.30.cloned.1.call-start = ((), (), s32[]{:S(2)}) async-start(), calls=%async_computation.30 | async-start | bytes 5242880 | tf_op jit(solution)/shard_map/all_gather | solution.py:52
  2367.0 93.2 %copy-start.6 = (f32[256,2048]{0,1:T(8,128)S(1)}, f32[256,2048]{0,1:T(8,128)}, u32[]{:S(2)}) copy-start(f32[256,2048]{0,1:T(8,128)} %reduce-scatter.11.cloned.1.call-done) | copy-start | bytes 6291460
  2367.0 93.2 %copy-start.64 = (f32[256,160]{0,1:T(8,128)S(1)}, f32[256,160]{0,1:T(8,128)}, u32[]{:S(2)}) copy-start(f32[256,160]{0,1:T(8,128)} %param.33) | copy-start | bytes 491524
  2466.5 240.2 %all-gather.18.cloned.1.call-start = ((), (), s32[]{:S(2)}) async-start(), calls=%async_computation.19 | async-start | bytes 10485760 | tf_op jit(solution)/shard_map/all_gather | solution.py:52
  2467.2 296.4 %reduce-scatter.29.cloned.1.call-start = ((), (), s32[]{:S(2)}) async-start(), calls=%async_computation.29 | async-start | bytes 5242880 | tf_op jit(solution)/shard_map/reduce_scatter | solution.py:58
  2565.6 251.8 %reduce-scatter.21.cloned.1.call-start = ((), (), s32[]{:S(2)}) async-start(), calls=%async_computation.20 | async-start | bytes 5242880 | tf_op jit(solution)/shard_map/reduce_scatter | solution.py:58
  2717.8 170.0 %all-reduce.42.cloned.1.call-start = ((), (), s32[]{:S(2)}) async-start(), calls=%async_computation.31 | async-start | bytes 38338560 | tf_op jit(solution)/shard_map/psum | solution.py:417
  2719.4 19.5 slice-start
  2758.1 59.3 %copy-start.19 = (f32[512,512]{1,0:T(8,128)S(1)}, f32[512,512]{1,0:T(8,128)}, u32[]{:S(2)}) copy-start(f32[512,512]{1,0:T(8,128)} %reduce-scatter.25.cloned.1.call-done) | copy-start | bytes 3145732
  2758.1 59.3 %copy-start.75 = (f32[512]{0:T(512)S(1)}, f32[512]{0:T(512)}, u32[]{:S(2)}) copy-start(f32[512]{0:T(512)} %copy-done.74) | copy-start | bytes 6148
  2758.1 59.3 %copy-start.79 = (f32[512]{0:T(512)S(1)}, f32[512]{0:T(512)}, u32[]{:S(2)}) copy-start(f32[512]{0:T(512)} %param.39) | copy-start | bytes 6148
  2758.1 59.3 %copy-start.82 = (f32[512]{0:T(512)S(1)}, f32[512]{0:T(512)}, u32[]{:S(2)}) copy-start(f32[512]{0:T(512)} %copy-done.81) | copy-start | bytes 6148
  2758.2 59.3 %copy-start.5 = (f32[512,512]{1,0:T(8,128)S(1)}, f32[512,512]{1,0:T(8,128)}, u32[]{:S(2)}) copy-start(f32[512,512]{1,0:T(8,128)} %copy-done.4) | copy-start | bytes 3145732
  2758.2 59.3 %copy-start.32 = (bf16[512,512]{1,0:T(8,128)(2,1)S(1)}, bf16[512,512]{1,0:T(8,128)(2,1)}, u32[]{:S(2)}) copy-start(bf16[512,512]{1,0:T(8,128)(2,1)} %param.43) | copy-start | bytes 1572868
  (79 other events, 233.8 us)
Sparse Core Ops, SparseCore 0:
  22.1 35.5 all-gather.11
  65.2 144.2 reduce-scatter.10
  217.4 114.1 all-reduce.39
  334.0 144.3 reduce-scatter.12
  649.9 80.6 all-gather.13
  738.0 50.7 reduce-scatter.14
  790.6 35.3 all-gather.19
  828.4 35.2 all-gather.15
  866.1 144.2 reduce-scatter.22
  1012.6 145.1 reduce-scatter.16
  1160.2 145.1 reduce-scatter.18
  1312.8 150.7 all-gather.21
  1465.2 147.8 all-gather.23
  1625.6 50.6 reduce-scatter.24
  1690.6 34.5 all-gather.25
  1731.9 76.8 reduce-scatter.26
  2100.4 80.6 all-gather.27
  2466.6 90.5 all-gather.29
  2558.7 147.8 all-gather.17
  2710.1 50.6 reduce-scatter.28
  2764.6 52.8 reduce-scatter.20
  2821.9 65.8 all-reduce.41
where the time goes:
time: 2950 us; the launch traced here: 2910 us
  waiting for transfers between devices  1580 us (54%)
  local copies, waits for them, and re-layouts  626 us (21%)
  other arithmetic  290 us (10%)
  matrix products  157 us (5%)
  blocking collectives  146 us (5%)
  loops' own time  95 us (3%)
    all_gather x6, waiting for transfers between devices, channel_block(): lax.all_gather(for_sending(items), 'col', axis=0, tiled=True)  592 us
    dot_general x24, matrix products, product(): lax.dot_general(multiplicand, multiplier, dims, preferred_element_type=jn...  157 us
    reduce_scatter x1, waiting for transfers between devices, body(): lax.psum_scatter(product(feed_up_low, normed_feed, contract_cross).astype...  148 us
    reduce_scatter x1, waiting for transfers between devices, body(): lax.psum_scatter(product(feed_gate_low, normed_feed, contract_cross).asty...  147 us
    reduce_scatter x1, waiting for transfers between devices, body(): lax.psum_scatter(product(value_low, normed_all, contract_cross), 'col', s...  144 us
    reduce_scatter x4, waiting for transfers between devices, row_total(): lax.psum_scatter(term_fn(jnp.int32(0), row_count * lax.axis_size('row')),...  131 us
    reduce_scatter x1, waiting for transfers between devices, body(): lax.psum_scatter(product(row_block, grad_all, contract_last).astype(jnp.b...  125 us
    all_gather x4, waiting for transfers between devices, token_block(): return lax.all_gather(values, 'row', axis=0, tiled=True)  118 us
  transfers between devices with their start and end apart: 22, of which 18 were waited for; matrix products, arithmetic and copies ran while one was open for 26% of the time, Pallas kernels for 0%

commit v1 on v0

v1 whole, which is shorter than its diff:
```python
import jax
import jax.numpy as jnp
import numpy as np
from jax import lax
from jax.experimental import pallas as pl
from jax.experimental.pallas import tpu as pltpu
from jax.sharding import PartitionSpec as P

STATE = 16
CONV = 4
DT_RANK = 128
LANES = 128
ROWS = 8
LOG2E = np.float32(np.log2(np.e))
LN2 = np.float32(np.log(2.0))

epsilon = 1e-05
contract_first = (((0,), (0,)), ((), ()))
contract_last = (((1,), (1,)), ((), ()))
contract_inner = (((1,), (0,)), ((), ()))


def sigmoid_linear(values):
    return values * jax.nn.sigmoid(values)


def sigmoid_slope(values):
    logistic = jax.nn.sigmoid(values)
    return logistic * (1.0 + values * (1.0 - logistic))


def product(multiplicand, multiplier, dims=contract_inner):
    return lax.dot_general(multiplicand, multiplier, dims, preferred_element_type=jnp.float32)


def low(values):
    return values.astype(jnp.bfloat16)


def swap(values, axis, distance):
    return lax.ppermute(
        values, axis, [(i, i ^ distance) for i in range(lax.axis_size(axis))]
    )


def shift(values, axis, distance):
    size = lax.axis_size(axis)
    pairs = [(i, i + distance) for i in range(size) if 0 <= i + distance < size]
    return lax.ppermute(values, axis, pairs)


def gather_by_swaps(values, axis_name, axis):
    size, length = lax.axis_size(axis_name), values.shape[axis]
    index = lax.axis_index(axis_name)
    shape = list(values.shape)
    shape[axis] = size * length
    joined = jnp.zeros(shape, values.dtype)
    for distance in range(size):
        part = swap(values, axis_name, distance) if distance else values
        joined = lax.dynamic_update_slice_in_dim(
            joined, part, (index ^ distance) * length, axis
        )
    return joined


def scatter_by_swaps(values, axis_name, axis, dtype):
    size = lax.axis_size(axis_name)
    length = values.shape[axis] // size
    index = lax.axis_index(axis_name)

    def block(distance):
        return lax.dynamic_slice_in_dim(values, (index ^ distance) * length, length, axis)

    total = block(0).astype(jnp.float32)
    for distance in range(1, size):
        total = total + swap(block(distance).astype(dtype), axis_name, distance).astype(
            jnp.float32
        )
    return total


def row_gather(values):
    if lax.axis_size("row") == 4:
        return gather_by_swaps(values, "row", 0)
    return lax.all_gather(values, "row", axis=0, tiled=True)


def row_scatter(values):
    if lax.axis_size("row") == 4:
        return scatter_by_swaps(values, "row", 0, jnp.bfloat16)
    return lax.psum_scatter(low(values), "row", scatter_dimension=0, tiled=True).astype(
        jnp.float32
    )


def row_total(values):
    if lax.axis_size("row") == 4:
        total = values
        for distance in range(1, 4):
            total = total + swap(values, "row", distance)
        return total
    return lax.psum(values, "row")


def block_moves():
    rows, cols = lax.axis_size("row"), lax.axis_size("col")
    return [(k, (k % rows) * cols + k // rows) for k in range(rows * cols)]


def to_whole_features(values):
    split = lax.all_to_all(values, "col", split_axis=0, concat_axis=1, tiled=True)
    return lax.ppermute(split, ("row", "col"), block_moves())


def to_feature_blocks(values):
    back = [(target, source) for source, target in block_moves()]
    split = lax.ppermute(values, ("row", "col"), back)
    return lax.all_to_all(split, "col", split_axis=1, concat_axis=0, tiled=True)


def gather_weight(weight, axis):
    half = weight.shape[axis] // lax.axis_size("dp")
    part = lax.dynamic_slice_in_dim(weight, lax.axis_index("dp") * half, half, axis)
    return lax.all_gather(low(part), ("col", "dp"), axis=axis, tiled=True)


def scatter_gradient(gradient, axis):
    own = lax.psum_scatter(
        low(gradient), ("col", "dp"), scatter_dimension=axis, tiled=True
    )
    other = swap(own, "dp", 1)
    first = lax.axis_index("dp") == 0
    return jnp.concatenate(
        [jnp.where(first, own, other), jnp.where(first, other, own)], axis=axis
    ).astype(jnp.float32)


def fold_rows(parts):
    row = lax.broadcasted_iota(jnp.int32, parts[0].shape, 0)
    for half in (1, 2, 4):
        mask = (row & half) == 0
        parts = [
            jnp.where(mask, a, b) + pltpu.roll(jnp.where(mask, b, a), ROWS - half, 0)
            for a, b in zip(parts[0::2], parts[1::2])
        ]
    return parts[0]


def spread(ref, token):
    return ref[pl.ds(token, ROWS, stride=0), :]


class Tiling:
    def __init__(self, tokens, channels, backward):
        groups = channels // LANES
        self.tokens, self.channels = tokens, channels
        self.per = min(8, groups)
        self.block = min(128, tokens)
        self.blocks = tokens // self.block
        self.grid = (groups // self.per, self.blocks)
        self.width = self.per * LANES
        self.backward = backward
        self.lanes = [slice(g * LANES, (g + 1) * LANES) for g in range(self.per)]

    def at(self, b):
        return self.blocks - 1 - b if self.backward else b

    def narrow(self):
        def spec(i):
            return pl.BlockSpec(
                (self.block, LANES), lambda g, b: (self.at(b), g * self.per + i)
            )

        return [spec(i) for i in range(self.per)]

    def token_spec(self):
        return pl.BlockSpec((self.block, self.width), lambda g, b: (self.at(b), g))

    def wide_spec(self):
        return pl.BlockSpec((self.block, STATE, LANES), lambda g, b: (self.at(b), 0, 0))

    def state_spec(self):
        return pl.BlockSpec((STATE, self.width), lambda g, b: (0, g))

    def history_spec(self):
        return pl.BlockSpec((self.block, STATE, self.width), lambda g, b: (self.at(b), 0, g))

    def part_spec(self):
        return pl.BlockSpec(
            (1, self.block, STATE, LANES), lambda g, b: (g, self.at(b), 0, 0)
        )

    def load(self, ref):
        out = []
        for lanes in self.lanes:
            out += [ref[0:8, lanes], ref[8:16, lanes]]
        return tuple(out)

    def store(self, ref, values):
        for g, lanes in enumerate(self.lanes):
            ref[0:8, lanes] = values[2 * g]
            ref[8:16, lanes] = values[2 * g + 1]

    def call(self, kernel, name, in_specs, out_specs, out_shape, scratch=()):
        return pl.pallas_call(
            kernel,
            out_shape=out_shape,
            grid=self.grid,
            in_specs=in_specs,
            out_specs=out_specs,
            scratch_shapes=list(scratch),
            compiler_params=pltpu.CompilerParams(
                dimension_semantics=("arbitrary", "arbitrary"),
                vmem_limit_bytes=56 * 2**20,
            ),
            name=name,
        )


def pair(ref, token):
    return ref[token, 0:8, :], ref[token, 8:16, :]


def f32(*shape):
    return jax.ShapeDtypeStruct(shape, jnp.float32)


def chunk_state(step, drive, wide, rate, backward):
    t = Tiling(*step.shape, backward)
    per = t.per

    def kernel(*refs):
        step_refs, drive_refs = refs[:per], refs[per : 2 * per]
        wide_ref, rate_ref, state_ref = refs[2 * per :]

        @pl.when(pl.program_id(1) == 0)
        def _():
            state_ref[...] = jnp.zeros_like(state_ref)

        rates = t.load(rate_ref)

        def some(i, state):
            state = list(state)
            base = t.block - ROWS - i * ROWS if backward else i * ROWS
            for j in range(ROWS - 1, -1, -1) if backward else range(ROWS):
                token = base + j
                wides = pair(wide_ref, token)
                for g in range(per):
                    now = spread(step_refs[g], token)
                    force = spread(drive_refs[g], token)
                    for k in (0, 1):
                        m = 2 * g + k
                        factor = jnp.exp2(now * rates[m])
                        if backward:
                            state[m] = factor * (state[m] + force * wides[k])
                        else:
                            state[m] = factor * state[m] + force * wides[k]
            return tuple(state)

        t.store(
            state_ref, lax.fori_loop(0, t.block // ROWS, some, t.load(state_ref))
        )

    return t.call(
        kernel,
        "chunk_state_back" if backward else "chunk_state",
        t.narrow() + t.narrow() + [t.wide_spec(), t.state_spec()],
        t.state_spec(),
        f32(STATE, t.channels),
    )(*[step] * per, *[drive] * per, wide, rate)


def scan_forward(step, drive, in_wide, out_wide, rate, entry):
    t = Tiling(*step.shape, False)
    per = t.per

    def kernel(*refs):
        step_refs, drive_refs = refs[:per], refs[per : 2 * per]
        in_ref, out_ref, rate_ref, entry_ref, y_ref, before_ref, last_ref = refs[2 * per :]

        @pl.when(pl.program_id(1) == 0)
        def _():
            last_ref[...] = entry_ref[...]

        rates = t.load(rate_ref)

        def some(i, state):
            state = list(state)
            base = pl.multiple_of(i * ROWS, ROWS)
            sums = [[None] * ROWS for _ in range(per)]
            for j in range(ROWS):
                token = base + j
                ins, outs = pair(in_ref, token), pair(out_ref, token)
                for g in range(per):
                    now = spread(step_refs[g], token)
                    force = spread(drive_refs[g], token)
                    total = None
                    for k in (0, 1):
                        m = 2 * g + k
                        before_ref[token, 8 * k : 8 * k + 8, t.lanes[g]] = state[m]
                        state[m] = jnp.exp2(now * rates[m]) * state[m] + force * ins[k]
                        term = state[m] * outs[k]
                        total = term if total is None else total + term
                    sums[g][j] = total
            for g in range(per):
                y_ref[pl.ds(base, ROWS), t.lanes[g]] = fold_rows(sums[g])
            return tuple(state)

        t.store(last_ref, lax.fori_loop(0, t.block // ROWS, some, t.load(last_ref)))

    return t.call(
        kernel,
        "scan_forward",
        t.narrow()
        + t.narrow()
        + [t.wide_spec(), t.wide_spec(), t.state_spec(), t.state_spec()],
        (t.token_spec(), t.history_spec(), t.state_spec()),
        (
            f32(t.tokens, t.channels),
            f32(t.tokens, STATE, t.channels),
            f32(STATE, t.channels),
        ),
    )(*[step] * per, *[drive] * per, in_wide, out_wide, rate, entry)


def scan_backward(step, drive, back, in_wide, out_wide, rate, entry, before, last):
    t = Tiling(*step.shape, True)
    per = t.per

    def kernel(*refs):
        step_refs, drive_refs, back_refs = (refs[i * per : (i + 1) * per] for i in range(3))
        in_ref, out_ref, rate_ref, entry_ref, before_ref, last_ref = refs[
            3 * per : 3 * per + 6
        ]
        rate_sum_ref, in_sum_ref, decay_ref, in_part_ref, out_part_ref = refs[
            3 * per + 6 : 3 * per + 11
        ]
        carry_ref, state_ref = refs[3 * per + 11 :]

        @pl.when(pl.program_id(1) == 0)
        def _():
            decay_ref[...] = jnp.zeros_like(decay_ref)
            carry_ref[...] = entry_ref[...]
            state_ref[...] = last_ref[...]

        rates = t.load(rate_ref)

        def some(i, carried):
            carry, state, decay = (list(part) for part in carried)
            base = pl.multiple_of(t.block - ROWS - i * ROWS, ROWS)
            rate_sums = [[None] * ROWS for _ in range(per)]
            in_sums = [[None] * ROWS for _ in range(per)]
            for j in range(ROWS - 1, -1, -1):
                token = base + j
                ins, outs = pair(in_ref, token), pair(out_ref, token)
                in_part, out_part = [None, None], [None, None]
                for g in range(per):
                    now = spread(step_refs[g], token)
                    force = spread(drive_refs[g], token)
                    above = spread(back_refs[g], token)
                    by_rate, by_in = [None, None], [None, None]
                    for k in (0, 1):
                        m = 2 * g + k
                        earlier = before_ref[token, 8 * k : 8 * k + 8, t.lanes[g]]
                        grad = carry[m] + above * outs[k]
                        carry[m] = jnp.exp2(now * rates[m]) * grad
                        weighted = carry[m] * earlier
                        decay[m] = decay[m] + weighted * now
                        by_rate[k] = weighted * rates[m]
                        by_in[k] = grad * ins[k]
                        for parts, term in (
                            (in_part, grad * force),
                            (out_part, above * state[m]),
                        ):
                            parts[k] = term if parts[k] is None else parts[k] + term
                        state[m] = earlier
                    rate_sums[g][j] = by_rate[0] + by_rate[1]
                    in_sums[g][j] = by_in[0] + by_in[1]
                for k in (0, 1):
                    in_part_ref[0, token, 8 * k : 8 * k + 8, :] = in_part[k]
                    out_part_ref[0, token, 8 * k : 8 * k + 8, :] = out_part[k]
            for g in range(per):
                rate_sum_ref[pl.ds(base, ROWS), t.lanes[g]] = fold_rows(rate_sums[g])
                in_sum_ref[pl.ds(base, ROWS), t.lanes[g]] = fold_rows(in_sums[g])
            return tuple(carry), tuple(state), tuple(decay)

        carry, state, decay = lax.fori_loop(
            0,
            t.block // ROWS,
            some,
            (t.load(carry_ref), t.load(state_ref), t.load(decay_ref)),
        )
        t.store(carry_ref, carry)
        t.store(state_ref, state)
        t.store(decay_ref, decay)

    parts = f32(t.grid[0], t.tokens, STATE, LANES)
    rate_sum, in_sum, decay, in_part, out_part = t.call(
        kernel,
        "scan_backward",
        t.narrow()
        + t.narrow()
        + t.narrow()
        + [
            t.wide_spec(),
            t.wide_spec(),
            t.state_spec(),
            t.state_spec(),
            t.history_spec(),
            t.state_spec(),
        ],
        (t.token_spec(), t.token_spec(), t.state_spec(), t.part_spec(), t.part_spec()),
        (
            f32(t.tokens, t.channels),
            f32(t.tokens, t.channels),
            f32(STATE, t.channels),
            parts,
            parts,
        ),
        [pltpu.VMEM((STATE, t.width), jnp.float32)] * 2,
    )(
        *[step] * per,
        *[drive] * per,
        *[back] * per,
        in_wide,
        out_wide,
        rate,
        entry,
        before,
        last,
    )
    return rate_sum, in_sum, decay, jnp.sum(in_part, (0, 3)), jnp.sum(out_part, (0, 3))


def chunk_entry(state, step_total, rate, direction):
    packed = jnp.concatenate([state, step_total], axis=0)
    entry = None
    for distance in range(lax.axis_size("col") - 1, 0, -1):
        got = shift(packed, "col", direction * distance)
        if entry is None:
            entry = got[:STATE]
        else:
            entry = got[:STATE] + jnp.exp2(got[STATE:] * rate) * entry
    return entry


def widen(coefficients):
    return jnp.broadcast_to(coefficients[:, :, None], coefficients.shape + (LANES,))


def norm_forward(values, weights):
    inverse = lax.rsqrt(jnp.mean(values * values, axis=1, keepdims=True) + epsilon)
    scaled = values * inverse
    return scaled, inverse, low(scaled * weights)


def norm_backward(upstream, scaled, inverse, weights):
    weighted = upstream * weights
    inner_mean = jnp.mean(weighted * scaled, axis=1, keepdims=True)
    return (
        inverse * (weighted - scaled * inner_mean),
        jnp.sum(upstream * scaled, axis=0, keepdims=True),
    )


def body(
    tokens,
    mixer_norm,
    in_value,
    in_gate,
    conv_weight,
    conv_bias,
    state_proj,
    step_proj,
    step_bias,
    decay_log,
    skip_gain,
    mixer_out,
    feed_norm,
    feed_gate,
    feed_up,
    feed_down,
    out_grad,
):
    value_low = gather_weight(in_value, 0)
    gate_low = gather_weight(in_gate, 0)
    mixer_low = gather_weight(mixer_out, 1)
    feed_gate_low = gather_weight(feed_gate, 0)
    feed_up_low = gather_weight(feed_up, 0)
    feed_down_low = gather_weight(feed_down, 1)

    inputs = to_whole_features(tokens).astype(jnp.float32)
    out_back_low = to_whole_features(out_grad)
    gains = gather_by_swaps(jnp.stack([mixer_norm, feed_norm]), "col", 1)
    mixer_gain, feed_gain = gains[0:1], gains[1:2]
    packed = jnp.concatenate(
        [
            conv_weight.T,
            conv_bias[None],
            step_bias[None],
            skip_gain[None],
            decay_log.T,
        ],
        axis=0,
    )
    packed = gather_by_swaps(packed, "col", 1)
    taps = packed[:CONV]
    conv_bias_row, step_bias_row, skip_row = (
        packed[CONV + i : CONV + i + 1] for i in range(3)
    )
    decay_rate = -jnp.exp(packed[CONV + 3 :])
    state_low = gather_by_swaps(low(state_proj), "col", 0)
    step_weight = gather_by_swaps(low(step_proj), "col", 1)

    scaled_first, inverse_first, normed_first = norm_forward(inputs, mixer_gain)
    normed_all = row_gather(normed_first)
    grad_all = row_gather(out_back_low)
    mixer_in = product(normed_all, value_low)
    gate_in = product(normed_all, gate_low)
    count = mixer_in.shape[0]
    earlier = shift(mixer_in[-ROWS:], "col", 1)
    padded = jnp.concatenate([earlier[ROWS - CONV + 1 :], mixer_in], axis=0)
    conv_out = conv_bias_row + sum(
        padded[k : k + count] * taps[k : k + 1] for k in range(CONV)
    )
    conv_act = low(sigmoid_linear(conv_out))
    projected = row_total(product(conv_act, state_low))
    step_low = low(projected[:, :DT_RANK])
    in_wide = widen(projected[:, DT_RANK : DT_RANK + STATE])
    out_wide = widen(projected[:, DT_RANK + STATE :])
    step_pre = product(step_low, step_weight) + step_bias_row
    step_size = jax.nn.softplus(step_pre)
    act_float = conv_act.astype(jnp.float32)
    drive = step_size * act_float
    rate = decay_rate * LOG2E
    step_total = jnp.sum(step_size, axis=0, keepdims=True)
    handed = chunk_state(step_size, drive, in_wide, rate, False)
    entry = chunk_entry(handed, step_total, rate, 1)
    scanned, before, last = scan_forward(step_size, drive, in_wide, out_wide, rate, entry)
    scan_out = scanned + skip_row * act_float
    gate_act = sigmoid_linear(gate_in)
    gated = low(scan_out * gate_act)
    middle = inputs + row_scatter(product(gated, mixer_low))

    scaled_second, inverse_second, normed_second = norm_forward(middle, feed_gain)
    normed_feed = row_gather(normed_second)
    gate_pre = product(normed_feed, feed_gate_low)
    up_pre = product(normed_feed, feed_up_low)
    gate_swish = sigmoid_linear(gate_pre)
    hidden = low(gate_swish * up_pre)
    output = to_feature_blocks(low(middle + row_scatter(product(hidden, feed_down_low))))

    feed_down_grad = scatter_gradient(product(hidden, grad_all, contract_first), 1)
    hidden_back = product(grad_all, feed_down_low, contract_last)
    gate_back = low(hidden_back * up_pre * sigmoid_slope(gate_pre))
    up_back = low(hidden_back * gate_swish)
    feed_gate_grad = scatter_gradient(product(normed_feed, gate_back, contract_first), 0)
    feed_up_grad = scatter_gradient(product(normed_feed, up_back, contract_first), 0)
    normed_back = row_scatter(
        product(gate_back, feed_gate_low, contract_last)
        + product(up_back, feed_up_low, contract_last)
    )
    middle_norm, feed_norm_part = norm_backward(
        normed_back, scaled_second, inverse_second, feed_gain
    )
    middle_back = out_back_low.astype(jnp.float32) + middle_norm
    middle_all = row_gather(low(middle_back))

    mixer_out_grad = scatter_gradient(product(gated, middle_all, contract_first), 1)
    gated_back = product(middle_all, mixer_low, contract_last)
    scan_back = gated_back * gate_act
    gate_in_back = low(gated_back * scan_out * sigmoid_slope(gate_in))
    in_gate_grad = scatter_gradient(product(normed_all, gate_in_back, contract_first), 0)
    handed_back = chunk_state(step_size, scan_back, out_wide, rate, True)
    entry_back = chunk_entry(handed_back, step_total, rate, -1)
    rate_sum, in_sum, decay_sum, in_back, out_back = scan_backward(
        step_size, drive, scan_back, in_wide, out_wide, rate, entry_back, before, last
    )
    step_back = rate_sum * LN2 + act_float * in_sum
    act_scan = step_size * in_sum + skip_row * scan_back
    pre_back = step_back * jax.nn.sigmoid(step_pre)
    pre_low = low(pre_back)
    rank_back = product(pre_low, step_weight, contract_last)
    proj_back = low(row_total(jnp.concatenate([rank_back, in_back, out_back], axis=1)))
    act_back = act_scan + product(proj_back, state_low, contract_last)
    conv_back = act_back * sigmoid_slope(conv_out)
    later = shift(conv_back[:ROWS], "col", -1)
    trailing = jnp.concatenate([conv_back, later[: CONV - 1]], axis=0)
    mixer_back = low(
        sum(
            trailing[CONV - 1 - k : CONV - 1 - k + count] * taps[k : k + 1]
            for k in range(CONV)
        )
    )
    in_value_grad = scatter_gradient(product(normed_all, mixer_back, contract_first), 0)
    normed_first_back = row_scatter(
        product(mixer_back, value_low, contract_last)
        + product(gate_in_back, gate_low, contract_last)
    )
    input_norm, mixer_norm_part = norm_backward(
        normed_first_back, scaled_first, inverse_first, mixer_gain
    )
    tokens_grad = to_feature_blocks(low(middle_back + input_norm)).astype(jnp.float32)

    def over_tokens(values):
        return jnp.sum(values, axis=0, keepdims=True)

    packed_grad = jnp.concatenate(
        [over_tokens(conv_back * padded[k : k + count]) for k in range(CONV)]
        + [
            over_tokens(conv_back),
            over_tokens(pre_back),
            over_tokens(scan_back * act_float),
            decay_sum * decay_rate,
        ],
        axis=0,
    )

    def over_group(values, axis, dtype):
        own = scatter_by_swaps(values, "col", axis, dtype)
        return own + swap(own, "dp", 1)

    packed_grad = over_group(packed_grad, 1, jnp.float32)
    state_proj_grad = over_group(
        product(conv_act, proj_back, contract_first), 0, jnp.bfloat16
    )
    step_proj_grad = over_group(product(step_low, pre_low, contract_first), 1, jnp.bfloat16)
    gain_sums = scatter_by_swaps(
        jnp.concatenate([mixer_norm_part, feed_norm_part], axis=0), "col", 1, jnp.float32
    )
    gain_sums = lax.psum(gain_sums, ("dp", "row"))
    return (
        output,
        tokens_grad,
        gain_sums[0],
        in_value_grad,
        in_gate_grad,
        packed_grad[:CONV].T,
        packed_grad[CONV],
        state_proj_grad,
        step_proj_grad,
        packed_grad[CONV + 1],
        packed_grad[CONV + 3 :].T,
        packed_grad[CONV + 2],
        mixer_out_grad,
        gain_sums[1],
        feed_gate_grad,
        feed_up_grad,
        feed_down_grad,
    )


def solution(mesh):
    token_spec = P(("dp", "row"), "col")
    weight_in, weight_out = P("col", "row"), P("row", "col")
    channel, channel_rows = P(("row", "col")), P(("row", "col"), None)
    parameters = (
        P("col"),
        weight_in,
        weight_in,
        channel_rows,
        channel,
        channel_rows,
        P(None, ("row", "col")),
        channel,
        channel_rows,
        channel,
        weight_out,
        P("col"),
        weight_in,
        weight_in,
        weight_out,
    )
    return jax.shard_map(
        body,
        mesh=mesh,
        in_specs=(token_spec,) + parameters + (token_spec,),
        out_specs=(token_spec, token_spec) + parameters,
        check_vma=False,
    )
```

time: 2950 us -> 1130 us (0.38)
  waiting for transfers between devices: 1580 us -> 568 us
  local copies, waits for them, and re-layouts: 626 us -> 51.2 us
  other arithmetic: 290 us -> 50.5 us
  starting transfers between devices: 2.8 us -> 199 us
  blocking collectives: 146 us -> 23.8 us
  loops' own time: 95 us -> 0 us
  Pallas kernels: 0 us -> 68.1 us
    reduce_scatter x10 -> x6, waiting for transfers between devices: 694 us -> 137 us  [scatter_gradient(): lax.psum_scatter(low(gradient), ('col', 'dp'), scatter_dimension=axis, ti...]
    all_gather x10 -> x6, waiting for transfers between devices: 711 us -> 162 us  [gather_weight(): return lax.all_gather(low(part), ('col', 'dp'), axis=axis, tiled=True)]
    ppermute x0 -> x75, waiting for transfers between devices: none -> 247 us  [the longest x63 228 us: swap(): lax.ppermute(values, axis, [(i, i ^ distance) for i in range(lax.axis_siz...]
    mul x272 -> x0, local copies, waits for them, and re-layouts: 226 us -> none  [the longest x80 70.2 us: advance(): drive_blocks[position][None] * in_blocks[position][:, None, :]]
    psum x2 -> x0, waiting for transfers between devices: 173 us -> none  [the longest x1 106 us: projection_total(): return lax.psum(values, ('row', 'col'))]
    ppermute x0 -> x75, starting transfers between devices: none -> 163 us  [the longest x63 139 us: swap(): lax.ppermute(values, axis, [(i, i ^ distance) for i in range(lax.axis_siz...]
    psum x7 -> x1, blocking collectives: 146 us -> 23.8 us  [body(): gain_sums = lax.psum(gain_sums, ('dp', 'row'))]
    pad x20 -> x0, local copies, waits for them, and re-layouts: 115 us -> none  [block_entries(): lax.associative_scan(link_blocks, (decays.reshape(split_shape), states.re...]
  transfers between devices with their start and end apart: 22 -> 91, of which waited for: 18 -> 40; matrix products, arithmetic and copies ran while one was open for 26% -> 18% of each run, Pallas kernels for 0% -> 6%
where the time goes in v1:
time: 1130 us; the launch traced here: 1120 us
  waiting for transfers between devices  568 us (50%)
  starting transfers between devices  199 us (18%)
  matrix products  141 us (12%)
  Pallas kernels  68.1 us (6%)
  local copies, waits for them, and re-layouts  51.2 us (5%)
  other arithmetic  50.5 us (4%)
  blocking collectives  23.8 us (2%)
  between operations  15.9 us (1%)
    ppermute x63, waiting for transfers between devices, swap(): lax.ppermute(values, axis, [(i, i ^ distance) for i in range(lax.axis_siz...  228 us
    all_gather x6, waiting for transfers between devices, gather_weight(): return lax.all_gather(low(part), ('col', 'dp'), axis=axis, tiled=True)  162 us
    dot_general x24, matrix products, product(): lax.dot_general(multiplicand, multiplier, dims, preferred_element_type=jn...  141 us
    ppermute x63, starting transfers between devices, swap(): lax.ppermute(values, axis, [(i, i ^ distance) for i in range(lax.axis_siz...  139 us
    reduce_scatter x6, waiting for transfers between devices, scatter_gradient(): lax.psum_scatter(low(gradient), ('col', 'dp'), scatter_dimension=axis, ti...  137 us
    pallas_call x1, Pallas kernels, scan_backward(): t.call(kernel, 'scan_backward', t.narrow() + t.narrow() + t.narrow() + [t...  31.1 us
    all_to_all x2, starting transfers between devices, to_feature_blocks(): return lax.all_to_all(split, 'col', split_axis=1, concat_axis=0, tiled=True)  27.7 us
    psum x1, blocking collectives, body(): gain_sums = lax.psum(gain_sums, ('dp', 'row'))  23.8 us
  transfers between devices with their start and end apart: 91, of which 40 were waited for; matrix products, arithmetic and copies ran while one was open for 18% of the time, Pallas kernels for 6%

profile of v1, /device:TPU:1, one launch (start us, length us, event | category | flops | bytes accessed | tf_op | source)
XLA Modules:
  0.0 1117.0 jit_solution(16177664330657598358)
XLA Ops:
  38.8 22.1 %all-to-all-done = bf16[4,128,512]{2,1,0:T(8,128)(2,1)S(1)} async-done(((bf16[4,128,512]{2,1,0:T(8,128)(2,1)}), bf16[4,128,512]{2,1,0:T(8,128)(2,1)S(1)}, u32[]{:S(2)}, u32[]{:S(2)}) %all-to-all-start) | async-done | bytes 524320 | tf_op jit(solution)/shard_map/all_to_all | solution.py:111
  71.8 59.4 %collective-permute-start.7 = (bf16[128,2048]{1,0:T(8,128)(2,1)S(1)}, bf16[128,2048]{1,0:T(8,128)(2,1)S(1)}, u32[]{:S(2)}, u32[]{:S(2)}) collective-permute-start(bf16[128,2048]{1,0:T(8,128)(2,1)S(1)} %get-tuple-element.62), channel_id=1, source_target_pairs={{0,4},{4,0},{8,12},{12,8},{1,5},{5,1},{9,13},{13,9},{2,6},{6,2},{1... | collective-permute-start | bytes 1572872 | tf_op jit(solution)/shard_map/ppermute | solution.py:41
  131.9 7.2 collective-permute-done.11
  139.2 5.3 collective-permute-done.12
  155.3 5.2 fusion.59
  186.4 8.6 chunk_state.1
  203.4 6.0 collective-permute-start.22
  215.6 19.8 %scan_forward.1 = (f32[512,1024]{1,0:T(8,128)}, f32[512,16,1024]{2,1,0:T(8,128)}, f32[16,1024]{1,0:T(8,128)}) custom-call(f32[512,1024]{1,0:T(8,128)} %copy-done.2, f32[512,1024]{1,0:T(8,128)} %copy-done.2, f32[512,1024]{1,0:T(8,128)} %copy-done.2, f32[512,1024]{1,0:T(8,128)} %copy-done.2, f32[512,1024]{1,0:T(8,128)} %copy-done.2, f32[512,1024]{1,0:T(8,128)} %copy-done.2, ...), custom_call_target="tpu_custom_call" | custom-call | tf_op jit(solution)/shard_map/scan_forward/pallas_call | solution.py:311
  235.5 7.4 multiply_convert_fusion.4
  264.6 6.5 collective-permute-done.24
  283.5 5.2 collective-permute-done.27
  289.5 6.7 collective-permute-done.28
  297.0 12.3 %all-gather.15.cloned.1.call-done = bf16[2048,2048]{1,0:T(8,128)(2,1)} async-done(((bf16[256,2048]{1,0:T(8,128)(2,1)}), bf16[2048,2048]{1,0:T(8,128)(2,1)}) %all-gather.15.cloned.1.call-update) | async-done | bytes 8388624 | tf_op jit(solution)/shard_map/all_gather | solution.py:124
  309.4 10.5 fusion.63
  319.9 77.9 %all-gather.13.cloned.1.call-done = bf16[2048,2048]{1,0:T(8,128)(2,1)} async-done(((bf16[256,2048]{1,0:T(8,128)(2,1)}), bf16[2048,2048]{1,0:T(8,128)(2,1)}) %all-gather.13.cloned.1.call-update) | async-done | bytes 8388624 | tf_op jit(solution)/shard_map/all_gather | solution.py:124
  397.8 11.0 fusion.62
  408.8 71.5 %all-gather.17.cloned.1.call-done = bf16[2048,2048]{1,0:T(8,128)(2,1)} async-done(((bf16[2048,256]{1,0:T(8,128)(2,1)}), bf16[2048,2048]{1,0:T(8,128)(2,1)}) %all-gather.17.cloned.1.call-update) | async-done | bytes 8388624 | tf_op jit(solution)/shard_map/all_gather | solution.py:124
  480.3 13.7 %multiply_convert_fusion = (bf16[512,2048]{1,0:T(8,128)(2,1)S(1)}, bf16[512,2048]{1,0:T(8,128)(2,1)S(1)}, bf16[512,2048]{1,0:T(8,128)(2,1)}) fusion(f32[512,2048]{1,0:T(8,128)} %fusion.62, f32[512,2048]{1,0:T(8,128)} %fusion.63, bf16[512,2048]{1,0:T(8,128)(2,1)} %constant_dynamic-update-slice_fusion.4, bf16[2048,2048]{1,0:T(8,128)(2,1)} %all-gather.17.cloned.1.call-done), kind=kOutput, calls=%fused_computation.4 | convolution fusion | flops 4310695936 | bytes 25165824 | tf_op jit(solution)/shard_map/dot_general | solution.py:33
  494.0 8.5 fusion.65
  502.5 7.2 convolution_add_fusion
  512.6 10.6 collective-permute-done.37
  523.2 12.2 %collective-permute-done.39 = bf16[128,2048]{1,0:T(8,128)(2,1)S(1)} collective-permute-done((bf16[128,2048]{1,0:T(8,128)(2,1)S(1)}, bf16[128,2048]{1,0:T(8,128)(2,1)S(1)}, u32[]{:S(2)}, u32[]{:S(2)}) %collective-permute-start.39) | collective-permute-done | bytes 524320 | tf_op jit(solution)/shard_map/ppermute | solution.py:41
  540.4 9.1 collective-permute-done.40
  551.3 9.3 collective-permute-done.42
  566.6 8.7 fusion.14
  576.3 5.9 convolution_convert_fusion.4
  582.3 8.6 chunk_state_back.1
  595.7 9.0 collective-permute-done.44
  607.1 31.1 %scan_backward.1 = (f32[512,1024]{1,0:T(8,128)}, f32[512,1024]{1,0:T(8,128)}, f32[16,1024]{1,0:T(8,128)}, f32[1,512,16,128]{3,2,1,0:T(8,128)}, f32[1,512,16,128]{3,2,1,0:T(8,128)}) custom-call(f32[512,1024]{1,0:T(8,128)} %copy-done.2, f32[512,1024]{1,0:T(8,128)} %copy-done.2, f32[512,1024]{1,0:T(8,128)} %copy-done.2, f32[512,1024]{1,0:T(8,128)} %copy-done.2, ...), custom_call_target="tpu_custom_call" | custom-call | tf_op jit(solution)/shard_map/scan_backward/pallas_call | solution.py:398
  653.9 11.8 %collective-permute-done.47 = f32[512,160]{0,1:T(8,128)S(1)} collective-permute-done((f32[512,160]{0,1:T(8,128)S(1)}, f32[512,160]{0,1:T(8,128)S(1)}, u32[]{:S(2)}, u32[]{:S(2)}) %collective-permute-start.47) | collective-permute-done | bytes 327712 | tf_op jit(solution)/shard_map/ppermute | solution.py:41
  669.9 5.2 collective-permute-done.49
  677.1 6.0 convolution_convert_fusion.5
  683.5 10.1 convolution_convert_fusion.1
  693.7 10.2 convolution_convert_fusion.2
  704.0 10.2 convolution_convert_fusion
  714.3 8.0 fusion.64
  737.8 5.9 collective-permute-start.70
  747.0 7.3 collective-permute-done.52
  756.5 6.0 collective-permute-done.29
  762.5 14.3 %collective-permute-done.31 = bf16[128,2048]{1,0:T(8,128)(2,1)} collective-permute-done((bf16[128,2048]{1,0:T(8,128)(2,1)}, bf16[128,2048]{1,0:T(8,128)(2,1)}, u32[]{:S(2)}, u32[]{:S(2)}) %collective-permute-start.31) | collective-permute-done | bytes 524320 | tf_op jit(solution)/shard_map/ppermute | solution.py:41
  785.3 59.9 %collective-permute-done.59 = f32[23,256]{1,0:T(8,128)S(1)} collective-permute-done((f32[23,256]{1,0:T(8,128)S(1)}, f32[23,256]{1,0:T(8,128)S(1)}, u32[]{:S(2)}, u32[]{:S(2)}) %collective-permute-start.59) | collective-permute-done | bytes 23584 | tf_op jit(solution)/shard_map/ppermute | solution.py:41
  857.1 14.4 %collective-permute-done.63 = bf16[256,160]{0,1:T(8,128)(2,1)S(1)} collective-permute-done((bf16[256,160]{0,1:T(8,128)(2,1)S(1)}, bf16[256,160]{0,1:T(8,128)(2,1)S(1)}, u32[]{:S(2)}, u32[]{:S(2)}) %collective-permute-start.63) | collective-permute-done | bytes 81952 | tf_op jit(solution)/shard_map/ppermute | solution.py:41
  873.4 11.1 collective-permute-done.64
  886.8 24.2 %all-to-all-start.3 = ((bf16[128,4,512]{2,0,1:T(8,128)(2,1)}), bf16[128,4,512]{2,0,1:T(8,128)(2,1)S(1)}, u32[]{:S(2)}, u32[]{:S(2)}) async-start(bf16[128,4,512]{2,0,1:T(8,128)(2,1)} %bitcast.105), calls=%async_computation.3 | async-start | bytes 1048576 | tf_op jit(solution)/shard_map/all_to_all | solution.py:118
  919.0 6.9 collective-permute-done.55
  926.1 23.8 %psum.7 = f32[2,512]{1,0:T(2,128)S(1)} all-reduce(f32[2,512]{1,0:T(2,128)S(1)} %add_add_fusion.3), channel_id=1, replica_groups=mesh['dp'=2,'row'=4,'col'=4] {'dp','row'}, use_global_device_ids=true, to_apply=%region_9.10 | all-reduce | flops 1024 | bytes 8192 | tf_op jit(solution)/shard_map/psum | solution.py:631
  952.3 53.2 %reduce-scatter.13.cloned.1.call-done = bf16[256,2048]{1,0:T(8,128)(2,1)} async-done(((bf16[2048,2048]{1,0:T(8,128)(2,1)}), bf16[256,2048]{1,0:T(8,128)(2,1)}) %reduce-scatter.13.cloned.1.call-update) | async-done | bytes 1048592 | tf_op jit(solution)/shard_map/reduce_scatter | solution.py:128
  1012.5 83.4 %reduce-scatter.17.cloned.1.call-done = bf16[2048,256]{1,0:T(8,128)(2,1)} async-done(((bf16[2048,2048]{1,0:T(8,128)(2,1)}), bf16[2048,256]{1,0:T(8,128)(2,1)}) %reduce-scatter.17.cloned.1.call-update) | async-done | bytes 1048592 | tf_op jit(solution)/shard_map/reduce_scatter | solution.py:128
  (436 shorter events, 252.4 us)
Async XLA Ops:
  7.2 148.1 %all-gather.7.cloned.1.call-start = ((), (), s32[]{:S(2)}) async-start(), calls=%async_computation.10 | async-start | bytes 4718592 | tf_op jit(solution)/shard_map/all_gather | solution.py:124
  9.7 225.8 %all-gather.9.cloned.1.call-start = ((), (), s32[]{:S(2)}) async-start(), calls=%async_computation.11 | async-start | bytes 4718592 | tf_op jit(solution)/shard_map/all_gather | solution.py:124
  11.9 231.0 %all-gather.11.cloned.1.call-start = ((), (), s32[]{:S(2)}) async-start(), calls=%async_computation.12 | async-start | bytes 4718592 | tf_op jit(solution)/shard_map/all_gather | solution.py:124
  14.0 295.3 %all-gather.15.cloned.1.call-start = ((), (), s32[]{:S(2)}) async-start(), calls=%async_computation.14 | async-start | bytes 9437184 | tf_op jit(solution)/shard_map/all_gather | solution.py:124
  16.9 380.9 %all-gather.13.cloned.1.call-start = ((), (), s32[]{:S(2)}) async-start(), calls=%async_computation.13 | async-start | bytes 9437184 | tf_op jit(solution)/shard_map/all_gather | solution.py:124
  24.5 44.6 %collective-permute-start.3 = (f32[23,256]{1,0:T(8,128)S(1)}, f32[23,256]{1,0:T(8,128)S(1)}, u32[]{:S(2)}, u32[]{:S(2)}) collective-permute-start(f32[23,256]{1,0:T(8,128)S(1)} %concatenate.42), channel_id=1, source_target_pairs={{0,3},{1,2},{2,1},{3,0},{4,7},{5,6},{6,5},{7,4},{8,11},{9,10},{10,... | collective-permute-start | bytes 70664 | tf_op jit(solution)/shard_map/ppermute | solution.py:41
  27.8 41.2 %collective-permute-start.2 = (f32[23,256]{1,0:T(8,128)S(1)}, f32[23,256]{1,0:T(8,128)S(1)}, u32[]{:S(2)}, u32[]{:S(2)}) collective-permute-start(f32[23,256]{1,0:T(8,128)S(1)} %concatenate.42), channel_id=1, source_target_pairs={{0,2},{1,3},{2,0},{3,1},{4,6},{5,7},{6,4},{7,5},{8,10},{9,11},{10,... | collective-permute-start | bytes 70664 | tf_op jit(solution)/shard_map/ppermute | solution.py:41
  27.8 33.2 %all-to-all-start = ((bf16[4,128,512]{2,1,0:T(8,128)(2,1)}), bf16[4,128,512]{2,1,0:T(8,128)(2,1)S(1)}, u32[]{:S(2)}, u32[]{:S(2)}) async-start(bf16[4,128,512]{2,1,0:T(8,128)(2,1)} %bitcast), calls=%async_computation | async-start | bytes 1048576 | tf_op jit(solution)/shard_map/all_to_all | solution.py:111
  31.6 448.8 %all-gather.17.cloned.1.call-start = ((), (), s32[]{:S(2)}) async-start(), calls=%async_computation.15 | async-start | bytes 9437184 | tf_op jit(solution)/shard_map/all_gather | solution.py:124
  35.2 30.1 %collective-permute-start.1 = (f32[23,256]{1,0:T(8,128)S(1)}, f32[23,256]{1,0:T(8,128)S(1)}, u32[]{:S(2)}, u32[]{:S(2)}) collective-permute-start(f32[23,256]{1,0:T(8,128)S(1)} %concatenate.42), channel_id=1, source_target_pairs={{0,1},{1,0},{2,3},{3,2},{4,5},{5,4},{6,7},{7,6},{8,9},{9,8},{10,11... | collective-permute-start | bytes 70664 | tf_op jit(solution)/shard_map/ppermute | solution.py:41
  36.7 134.8 %collective-permute-start.18 = (bf16[128,256]{1,0:T(8,128)(2,1)}, bf16[128,256]{1,0:T(8,128)(2,1)}, u32[]{:S(2)}, u32[]{:S(2)}) collective-permute-start(bf16[128,256]{1,0:T(8,128)(2,1)} %get-tuple-element.64), channel_id=1, source_target_pairs={{0,2},{1,3},{2,0},{3,1},{4,6},{5,7},{6,4},{7,5},{8,10},{9,11},{10,... | collective-permute-start | bytes 196616 | tf_op jit(solution)/shard_map/ppermute | solution.py:41
  61.0 139.8 %all-to-all-start.2 = ((bf16[4,128,512]{2,1,0:T(8,128)(2,1)}), bf16[4,128,512]{2,1,0:T(8,128)(2,1)S(1)}, u32[]{:S(2)}, u32[]{:S(2)}) async-start(bf16[4,128,512]{2,1,0:T(8,128)(2,1)} %bitcast.23), calls=%async_computation.2 | async-start | bytes 1048576 | tf_op jit(solution)/shard_map/all_to_all | solution.py:111
  64.4 851.1 %reduce-scatter.11.cloned.1.call-start = ((), (), s32[]{:S(2)}) async-start(), calls=%async_computation.18 | async-start | bytes 4718592 | tf_op jit(solution)/shard_map/reduce_scatter | solution.py:128
  65.3 105.1 %collective-permute-start.17 = (bf16[128,256]{1,0:T(8,128)(2,1)}, bf16[128,256]{1,0:T(8,128)(2,1)}, u32[]{:S(2)}, u32[]{:S(2)}) collective-permute-start(bf16[128,256]{1,0:T(8,128)(2,1)} %get-tuple-element.64), channel_id=1, source_target_pairs={{0,1},{1,0},{2,3},{3,2},{4,5},{5,4},{6,7},{7,6},{8,9},{9,8},{10,11... | collective-permute-start | bytes 196616 | tf_op jit(solution)/shard_map/ppermute | solution.py:41
  68.9 70.2 %collective-permute-start.11 = (bf16[256,160]{0,1:T(8,128)(2,1)S(1)}, bf16[256,160]{0,1:T(8,128)(2,1)S(1)}, u32[]{:S(2)}, u32[]{:S(2)}) collective-permute-start(bf16[256,160]{0,1:T(8,128)(2,1)S(1)} %get-tuple-element.58), channel_id=1, source_target_pairs={{0,1},{1,0},{2,3},{3,2},{4,5},{5,4},{6,7},{7,6},{8,9},{9,8},{10,11... | collective-permute-start | bytes 245768 | tf_op jit(solution)/shard_map/ppermute | solution.py:41
  71.8 72.7 %collective-permute-start.7 = (bf16[128,2048]{1,0:T(8,128)(2,1)S(1)}, bf16[128,2048]{1,0:T(8,128)(2,1)S(1)}, u32[]{:S(2)}, u32[]{:S(2)}) collective-permute-start(bf16[128,2048]{1,0:T(8,128)(2,1)S(1)} %get-tuple-element.62), channel_id=1, source_target_pairs={{0,4},{4,0},{8,12},{12,8},{1,5},{5,1},{9,13},{13,9},{2,6},{6,2},{1... | collective-permute-start | bytes 1572872 | tf_op jit(solution)/shard_map/ppermute | solution.py:41
  144.5 27.9 %collective-permute-start.19 = (bf16[128,256]{1,0:T(8,128)(2,1)}, bf16[128,256]{1,0:T(8,128)(2,1)S(1)}, u32[]{:S(2)}, u32[]{:S(2)}) collective-permute-start(bf16[128,256]{1,0:T(8,128)(2,1)} %get-tuple-element.64), channel_id=1, source_target_pairs={{0,3},{1,2},{2,1},{3,0},{4,7},{5,6},{6,5},{7,4},{8,11},{9,10},{10,... | collective-permute-start | bytes 196616 | tf_op jit(solution)/shard_map/ppermute | solution.py:41
  201.7 50.3 %collective-permute-start.33 = (bf16[128,2048]{1,0:T(8,128)(2,1)}, bf16[128,2048]{1,0:T(8,128)(2,1)S(1)}, u32[]{:S(2)}, u32[]{:S(2)}) collective-permute-start(bf16[128,2048]{1,0:T(8,128)(2,1)} %bitcast.54), channel_id=1, source_target_pairs={{0,0},{1,4},{2,8},{3,12},{4,1},{5,5},{6,9},{7,13},{8,2},{9,6},{10,... | collective-permute-start | bytes 1572872 | tf_op jit(solution)/shard_map/ppermute | solution.py:112
  250.7 20.4 %collective-permute-start.24 = (bf16[128,2048]{1,0:T(8,128)(2,1)S(1)}, bf16[128,2048]{1,0:T(8,128)(2,1)S(1)}, u32[]{:S(2)}, u32[]{:S(2)}) collective-permute-start(bf16[128,2048]{1,0:T(8,128)(2,1)S(1)} %get-tuple-element.80), channel_id=1, source_target_pairs={{0,8},{4,12},{8,0},{12,4},{1,9},{5,13},{9,1},{13,5},{2,10},{6,14},... | collective-permute-start | bytes 1572872 | tf_op jit(solution)/shard_map/ppermute | solution.py:41
  251.9 29.1 %collective-permute-start.36 = (bf16[128,2048]{1,0:T(8,128)(2,1)S(1)}, bf16[128,2048]{1,0:T(8,128)(2,1)S(1)}, u32[]{:S(2)}, u32[]{:S(2)}) collective-permute-start(bf16[128,2048]{1,0:T(8,128)(2,1)S(1)} %collective-permute-done.33), channel_id=1, source_target_pairs={{0,12},{4,8},{8,4},{12,0},{1,13},{5,9},{9,5},{13,1},{2,14},{6,10},... | collective-permute-start | bytes 1572872 | tf_op jit(solution)/shard_map/ppermute | solution.py:41
  253.2 24.2 %collective-permute-start.35 = (bf16[128,2048]{1,0:T(8,128)(2,1)S(1)}, bf16[128,2048]{1,0:T(8,128)(2,1)S(1)}, u32[]{:S(2)}, u32[]{:S(2)}) collective-permute-start(bf16[128,2048]{1,0:T(8,128)(2,1)S(1)} %collective-permute-done.33), channel_id=1, source_target_pairs={{0,8},{4,12},{8,0},{12,4},{1,9},{5,13},{9,1},{13,5},{2,10},{6,14},... | collective-permute-start | bytes 1572872 | tf_op jit(solution)/shard_map/ppermute | solution.py:41
  511.1 24.3 %collective-permute-start.39 = (bf16[128,2048]{1,0:T(8,128)(2,1)S(1)}, bf16[128,2048]{1,0:T(8,128)(2,1)S(1)}, u32[]{:S(2)}, u32[]{:S(2)}) collective-permute-start(bf16[128,2048]{1,0:T(8,128)(2,1)S(1)} %get-tuple-element.73), channel_id=1, source_target_pairs={{0,12},{4,8},{8,4},{12,0},{1,13},{5,9},{9,5},{13,1},{2,14},{6,10},... | collective-permute-start | bytes 1572872 | tf_op jit(solution)/shard_map/ppermute | solution.py:41
  512.3 23.9 %collective-permute-start.38 = (bf16[128,2048]{1,0:T(8,128)(2,1)S(1)}, bf16[128,2048]{1,0:T(8,128)(2,1)S(1)}, u32[]{:S(2)}, u32[]{:S(2)}) collective-permute-start(bf16[128,2048]{1,0:T(8,128)(2,1)S(1)} %get-tuple-element.74), channel_id=1, source_target_pairs={{0,8},{4,12},{8,0},{12,4},{1,9},{5,13},{9,1},{13,5},{2,10},{6,14},... | collective-permute-start | bytes 1572872 | tf_op jit(solution)/shard_map/ppermute | solution.py:41
  539.2 21.5 %collective-permute-start.42 = (bf16[128,2048]{1,0:T(8,128)(2,1)S(1)}, bf16[128,2048]{1,0:T(8,128)(2,1)S(1)}, u32[]{:S(2)}, u32[]{:S(2)}) collective-permute-start(bf16[128,2048]{1,0:T(8,128)(2,1)S(1)} %get-tuple-element.49), channel_id=1, source_target_pairs={{0,12},{4,8},{8,4},{12,0},{1,13},{5,9},{9,5},{13,1},{2,14},{6,10},... | collective-permute-start | bytes 1572872 | tf_op jit(solution)/shard_map/ppermute | solution.py:41
  566.5 383.3 %reduce-scatter.9.cloned.1.call-start = ((), (), s32[]{:S(2)}) async-start(), calls=%async_computation.17 | async-start | bytes 4718592 | tf_op jit(solution)/shard_map/reduce_scatter | solution.py:128
  582.3 367.7 %reduce-scatter.7.cloned.1.call-start = ((), (), s32[]{:S(2)}) async-start(), calls=%async_computation.16 | async-start | bytes 4718592 | tf_op jit(solution)/shard_map/reduce_scatter | solution.py:128
  683.1 269.1 %reduce-scatter.15.cloned.1.call-start = ((), (), s32[]{:S(2)}) async-start(), calls=%async_computation.20 | async-start | bytes 9437184 | tf_op jit(solution)/shard_map/reduce_scatter | solution.py:128
  693.7 311.8 %reduce-scatter.13.cloned.1.call-start = ((), (), s32[]{:S(2)}) async-start(), calls=%async_computation.19 | async-start | bytes 9437184 | tf_op jit(solution)/shard_map/reduce_scatter | solution.py:128
  703.9 392.0 %reduce-scatter.17.cloned.1.call-start = ((), (), s32[]{:S(2)}) async-start(), calls=%async_computation.21 | async-start | bytes 9437184 | tf_op jit(solution)/shard_map/reduce_scatter | solution.py:128
  733.2 21.1 %collective-permute-start.52 = (bf16[128,2048]{1,0:T(8,128)(2,1)}, bf16[128,2048]{1,0:T(8,128)(2,1)}, u32[]{:S(2)}, u32[]{:S(2)}) collective-permute-start(bf16[128,2048]{1,0:T(8,128)(2,1)} %get-tuple-element.70), channel_id=1, source_target_pairs={{0,12},{4,8},{8,4},{12,0},{1,13},{5,9},{9,5},{13,1},{2,14},{6,10},... | collective-permute-start | bytes 1572872 | tf_op jit(solution)/shard_map/ppermute | solution.py:41
  736.6 25.9 %collective-permute-start.29 = (bf16[128,2048]{1,0:T(8,128)(2,1)}, bf16[128,2048]{1,0:T(8,128)(2,1)S(1)}, u32[]{:S(2)}, u32[]{:S(2)}) collective-permute-start(bf16[128,2048]{1,0:T(8,128)(2,1)} %get-tuple-element.75), channel_id=1, source_target_pairs={{0,4},{4,0},{8,12},{12,8},{1,5},{5,1},{9,13},{13,9},{2,6},{6,2},{1... | collective-permute-start | bytes 1572872 | tf_op jit(solution)/shard_map/ppermute | solution.py:41
  744.7 32.1 %collective-permute-start.31 = (bf16[128,2048]{1,0:T(8,128)(2,1)}, bf16[128,2048]{1,0:T(8,128)(2,1)}, u32[]{:S(2)}, u32[]{:S(2)}) collective-permute-start(bf16[128,2048]{1,0:T(8,128)(2,1)} %get-tuple-element.76), channel_id=1, source_target_pairs={{0,12},{4,8},{8,4},{12,0},{1,13},{5,9},{9,5},{13,1},{2,14},{6,10},... | collective-permute-start | bytes 1572872 | tf_op jit(solution)/shard_map/ppermute | solution.py:41
  746.8 30.0 %collective-permute-start.30 = (bf16[128,2048]{1,0:T(8,128)(2,1)}, bf16[128,2048]{1,0:T(8,128)(2,1)S(1)}, u32[]{:S(2)}, u32[]{:S(2)}) collective-permute-start(bf16[128,2048]{1,0:T(8,128)(2,1)} %get-tuple-element.77), channel_id=1, source_target_pairs={{0,8},{4,12},{8,0},{12,4},{1,9},{5,13},{9,1},{13,5},{2,10},{6,14},... | collective-permute-start | bytes 1572872 | tf_op jit(solution)/shard_map/ppermute | solution.py:41
  779.3 67.9 %collective-permute-start.32 = (bf16[128,2048]{1,0:T(8,128)(2,1)S(1)}, bf16[128,2048]{1,0:T(8,128)(2,1)S(1)}, u32[]{:S(2)}, u32[]{:S(2)}) collective-permute-start(bf16[128,2048]{1,0:T(8,128)(2,1)S(1)} %get-tuple-element.94), channel_id=1, source_target_pairs={{0,0},{4,1},{8,2},{12,3},{1,4},{5,5},{9,6},{13,7},{2,8},{6,9},{10,... | collective-permute-start | bytes 1572872 | tf_op jit(solution)/shard_map/ppermute | solution.py:117
  780.1 65.1 %collective-permute-start.59 = (f32[23,256]{1,0:T(8,128)S(1)}, f32[23,256]{1,0:T(8,128)S(1)}, u32[]{:S(2)}, u32[]{:S(2)}) collective-permute-start(f32[23,256]{1,0:T(8,128)S(1)} %get-tuple-element.103), channel_id=1, source_target_pairs={{0,1},{1,0},{2,3},{3,2},{4,5},{5,4},{6,7},{7,6},{8,9},{9,8},{10,11... | collective-permute-start | bytes 70664 | tf_op jit(solution)/shard_map/ppermute | solution.py:41
  783.7 61.5 %collective-permute-start.61 = (f32[23,256]{1,0:T(8,128)S(1)}, f32[23,256]{1,0:T(8,128)S(1)}, u32[]{:S(2)}, u32[]{:S(2)}) collective-permute-start(f32[23,256]{1,0:T(8,128)S(1)} %get-tuple-element.104), channel_id=1, source_target_pairs={{0,3},{1,2},{2,1},{3,0},{4,7},{5,6},{6,5},{7,4},{8,11},{9,10},{10,... | collective-permute-start | bytes 70664 | tf_op jit(solution)/shard_map/ppermute | solution.py:41
  784.4 60.8 %collective-permute-start.60 = (f32[23,256]{1,0:T(8,128)S(1)}, f32[23,256]{1,0:T(8,128)S(1)}, u32[]{:S(2)}, u32[]{:S(2)}) collective-permute-start(f32[23,256]{1,0:T(8,128)S(1)} %get-tuple-element.105), channel_id=1, source_target_pairs={{0,2},{1,3},{2,0},{3,1},{4,6},{5,7},{6,4},{7,5},{8,10},{9,11},{10,... | collective-permute-start | bytes 70664 | tf_op jit(solution)/shard_map/ppermute | solution.py:41
  848.1 38.7 %all-to-all-start.1 = ((bf16[128,4,512]{2,0,1:T(8,128)(2,1)}), bf16[128,4,512]{2,0,1:T(8,128)(2,1)S(1)}, u32[]{:S(2)}, u32[]{:S(2)}) async-start(bf16[128,4,512]{2,0,1:T(8,128)(2,1)} %bitcast.106), calls=%async_computation.1 | async-start | bytes 1048576 | tf_op jit(solution)/shard_map/all_to_all | solution.py:118
  853.1 20.3 %collective-permute-start.65 = (bf16[256,160]{0,1:T(8,128)(2,1)S(1)}, bf16[256,160]{0,1:T(8,128)(2,1)S(1)}, u32[]{:S(2)}, u32[]{:S(2)}) collective-permute-start(bf16[256,160]{0,1:T(8,128)(2,1)S(1)} %get-tuple-element.96), channel_id=1, source_target_pairs={{0,3},{1,2},{2,1},{3,0},{4,7},{5,6},{6,5},{7,4},{8,11},{9,10},{10,... | collective-permute-start | bytes 245768 | tf_op jit(solution)/shard_map/ppermute | solution.py:41
  855.2 29.3 %collective-permute-start.64 = (bf16[256,160]{0,1:T(8,128)(2,1)S(1)}, bf16[256,160]{0,1:T(8,128)(2,1)S(1)}, u32[]{:S(2)}, u32[]{:S(2)}) collective-permute-start(bf16[256,160]{0,1:T(8,128)(2,1)S(1)} %get-tuple-element.97), channel_id=1, source_target_pairs={{0,2},{1,3},{2,0},{3,1},{4,6},{5,7},{6,4},{7,5},{8,10},{9,11},{10,... | collective-permute-start | bytes 245768 | tf_op jit(solution)/shard_map/ppermute | solution.py:41
  855.2 30.7 %collective-permute-start.53 = (bf16[128,2048]{1,0:T(8,128)(2,1)S(1)}, bf16[128,2048]{1,0:T(8,128)(2,1)S(1)}, u32[]{:S(2)}, u32[]{:S(2)}) collective-permute-start(bf16[128,2048]{1,0:T(8,128)(2,1)S(1)} %get-tuple-element.93), channel_id=1, source_target_pairs={{0,0},{4,1},{8,2},{12,3},{1,4},{5,5},{9,6},{13,7},{2,8},{6,9},{10,... | collective-permute-start | bytes 1572872 | tf_op jit(solution)/shard_map/ppermute | solution.py:117
  884.6 32.9 %collective-permute-start.66 = (f32[256,160]{0,1:T(8,128)S(1)}, f32[256,160]{0,1:T(8,128)S(1)}, u32[]{:S(2)}, u32[]{:S(2)}) collective-permute-start(f32[256,160]{0,1:T(8,128)S(1)} %convert_add_fusion.3), channel_id=1, source_target_pairs={{0,16},{16,0},{1,17},{17,1},{2,18},{18,2},{3,19},{19,3},{4,20},{20... | collective-permute-start | bytes 491528 | tf_op jit(solution)/shard_map/ppermute | solution.py:41
  886.8 64.3 %all-to-all-start.3 = ((bf16[128,4,512]{2,0,1:T(8,128)(2,1)}), bf16[128,4,512]{2,0,1:T(8,128)(2,1)S(1)}, u32[]{:S(2)}, u32[]{:S(2)}) async-start(bf16[128,4,512]{2,0,1:T(8,128)(2,1)} %bitcast.105), calls=%async_computation.3 | async-start | bytes 1048576 | tf_op jit(solution)/shard_map/all_to_all | solution.py:118
  915.6 89.9 %collective-permute-start.71 = (bf16[1024,256]{1,0:T(8,128)(2,1)}, bf16[1024,256]{1,0:T(8,128)(2,1)S(1)}, u32[]{:S(2)}, u32[]{:S(2)}) collective-permute-start(bf16[1024,256]{1,0:T(8,128)(2,1)} %reduce-scatter.11.cloned.1.call-done), channel_id=1, source_target_pairs={{0,16},{16,0},{1,17},{17,1},{2,18},{18,2},{3,19},{19,3},{4,20},{20... | collective-permute-start | bytes 1572872 | tf_op jit(solution)/shard_map/ppermute | solution.py:41
  949.9 57.3 %collective-permute-start.58 = (bf16[256,1024]{1,0:T(8,128)(2,1)}, bf16[256,1024]{1,0:T(8,128)(2,1)S(1)}, u32[]{:S(2)}, u32[]{:S(2)}) collective-permute-start(bf16[256,1024]{1,0:T(8,128)(2,1)} %reduce-scatter.9.cloned.1.call-done), channel_id=1, source_target_pairs={{0,16},{16,0},{1,17},{17,1},{2,18},{18,2},{3,19},{19,3},{4,20},{20... | collective-permute-start | bytes 1572872 | tf_op jit(solution)/shard_map/ppermute | solution.py:41
  950.0 58.0 %collective-permute-start.57 = (bf16[256,1024]{1,0:T(8,128)(2,1)}, bf16[256,1024]{1,0:T(8,128)(2,1)}, u32[]{:S(2)}, u32[]{:S(2)}) collective-permute-start(bf16[256,1024]{1,0:T(8,128)(2,1)} %reduce-scatter.7.cloned.1.call-done), channel_id=1, source_target_pairs={{0,16},{16,0},{1,17},{17,1},{2,18},{18,2},{3,19},{19,3},{4,20},{20... | collective-permute-start | bytes 1572872 | tf_op jit(solution)/shard_map/ppermute | solution.py:41
  952.2 146.6 %collective-permute-start.73 = (bf16[256,2048]{1,0:T(8,128)(2,1)}, bf16[256,2048]{1,0:T(8,128)(2,1)}, u32[]{:S(2)}, u32[]{:S(2)}) collective-permute-start(bf16[256,2048]{1,0:T(8,128)(2,1)} %reduce-scatter.15.cloned.1.call-done), channel_id=1, source_target_pairs={{0,16},{16,0},{1,17},{17,1},{2,18},{18,2},{3,19},{19,3},{4,20},{20... | collective-permute-start | bytes 3145736 | tf_op jit(solution)/shard_map/ppermute | solution.py:41
  1005.5 93.3 %collective-permute-start.72 = (bf16[256,2048]{1,0:T(8,128)(2,1)}, bf16[256,2048]{1,0:T(8,128)(2,1)}, u32[]{:S(2)}, u32[]{:S(2)}) collective-permute-start(bf16[256,2048]{1,0:T(8,128)(2,1)} %reduce-scatter.13.cloned.1.call-done), channel_id=1, source_target_pairs={{0,16},{16,0},{1,17},{17,1},{2,18},{18,2},{3,19},{19,3},{4,20},{20... | collective-permute-start | bytes 3145736 | tf_op jit(solution)/shard_map/ppermute | solution.py:41
  (111 other events, 1768.3 us)
Sparse Core Ops, SparseCore 0:
  10.2 87.5 all-gather.6
  99.5 57.7 all-gather.8
  158.8 48.1 all-gather.10
  209.0 100.3 all-gather.14
  311.4 86.3 all-gather.12
  399.2 81.0 all-gather.16
  566.7 54.2 reduce-scatter.10
  623.3 49.4 reduce-scatter.8
  683.2 55.4 reduce-scatter.6
  740.9 172.3 reduce-scatter.14
  915.6 89.8 reduce-scatter.12
  1007.6 88.2 reduce-scatter.16

commit v2 on v1

--- a/solution.py
+++ b/solution.py
@@ -107,12 +107,35 @@
     return [(k, (k % rows) * cols + k // rows) for k in range(rows * cols)]
 
 
+def exchange(pieces, axis_name):
+    index = lax.axis_index(axis_name)
+    joined = jnp.zeros_like(pieces)
+    for distance in range(lax.axis_size(axis_name)):
+        part = lax.dynamic_slice_in_dim(pieces, index ^ distance, 1, 0)
+        if distance:
+            part = swap(part, axis_name, distance)
+        joined = lax.dynamic_update_slice_in_dim(joined, part, index ^ distance, 0)
+    return joined
+
+
 def to_whole_features(values):
+    rows, cols = lax.axis_size("row"), lax.axis_size("col")
+    if rows == cols:
+        count, features = values.shape
+        pieces = values.reshape(rows, count // rows, features)
+        pieces = exchange(exchange(pieces, "row"), "col")
+        return jnp.concatenate([pieces[c] for c in range(cols)], axis=1)
     split = lax.all_to_all(values, "col", split_axis=0, concat_axis=1, tiled=True)
     return lax.ppermute(split, ("row", "col"), block_moves())
 
 
 def to_feature_blocks(values):
+    rows, cols = lax.axis_size("row"), lax.axis_size("col")
+    if rows == cols:
+        count, features = values.shape[0], values.shape[1] // cols
+        pieces = jnp.stack([values[:, c * features : (c + 1) * features] for c in range(cols)])
+        pieces = exchange(exchange(pieces, "col"), "row")
+        return pieces.reshape(rows * count, features)
     back = [(target, source) for source, target in block_moves()]
     split = lax.ppermute(values, ("row", "col"), back)
     return lax.all_to_all(split, "col", split_axis=1, concat_axis=0, tiled=True)
@@ -124,10 +147,13 @@
     return lax.all_gather(low(part), ("col", "dp"), axis=axis, tiled=True)
 
 
-def scatter_gradient(gradient, axis):
-    own = lax.psum_scatter(
-        low(gradient), ("col", "dp"), scatter_dimension=axis, tiled=True
-    )
+def scatter_gradient(gradient, axis, after=None):
+    if after is not None:
+        gradient, _ = lax.optimization_barrier((gradient, after))
+    return lax.psum_scatter(gradient, ("col", "dp"), scatter_dimension=axis, tiled=True)
+
+
+def both_halves(own, axis):
     other = swap(own, "dp", 1)
     first = lax.axis_index("dp") == 0
     return jnp.concatenate(
@@ -482,11 +508,10 @@
     feed_down,
     out_grad,
 ):
-    value_low = gather_weight(in_value, 0)
-    gate_low = gather_weight(in_gate, 0)
+    channels, units = in_value.shape[1], feed_gate.shape[1]
+    in_low = gather_weight(jnp.concatenate([in_value, in_gate], axis=1), 0)
     mixer_low = gather_weight(mixer_out, 1)
-    feed_gate_low = gather_weight(feed_gate, 0)
-    feed_up_low = gather_weight(feed_up, 0)
+    feed_low = gather_weight(jnp.concatenate([feed_gate, feed_up], axis=1), 0)
     feed_down_low = gather_weight(feed_down, 1)
 
     inputs = to_whole_features(tokens).astype(jnp.float32)
@@ -515,8 +540,8 @@
     scaled_first, inverse_first, normed_first = norm_forward(inputs, mixer_gain)
     normed_all = row_gather(normed_first)
     grad_all = row_gather(out_back_low)
-    mixer_in = product(normed_all, value_low)
-    gate_in = product(normed_all, gate_low)
+    both_in = product(normed_all, in_low)
+    mixer_in, gate_in = both_in[:, :channels], both_in[:, channels:]
     count = mixer_in.shape[0]
     earlier = shift(mixer_in[-ROWS:], "col", 1)
     padded = jnp.concatenate([earlier[ROWS - CONV + 1 :], mixer_in], axis=0)
@@ -544,33 +569,40 @@
 
     scaled_second, inverse_second, normed_second = norm_forward(middle, feed_gain)
     normed_feed = row_gather(normed_second)
-    gate_pre = product(normed_feed, feed_gate_low)
-    up_pre = product(normed_feed, feed_up_low)
+    both_pre = product(normed_feed, feed_low)
+    gate_pre, up_pre = both_pre[:, :units], both_pre[:, units:]
     gate_swish = sigmoid_linear(gate_pre)
     hidden = low(gate_swish * up_pre)
+    feed_down_grad = low(product(hidden, grad_all, contract_first))
+    hidden, feed_down_grad = lax.optimization_barrier((hidden, feed_down_grad))
+    down_own = scatter_gradient(feed_down_grad, 1)
     output = to_feature_blocks(low(middle + row_scatter(product(hidden, feed_down_low))))
 
-    feed_down_grad = scatter_gradient(product(hidden, grad_all, contract_first), 1)
     hidden_back = product(grad_all, feed_down_low, contract_last)
     gate_back = low(hidden_back * up_pre * sigmoid_slope(gate_pre))
     up_back = low(hidden_back * gate_swish)
-    feed_gate_grad = scatter_gradient(product(normed_feed, gate_back, contract_first), 0)
-    feed_up_grad = scatter_gradient(product(normed_feed, up_back, contract_first), 0)
-    normed_back = row_scatter(
-        product(gate_back, feed_gate_low, contract_last)
-        + product(up_back, feed_up_low, contract_last)
-    )
+    both_back = jnp.concatenate([gate_back, up_back], axis=1)
+    feed_grad = low(product(normed_feed, both_back, contract_first))
+    both_back, feed_grad = lax.optimization_barrier((both_back, feed_grad))
+    feed_own = scatter_gradient(feed_grad, 0)
+    normed_back = row_scatter(product(both_back, feed_low, contract_last))
     middle_norm, feed_norm_part = norm_backward(
         normed_back, scaled_second, inverse_second, feed_gain
     )
     middle_back = out_back_low.astype(jnp.float32) + middle_norm
     middle_all = row_gather(low(middle_back))
 
-    mixer_out_grad = scatter_gradient(product(gated, middle_all, contract_first), 1)
+    mixer_out_grad = low(product(gated, middle_all, contract_first))
+    middle_all, mixer_out_grad = lax.optimization_barrier((middle_all, mixer_out_grad))
+    mixer_own = scatter_gradient(mixer_out_grad, 1)
+    mixer_out_grad = both_halves(mixer_own, 1)
     gated_back = product(middle_all, mixer_low, contract_last)
     scan_back = gated_back * gate_act
     gate_in_back = low(gated_back * scan_out * sigmoid_slope(gate_in))
-    in_gate_grad = scatter_gradient(product(normed_all, gate_in_back, contract_first), 0)
+    in_gate_grad = low(product(normed_all, gate_in_back, contract_first))
+    scan_back, in_gate_grad = lax.optimization_barrier((scan_back, in_gate_grad))
+    gate_own = scatter_gradient(in_gate_grad, 0)
+    in_gate_grad = both_halves(gate_own, 0)
     handed_back = chunk_state(step_size, scan_back, out_wide, rate, True)
     entry_back = chunk_entry(handed_back, step_total, rate, -1)
     rate_sum, in_sum, decay_sum, in_back, out_back = scan_backward(
@@ -592,11 +624,15 @@
             for k in range(CONV)
         )
     )
-    in_value_grad = scatter_gradient(product(normed_all, mixer_back, contract_first), 0)
-    normed_first_back = row_scatter(
-        product(mixer_back, value_low, contract_last)
-        + product(gate_in_back, gate_low, contract_last)
-    )
+    in_value_grad = low(product(normed_all, mixer_back, contract_first))
+    mixer_back, in_value_grad, down_own, feed_own = lax.optimization_barrier(
+        (mixer_back, in_value_grad, down_own, feed_own)
+    )
+    feed_down_grad = both_halves(down_own, 1)
+    feed_grad = both_halves(feed_own, 0)
+    in_value_grad = both_halves(scatter_gradient(in_value_grad, 0), 0)
+    both_in_back = jnp.concatenate([mixer_back, gate_in_back], axis=1)
+    normed_first_back = row_scatter(product(both_in_back, in_low, contract_last))
     input_norm, mixer_norm_part = norm_backward(
         normed_first_back, scaled_first, inverse_first, mixer_gain
     )
@@ -644,8 +680,8 @@
         packed_grad[CONV + 2],
         mixer_out_grad,
         gain_sums[1],
-        feed_gate_grad,
-        feed_up_grad,
+        feed_grad[:, :units],
+        feed_grad[:, units:],
         feed_down_grad,
     )
 

time: 1130 us -> 930 us (0.82)
  waiting for transfers between devices: 568 us -> 441 us
  starting transfers between devices: 199 us -> 119 us
  other arithmetic: 50.5 us -> 73.9 us
  matrix products: 141 us -> 127 us
    reduce_scatter x6 -> x5, waiting for transfers between devices: 137 us -> 83.5 us  [scatter_gradient(): lax.psum_scatter(gradient, ('col', 'dp'), scatter_dimension=axis, tiled=T...]
    ppermute x63 -> x86, waiting for transfers between devices: 228 us -> 192 us  [swap(): lax.ppermute(values, axis, [(i, i ^ distance) for i in range(lax.axis_siz...]
    ppermute x63 -> x86, starting transfers between devices: 139 us -> 104 us  [swap(): lax.ppermute(values, axis, [(i, i ^ distance) for i in range(lax.axis_siz...]
    all_to_all x4 -> x0, starting transfers between devices: 35 us -> none  [the longest x2 27.7 us: to_feature_blocks(): return lax.all_to_all(split, 'col', split_axis=1, concat_axis=0, tiled=True)]
    all_to_all x4 -> x0, waiting for transfers between devices: 22.1 us -> none  [the longest x2 22.1 us: to_whole_features(): lax.all_to_all(values, 'col', split_axis=0, concat_axis=1, tiled=True)]
    all_gather x6 -> x4, waiting for transfers between devices: 162 us -> 143 us  [gather_weight(): return lax.all_gather(low(part), ('col', 'dp'), axis=axis, tiled=True)]
    dot_general x24 -> x19, matrix products: 141 us -> 127 us  [product(): lax.dot_general(multiplicand, multiplier, dims, preferred_element_type=jn...]
  transfers between devices with their start and end apart: 91 -> 103, of which waited for: 40 -> 47; matrix products, arithmetic and copies ran while one was open for 18% -> 24% of each run, Pallas kernels for 6% -> 7%
where the time goes in v2:
time: 930 us; the launch traced here: 918 us
  waiting for transfers between devices  441 us (47%)
  matrix products  127 us (14%)
  starting transfers between devices  119 us (13%)
  other arithmetic  73.9 us (8%)
  Pallas kernels  68.2 us (7%)
  local copies, waits for them, and re-layouts  58.1 us (6%)
  between operations  16.3 us (2%)
  blocking collectives  15 us (2%)
    ppermute x86, waiting for transfers between devices, swap(): lax.ppermute(values, axis, [(i, i ^ distance) for i in range(lax.axis_siz...  192 us
    all_gather x4, waiting for transfers between devices, gather_weight(): return lax.all_gather(low(part), ('col', 'dp'), axis=axis, tiled=True)  143 us
    dot_general x19, matrix products, product(): lax.dot_general(multiplicand, multiplier, dims, preferred_element_type=jn...  127 us
    ppermute x86, starting transfers between devices, swap(): lax.ppermute(values, axis, [(i, i ^ distance) for i in range(lax.axis_siz...  104 us
    reduce_scatter x5, waiting for transfers between devices, scatter_gradient(): lax.psum_scatter(gradient, ('col', 'dp'), scatter_dimension=axis, tiled=T...  83.5 us
    pallas_call x1, Pallas kernels, scan_backward(): t.call(kernel, 'scan_backward', t.narrow() + t.narrow() + t.narrow() + [t...  31 us
    ppermute x8, waiting for transfers between devices, shift(): return lax.ppermute(values, axis, pairs)  21.3 us
    pallas_call x1, Pallas kernels, scan_forward(): t.call(kernel, 'scan_forward', t.narrow() + t.narrow() + [t.wide_spec(),...  20 us
  transfers between devices with their start and end apart: 103, of which 47 were waited for; matrix products, arithmetic and copies ran while one was open for 24% of the time, Pallas kernels for 7%

profile of v2, /device:TPU:1, one launch (start us, length us, event | category | flops | bytes accessed | tf_op | source)
XLA Modules:
  0.0 917.6 jit_solution(3914009329982867563)
XLA Ops:
  50.8 11.7 %collective-permute-done.3 = bf16[1,128,512]{2,1,0:T(8,128)(2,1)S(1)} collective-permute-done((bf16[1,128,512]{2,1,0:T(8,128)(2,1)S(1)}, bf16[1,128,512]{2,1,0:T(8,128)(2,1)S(1)}, u32[]{:S(2)}, u32[]{:S(2)}) %collective-permute-start.3) | collective-permute-done | bytes 131104 | tf_op jit(solution)/shard_map/ppermute | solution.py:41
  65.2 6.7 collective-permute-done.5
  82.0 11.2 %collective-permute-done.13 = bf16[128,2048]{1,0:T(8,128)(2,1)S(1)} collective-permute-done((bf16[128,2048]{1,0:T(8,128)(2,1)S(1)}, bf16[128,2048]{1,0:T(8,128)(2,1)S(1)}, u32[]{:S(2)}, u32[]{:S(2)}) %collective-permute-start.13) | collective-permute-done | bytes 524320 | tf_op jit(solution)/shard_map/ppermute | solution.py:41
  93.3 26.6 %all-gather.5.cloned.1.call-done = bf16[2048,2048]{1,0:T(8,128)(2,1)} async-done(((bf16[256,2048]{1,0:T(8,128)(2,1)}), bf16[2048,2048]{1,0:T(8,128)(2,1)}) %all-gather.5.cloned.1.call-update) | async-done | bytes 8388624 | tf_op jit(solution)/shard_map/all_gather | solution.py:147
  119.9 6.9 fusion.72
  141.8 8.5 collective-permute-done.20
  159.3 8.7 chunk_state.1
  177.5 6.6 collective-permute-done.25
  187.5 20.0 %scan_forward.1 = (f32[512,1024]{1,0:T(8,128)}, f32[512,16,1024]{2,1,0:T(8,128)}, f32[16,1024]{1,0:T(8,128)}) custom-call(f32[512,1024]{1,0:T(8,128)} %copy-done.2, f32[512,1024]{1,0:T(8,128)} %copy-done.2, f32[512,1024]{1,0:T(8,128)} %copy-done.2, f32[512,1024]{1,0:T(8,128)} %copy-done.2, f32[512,1024]{1,0:T(8,128)} %copy-done.2, f32[512,1024]{1,0:T(8,128)} %copy-done.2, ...), custom_call_target="tpu_custom_call" | custom-call | tf_op jit(solution)/shard_map/scan_forward/pallas_call | solution.py:337
  209.8 4.9 fusion.74
  222.5 5.6 collective-permute-done.28
  228.6 11.6 %collective-permute-done.30 = bf16[128,2048]{1,0:T(8,128)(2,1)S(1)} collective-permute-done((bf16[128,2048]{1,0:T(8,128)(2,1)S(1)}, bf16[128,2048]{1,0:T(8,128)(2,1)S(1)}, u32[]{:S(2)}, u32[]{:S(2)}) %collective-permute-start.30) | collective-permute-done | bytes 524320 | tf_op jit(solution)/shard_map/ppermute | solution.py:41
  243.4 7.2 collective-permute-done.40
  255.0 7.7 collective-permute-done.42
  263.6 9.5 %collective-permute-done.31 = bf16[128,2048]{1,0:T(8,128)(2,1)S(1)} collective-permute-done((bf16[128,2048]{1,0:T(8,128)(2,1)S(1)}, bf16[128,2048]{1,0:T(8,128)(2,1)S(1)}, u32[]{:S(2)}, u32[]{:S(2)}) %collective-permute-start.31) | collective-permute-done | bytes 524320 | tf_op jit(solution)/shard_map/ppermute | solution.py:41
  274.0 12.4 %collective-permute-done.32 = bf16[128,2048]{1,0:T(8,128)(2,1)S(1)} collective-permute-done((bf16[128,2048]{1,0:T(8,128)(2,1)S(1)}, bf16[128,2048]{1,0:T(8,128)(2,1)S(1)}, u32[]{:S(2)}, u32[]{:S(2)}) %collective-permute-start.32) | collective-permute-done | bytes 524320 | tf_op jit(solution)/shard_map/ppermute | solution.py:41
  288.1 49.8 %all-gather.9.cloned.1.call-done = bf16[2048,4096]{1,0:T(8,128)(2,1)} async-done(((bf16[256,4096]{1,0:T(8,128)(2,1)}), bf16[2048,4096]{1,0:T(8,128)(2,1)}) %all-gather.9.cloned.1.call-update) | async-done | bytes 16777232 | tf_op jit(solution)/shard_map/all_gather | solution.py:147
  337.9 15.5 %fusion.75 = f32[512,4096]{1,0:T(8,128)} fusion(bf16[512,2048]{1,0:T(8,128)(2,1)} %constant_dynamic-update-slice_fusion.26, bf16[2048,4096]{1,0:T(8,128)(2,1)} %all-gather.9.cloned.1.call-done), kind=kOutput, calls=%fused_computation.299 | convolution fusion | flops 8589934592 | bytes 27262976 | tf_op jit(solution)/shard_map/dot_general | solution.py:33
  353.4 66.7 %all-gather.11.cloned.1.call-done = bf16[2048,2048]{1,0:T(8,128)(2,1)} async-done(((bf16[2048,256]{1,0:T(8,128)(2,1)}), bf16[2048,2048]{1,0:T(8,128)(2,1)}) %all-gather.11.cloned.1.call-update) | async-done | bytes 8388624 | tf_op jit(solution)/shard_map/all_gather | solution.py:147
  420.1 14.3 %multiply_convert_fusion.1 = (bf16[512,2048]{1,0:T(8,128)(2,1)}, bf16[512,2048]{1,0:T(8,128)(2,1)}, bf16[512,2048]{1,0:T(8,128)(2,1)S(1)}) fusion(f32[512,4096]{1,0:T(8,128)} %fusion.75, bf16[512,2048]{1,0:T(8,128)(2,1)} %constant_dynamic-update-slice_fusion.16, bf16[2048,2048]{1,0:T(8,128)(2,1)} %all-gather.11.cloned.1.call-done), kind=kOutput, calls=%fused_computation.12 | convolution fusion | flops 4310695936 | bytes 25165824 | tf_op jit(solution)/shard_map/dot_general | solution.py:33
  435.7 8.4 convolution_convert_fusion.1
  444.2 5.0 pad_maximum_fusion
  449.2 14.3 %convolution_convert_fusion = bf16[2048,4096]{1,0:T(8,128)(2,1)} fusion(bf16[512,2048]{1,0:T(8,128)(2,1)} %constant_dynamic-update-slice_fusion.26, bf16[512,2048]{1,0:T(8,128)(2,1)S(1)} %copy-done.44, bf16[512,2048]{1,0:T(8,128)(2,1)S(1)} %copy-done.43), kind=kOutput, calls=%fused_computation | convolution fusion | flops 8606711808 | bytes 23068672 | tf_op jit(solution)/shard_map/dot_general | solution.py:33
  463.5 8.0 fusion.76
  475.4 13.9 %fusion.77 = f32[512,2048]{1,0:T(8,128)} fusion(bf16[512,4096]{1,0:T(8,128)(2,1)S(1)} %copy-done.23, bf16[2048,4096]{1,0:T(8,128)(2,1)} %all-gather.9.cloned.1.call-done), kind=kOutput, calls=%fused_computation.301 | convolution fusion | flops 8589934592 | bytes 25165824 | tf_op jit(solution)/shard_map/dot_general | solution.py:33
  494.0 4.5 collective-permute-done.45
  498.5 10.3 %collective-permute-done.52 = bf16[128,2048]{1,0:T(8,128)(2,1)S(1)} collective-permute-done((bf16[128,2048]{1,0:T(8,128)(2,1)S(1)}, bf16[128,2048]{1,0:T(8,128)(2,1)S(1)}, u32[]{:S(2)}, u32[]{:S(2)}) %collective-permute-start.52) | collective-permute-done | bytes 524320 | tf_op jit(solution)/shard_map/ppermute | solution.py:41
  508.8 12.2 %collective-permute-done.54 = bf16[128,2048]{1,0:T(8,128)(2,1)S(1)} collective-permute-done((bf16[128,2048]{1,0:T(8,128)(2,1)S(1)}, bf16[128,2048]{1,0:T(8,128)(2,1)S(1)}, u32[]{:S(2)}, u32[]{:S(2)}) %collective-permute-start.54) | collective-permute-done | bytes 524320 | tf_op jit(solution)/shard_map/ppermute | solution.py:41
  529.2 9.3 %collective-permute-done.55 = bf16[128,2048]{1,0:T(8,128)(2,1)S(1)} collective-permute-done((bf16[128,2048]{1,0:T(8,128)(2,1)S(1)}, bf16[128,2048]{1,0:T(8,128)(2,1)S(1)}, u32[]{:S(2)}, u32[]{:S(2)}) %collective-permute-start.55) | collective-permute-done | bytes 524320 | tf_op jit(solution)/shard_map/ppermute | solution.py:41
  540.3 9.7 %collective-permute-done.57 = bf16[128,2048]{1,0:T(8,128)(2,1)S(1)} collective-permute-done((bf16[128,2048]{1,0:T(8,128)(2,1)S(1)}, bf16[128,2048]{1,0:T(8,128)(2,1)S(1)}, u32[]{:S(2)}, u32[]{:S(2)}) %collective-permute-start.57) | collective-permute-done | bytes 524320 | tf_op jit(solution)/shard_map/ppermute | solution.py:41
  556.1 8.7 fusion.41
  565.7 4.4 convolution_convert_fusion.3
  575.0 6.7 collective-permute-done.46
  582.2 7.6 collective-permute-done.48
  596.0 8.6 chunk_state_back.1
  609.4 6.6 collective-permute-done.59
  621.4 31.0 %scan_backward.1 = (f32[512,1024]{1,0:T(8,128)}, f32[512,1024]{1,0:T(8,128)}, f32[16,1024]{1,0:T(8,128)}, f32[1,512,16,128]{3,2,1,0:T(8,128)}, f32[1,512,16,128]{3,2,1,0:T(8,128)}) custom-call(f32[512,1024]{1,0:T(8,128)} %copy-done.2, f32[512,1024]{1,0:T(8,128)} %copy-done.2, f32[512,1024]{1,0:T(8,128)} %copy-done.2, f32[512,1024]{1,0:T(8,128)} %copy-done.2, ...), custom_call_target="tpu_custom_call" | custom-call | tf_op jit(solution)/shard_map/scan_backward/pallas_call | solution.py:424
  652.4 4.8 fusion.61
  685.7 6.0 collective-permute-start.90
  717.3 7.9 collective-permute-start.82
  725.2 5.6 convolution_convert_fusion.2
  733.3 49.8 %reduce-scatter.14.cloned.1.call-done = bf16[1024,256]{1,0:T(8,128)(2,1)} async-done(((bf16[1024,2048]{1,0:T(8,128)(2,1)}), bf16[1024,256]{1,0:T(8,128)(2,1)}) %reduce-scatter.14.cloned.1.call-update) | async-done | bytes 524304 | tf_op jit(solution)/shard_map/reduce_scatter | solution.py:153
  785.9 6.9 fusion.20
  799.8 33.8 %reduce-scatter.12.cloned.1.call-done = bf16[256,1024]{1,0:T(8,128)(2,1)} async-done(((bf16[2048,1024]{1,0:T(8,128)(2,1)}), bf16[256,1024]{1,0:T(8,128)(2,1)}) %reduce-scatter.12.cloned.1.call-update) | async-done | bytes 524304 | tf_op jit(solution)/shard_map/reduce_scatter | solution.py:153
  849.5 15.0 %psum.7 = f32[2,512]{1,0:T(2,128)S(1)} all-reduce(f32[2,512]{1,0:T(2,128)S(1)} %add_add_fusion.2), channel_id=1, replica_groups=mesh['dp'=2,'row'=4,'col'=4] {'dp','row'}, use_global_device_ids=true, to_apply=%region_11.12 | all-reduce | flops 1024 | bytes 8192 | tf_op jit(solution)/shard_map/psum | solution.py:667
  867.6 7.4 collective-permute-done.70
  891.9 4.4 maximum_convert_fusion
  899.6 8.0 fusion.66
  (581 shorter events, 270.6 us)
Async XLA Ops:
  7.2 112.7 %all-gather.5.cloned.1.call-start = ((), (), s32[]{:S(2)}) async-start(), calls=%async_computation.5 | async-start | bytes 9437184 | tf_op jit(solution)/shard_map/all_gather | solution.py:147
  10.1 199.7 %all-gather.7.cloned.1.call-start = ((), (), s32[]{:S(2)}) async-start(), calls=%async_computation.6 | async-start | bytes 4718592 | tf_op jit(solution)/shard_map/all_gather | solution.py:147
  11.0 326.8 %all-gather.9.cloned.1.call-start = ((), (), s32[]{:S(2)}) async-start(), calls=%async_computation.7 | async-start | bytes 18874368 | tf_op jit(solution)/shard_map/all_gather | solution.py:147
  15.0 405.1 %all-gather.11.cloned.1.call-start = ((), (), s32[]{:S(2)}) async-start(), calls=%async_computation.8 | async-start | bytes 9437184 | tf_op jit(solution)/shard_map/all_gather | solution.py:147
  26.4 705.7 %reduce-scatter.6.cloned.1.call-start = ((), (), s32[]{:S(2)}) async-start(), calls=%async_computation.9 | async-start | bytes 9437184 | tf_op jit(solution)/shard_map/reduce_scatter | solution.py:153
  29.4 105.6 %collective-permute-start.23 = (bf16[128,256]{1,0:T(8,128)(2,1)}, bf16[128,256]{1,0:T(8,128)(2,1)}, u32[]{:S(2)}, u32[]{:S(2)}) collective-permute-start(bf16[128,256]{1,0:T(8,128)(2,1)} %get-tuple-element.88), channel_id=1, source_target_pairs={{0,2},{1,3},{2,0},{3,1},{4,6},{5,7},{6,4},{7,5},{8,10},{9,11},{10,... | collective-permute-start | bytes 196616 | tf_op jit(solution)/shard_map/ppermute | solution.py:41
  32.8 40.0 %collective-permute-start.17 = (bf16[256,160]{0,1:T(8,128)(2,1)}, bf16[256,160]{0,1:T(8,128)(2,1)S(1)}, u32[]{:S(2)}, u32[]{:S(2)}) collective-permute-start(bf16[256,160]{0,1:T(8,128)(2,1)} %get-tuple-element.82), channel_id=1, source_target_pairs={{0,2},{1,3},{2,0},{3,1},{4,6},{5,7},{6,4},{7,5},{8,10},{9,11},{10,... | collective-permute-start | bytes 245768 | tf_op jit(solution)/shard_map/ppermute | solution.py:41
  45.9 28.4 %collective-permute-start.18 = (bf16[256,160]{0,1:T(8,128)(2,1)}, bf16[256,160]{0,1:T(8,128)(2,1)S(1)}, u32[]{:S(2)}, u32[]{:S(2)}) collective-permute-start(bf16[256,160]{0,1:T(8,128)(2,1)} %get-tuple-element.82), channel_id=1, source_target_pairs={{0,3},{1,2},{2,1},{3,0},{4,7},{5,6},{6,5},{7,4},{8,11},{9,10},{10,... | collective-permute-start | bytes 245768 | tf_op jit(solution)/shard_map/ppermute | solution.py:41
  46.5 16.0 %collective-permute-start.3 = (bf16[1,128,512]{2,1,0:T(8,128)(2,1)S(1)}, bf16[1,128,512]{2,1,0:T(8,128)(2,1)S(1)}, u32[]{:S(2)}, u32[]{:S(2)}) collective-permute-start(bf16[1,128,512]{2,1,0:T(8,128)(2,1)S(1)} %get-tuple-element.171), channel_id=1, source_target_pairs={{0,1},{1,0},{2,3},{3,2},{4,5},{5,4},{6,7},{7,6},{8,9},{9,8},{10,11... | collective-permute-start | bytes 393224 | tf_op jit(solution)/shard_map/ppermute | solution.py:41
  76.3 16.9 %collective-permute-start.13 = (bf16[128,2048]{1,0:T(8,128)(2,1)S(1)}, bf16[128,2048]{1,0:T(8,128)(2,1)S(1)}, u32[]{:S(2)}, u32[]{:S(2)}) collective-permute-start(bf16[128,2048]{1,0:T(8,128)(2,1)S(1)} %get-tuple-element.86), channel_id=1, source_target_pairs={{0,8},{4,12},{8,0},{12,4},{1,9},{5,13},{9,1},{13,5},{2,10},{6,14},... | collective-permute-start | bytes 1572872 | tf_op jit(solution)/shard_map/ppermute | solution.py:41
  78.6 57.6 %collective-permute-start.24 = (bf16[128,256]{1,0:T(8,128)(2,1)}, bf16[128,256]{1,0:T(8,128)(2,1)}, u32[]{:S(2)}, u32[]{:S(2)}) collective-permute-start(bf16[128,256]{1,0:T(8,128)(2,1)} %get-tuple-element.88), channel_id=1, source_target_pairs={{0,3},{1,2},{2,1},{3,0},{4,7},{5,6},{6,5},{7,4},{8,11},{9,10},{10,... | collective-permute-start | bytes 196616 | tf_op jit(solution)/shard_map/ppermute | solution.py:41
  137.0 80.7 %collective-permute-start.39 = (bf16[1,128,512]{2,1,0:T(8,128)(2,1)}, bf16[1,128,512]{2,1,0:T(8,128)(2,1)}, u32[]{:S(2)}, u32[]{:S(2)}) collective-permute-start(bf16[1,128,512]{2,1,0:T(8,128)(2,1)} %get-tuple-element.157), channel_id=1, source_target_pairs={{0,3},{1,2},{2,1},{3,0},{4,7},{5,6},{6,5},{7,4},{8,11},{9,10},{10,... | collective-permute-start | bytes 393224 | tf_op jit(solution)/shard_map/ppermute | solution.py:41
  140.3 32.2 %collective-permute-start.38 = (bf16[1,128,512]{2,1,0:T(8,128)(2,1)}, bf16[1,128,512]{2,1,0:T(8,128)(2,1)}, u32[]{:S(2)}, u32[]{:S(2)}) collective-permute-start(bf16[1,128,512]{2,1,0:T(8,128)(2,1)} %get-tuple-element.158), channel_id=1, source_target_pairs={{0,2},{1,3},{2,0},{3,1},{4,6},{5,7},{6,4},{7,5},{8,10},{9,11},{10,... | collective-permute-start | bytes 393224 | tf_op jit(solution)/shard_map/ppermute | solution.py:41
  216.2 24.0 %collective-permute-start.30 = (bf16[128,2048]{1,0:T(8,128)(2,1)S(1)}, bf16[128,2048]{1,0:T(8,128)(2,1)S(1)}, u32[]{:S(2)}, u32[]{:S(2)}) collective-permute-start(bf16[128,2048]{1,0:T(8,128)(2,1)S(1)} %get-tuple-element.108), channel_id=1, source_target_pairs={{0,12},{4,8},{8,4},{12,0},{1,13},{5,9},{9,5},{13,1},{2,14},{6,10},... | collective-permute-start | bytes 1572872 | tf_op jit(solution)/shard_map/ppermute | solution.py:41
  217.4 22.8 %collective-permute-start.29 = (bf16[128,2048]{1,0:T(8,128)(2,1)S(1)}, bf16[128,2048]{1,0:T(8,128)(2,1)S(1)}, u32[]{:S(2)}, u32[]{:S(2)}) collective-permute-start(bf16[128,2048]{1,0:T(8,128)(2,1)S(1)} %get-tuple-element.109), channel_id=1, source_target_pairs={{0,8},{4,12},{8,0},{12,4},{1,9},{5,13},{9,1},{13,5},{2,10},{6,14},... | collective-permute-start | bytes 1572872 | tf_op jit(solution)/shard_map/ppermute | solution.py:41
  221.1 31.9 %collective-permute-start.41 = (bf16[128,2048]{1,0:T(8,128)(2,1)S(1)}, bf16[128,2048]{1,0:T(8,128)(2,1)S(1)}, u32[]{:S(2)}, u32[]{:S(2)}) collective-permute-start(bf16[128,2048]{1,0:T(8,128)(2,1)S(1)} %get-tuple-element.151), channel_id=1, source_target_pairs={{0,8},{4,12},{8,0},{12,4},{1,9},{5,13},{9,1},{13,5},{2,10},{6,14},... | collective-permute-start | bytes 1572872 | tf_op jit(solution)/shard_map/ppermute | solution.py:41
  222.4 28.2 %collective-permute-start.40 = (bf16[128,2048]{1,0:T(8,128)(2,1)S(1)}, bf16[128,2048]{1,0:T(8,128)(2,1)S(1)}, u32[]{:S(2)}, u32[]{:S(2)}) collective-permute-start(bf16[128,2048]{1,0:T(8,128)(2,1)S(1)} %get-tuple-element.151), channel_id=1, source_target_pairs={{0,4},{4,0},{8,12},{12,8},{1,5},{5,1},{9,13},{13,9},{2,6},{6,2},{1... | collective-permute-start | bytes 1572872 | tf_op jit(solution)/shard_map/ppermute | solution.py:41
  228.1 34.6 %collective-permute-start.42 = (bf16[128,2048]{1,0:T(8,128)(2,1)S(1)}, bf16[128,2048]{1,0:T(8,128)(2,1)S(1)}, u32[]{:S(2)}, u32[]{:S(2)}) collective-permute-start(bf16[128,2048]{1,0:T(8,128)(2,1)S(1)} %get-tuple-element.151), channel_id=1, source_target_pairs={{0,12},{4,8},{8,4},{12,0},{1,13},{5,9},{9,5},{13,1},{2,14},{6,10},... | collective-permute-start | bytes 1572872 | tf_op jit(solution)/shard_map/ppermute | solution.py:41
  243.4 29.7 %collective-permute-start.31 = (bf16[128,2048]{1,0:T(8,128)(2,1)S(1)}, bf16[128,2048]{1,0:T(8,128)(2,1)S(1)}, u32[]{:S(2)}, u32[]{:S(2)}) collective-permute-start(bf16[128,2048]{1,0:T(8,128)(2,1)S(1)} %get-tuple-element.76), channel_id=1, source_target_pairs={{0,4},{4,0},{8,12},{12,8},{1,5},{5,1},{9,13},{13,9},{2,6},{6,2},{1... | collective-permute-start | bytes 1572872 | tf_op jit(solution)/shard_map/ppermute | solution.py:41
  251.5 34.9 %collective-permute-start.32 = (bf16[128,2048]{1,0:T(8,128)(2,1)S(1)}, bf16[128,2048]{1,0:T(8,128)(2,1)S(1)}, u32[]{:S(2)}, u32[]{:S(2)}) collective-permute-start(bf16[128,2048]{1,0:T(8,128)(2,1)S(1)} %get-tuple-element.76), channel_id=1, source_target_pairs={{0,8},{4,12},{8,0},{12,4},{1,9},{5,13},{9,1},{13,5},{2,10},{6,14},... | collective-permute-start | bytes 1572872 | tf_op jit(solution)/shard_map/ppermute | solution.py:41
  253.9 33.3 %collective-permute-start.33 = (bf16[128,2048]{1,0:T(8,128)(2,1)S(1)}, bf16[128,2048]{1,0:T(8,128)(2,1)S(1)}, u32[]{:S(2)}, u32[]{:S(2)}) collective-permute-start(bf16[128,2048]{1,0:T(8,128)(2,1)S(1)} %get-tuple-element.76), channel_id=1, source_target_pairs={{0,12},{4,8},{8,4},{12,0},{1,13},{5,9},{9,5},{13,1},{2,14},{6,10},... | collective-permute-start | bytes 1572872 | tf_op jit(solution)/shard_map/ppermute | solution.py:41
  444.1 287.9 %reduce-scatter.8.cloned.1.call-start = ((), (), s32[]{:S(2)}) async-start(), calls=%async_computation.10 | async-start | bytes 18874368 | tf_op jit(solution)/shard_map/reduce_scatter | solution.py:153
  463.5 319.6 %reduce-scatter.14.cloned.1.call-start = ((), (), s32[]{:S(2)}) async-start(), calls=%async_computation.13 | async-start | bytes 4718592 | tf_op jit(solution)/shard_map/reduce_scatter | solution.py:153
  472.7 21.0 %collective-permute-start.43 = (bf16[128,2048]{1,0:T(8,128)(2,1)}, bf16[128,2048]{1,0:T(8,128)(2,1)S(1)}, u32[]{:S(2)}, u32[]{:S(2)}) collective-permute-start(bf16[128,2048]{1,0:T(8,128)(2,1)} %get-tuple-element.104), channel_id=1, source_target_pairs={{0,4},{4,0},{8,12},{12,8},{1,5},{5,1},{9,13},{13,9},{2,6},{6,2},{1... | collective-permute-start | bytes 1572872 | tf_op jit(solution)/shard_map/ppermute | solution.py:41
  473.9 24.6 %collective-permute-start.45 = (bf16[128,2048]{1,0:T(8,128)(2,1)}, bf16[128,2048]{1,0:T(8,128)(2,1)S(1)}, u32[]{:S(2)}, u32[]{:S(2)}) collective-permute-start(bf16[128,2048]{1,0:T(8,128)(2,1)} %get-tuple-element.105), channel_id=1, source_target_pairs={{0,12},{4,8},{8,4},{12,0},{1,13},{5,9},{9,5},{13,1},{2,14},{6,10},... | collective-permute-start | bytes 1572872 | tf_op jit(solution)/shard_map/ppermute | solution.py:41
  475.1 23.4 %collective-permute-start.44 = (bf16[128,2048]{1,0:T(8,128)(2,1)S(1)}, bf16[128,2048]{1,0:T(8,128)(2,1)S(1)}, u32[]{:S(2)}, u32[]{:S(2)}) collective-permute-start(bf16[128,2048]{1,0:T(8,128)(2,1)S(1)} %get-tuple-element.106), channel_id=1, source_target_pairs={{0,8},{4,12},{8,0},{12,4},{1,9},{5,13},{9,1},{13,5},{2,10},{6,14},... | collective-permute-start | bytes 1572872 | tf_op jit(solution)/shard_map/ppermute | solution.py:41
  491.3 17.5 %collective-permute-start.52 = (bf16[128,2048]{1,0:T(8,128)(2,1)S(1)}, bf16[128,2048]{1,0:T(8,128)(2,1)S(1)}, u32[]{:S(2)}, u32[]{:S(2)}) collective-permute-start(bf16[128,2048]{1,0:T(8,128)(2,1)S(1)} %get-tuple-element.101), channel_id=1, source_target_pairs={{0,4},{4,0},{8,12},{12,8},{1,5},{5,1},{9,13},{13,9},{2,6},{6,2},{1... | collective-permute-start | bytes 1572872 | tf_op jit(solution)/shard_map/ppermute | solution.py:41
  492.6 28.4 %collective-permute-start.54 = (bf16[128,2048]{1,0:T(8,128)(2,1)S(1)}, bf16[128,2048]{1,0:T(8,128)(2,1)S(1)}, u32[]{:S(2)}, u32[]{:S(2)}) collective-permute-start(bf16[128,2048]{1,0:T(8,128)(2,1)S(1)} %get-tuple-element.102), channel_id=1, source_target_pairs={{0,12},{4,8},{8,4},{12,0},{1,13},{5,9},{9,5},{13,1},{2,14},{6,10},... | collective-permute-start | bytes 1572872 | tf_op jit(solution)/shard_map/ppermute | solution.py:41
  493.8 28.0 %collective-permute-start.53 = (bf16[128,2048]{1,0:T(8,128)(2,1)S(1)}, bf16[128,2048]{1,0:T(8,128)(2,1)S(1)}, u32[]{:S(2)}, u32[]{:S(2)}) collective-permute-start(bf16[128,2048]{1,0:T(8,128)(2,1)S(1)} %get-tuple-element.103), channel_id=1, source_target_pairs={{0,8},{4,12},{8,0},{12,4},{1,9},{5,13},{9,1},{13,5},{2,10},{6,14},... | collective-permute-start | bytes 1572872 | tf_op jit(solution)/shard_map/ppermute | solution.py:41
  528.1 21.9 %collective-permute-start.57 = (bf16[128,2048]{1,0:T(8,128)(2,1)S(1)}, bf16[128,2048]{1,0:T(8,128)(2,1)S(1)}, u32[]{:S(2)}, u32[]{:S(2)}) collective-permute-start(bf16[128,2048]{1,0:T(8,128)(2,1)S(1)} %get-tuple-element.73), channel_id=1, source_target_pairs={{0,12},{4,8},{8,4},{12,0},{1,13},{5,9},{9,5},{13,1},{2,14},{6,10},... | collective-permute-start | bytes 1572872 | tf_op jit(solution)/shard_map/ppermute | solution.py:41
  555.9 277.8 %reduce-scatter.12.cloned.1.call-start = ((), (), s32[]{:S(2)}) async-start(), calls=%async_computation.12 | async-start | bytes 4718592 | tf_op jit(solution)/shard_map/reduce_scatter | solution.py:153
  570.1 326.2 %reduce-scatter.10.cloned.1.call-start = ((), (), s32[]{:S(2)}) async-start(), calls=%async_computation.11 | async-start | bytes 4718592 | tf_op jit(solution)/shard_map/reduce_scatter | solution.py:153
  572.3 17.5 %collective-permute-start.48 = (bf16[1,128,512]{2,1,0:T(8,128)(2,1)S(1)}, bf16[1,128,512]{2,1,0:T(8,128)(2,1)S(1)}, u32[]{:S(2)}, u32[]{:S(2)}) collective-permute-start(bf16[1,128,512]{2,1,0:T(8,128)(2,1)S(1)} %get-tuple-element.143), channel_id=1, source_target_pairs={{0,3},{1,2},{2,1},{3,0},{4,7},{5,6},{6,5},{7,4},{8,11},{9,10},{10,... | collective-permute-start | bytes 393224 | tf_op jit(solution)/shard_map/ppermute | solution.py:41
  660.2 23.1 %collective-permute-start.87 = (bf16[128,256]{1,0:T(8,128)(2,1)}, bf16[128,256]{1,0:T(8,128)(2,1)}, u32[]{:S(2)}, u32[]{:S(2)}) collective-permute-start(bf16[128,256]{1,0:T(8,128)(2,1)} %get-tuple-element.124), channel_id=1, source_target_pairs={{0,1},{1,0},{2,3},{3,2},{4,5},{5,4},{6,7},{7,6},{8,9},{9,8},{10,11... | collective-permute-start | bytes 196616 | tf_op jit(solution)/shard_map/ppermute | solution.py:41
  663.4 21.2 %collective-permute-start.89 = (bf16[128,256]{1,0:T(8,128)(2,1)}, bf16[128,256]{1,0:T(8,128)(2,1)}, u32[]{:S(2)}, u32[]{:S(2)}) collective-permute-start(bf16[128,256]{1,0:T(8,128)(2,1)} %get-tuple-element.125), channel_id=1, source_target_pairs={{0,3},{1,2},{2,1},{3,0},{4,7},{5,6},{6,5},{7,4},{8,11},{9,10},{10,... | collective-permute-start | bytes 196616 | tf_op jit(solution)/shard_map/ppermute | solution.py:41
  666.2 18.4 %collective-permute-start.88 = (bf16[128,256]{1,0:T(8,128)(2,1)}, bf16[128,256]{1,0:T(8,128)(2,1)}, u32[]{:S(2)}, u32[]{:S(2)}) collective-permute-start(bf16[128,256]{1,0:T(8,128)(2,1)} %get-tuple-element.126), channel_id=1, source_target_pairs={{0,2},{1,3},{2,0},{3,1},{4,6},{5,7},{6,4},{7,5},{8,10},{9,11},{10,... | collective-permute-start | bytes 196616 | tf_op jit(solution)/shard_map/ppermute | solution.py:41
  712.9 19.2 %collective-permute-start.83 = (bf16[256,160]{0,1:T(8,128)(2,1)}, bf16[256,160]{0,1:T(8,128)(2,1)}, u32[]{:S(2)}, u32[]{:S(2)}) collective-permute-start(bf16[256,160]{0,1:T(8,128)(2,1)} %get-tuple-element.121), channel_id=1, source_target_pairs={{0,1},{1,0},{2,3},{3,2},{4,5},{5,4},{6,7},{7,6},{8,9},{9,8},{10,11... | collective-permute-start | bytes 245768 | tf_op jit(solution)/shard_map/ppermute | solution.py:41
  714.4 17.7 %collective-permute-start.85 = (bf16[256,160]{0,1:T(8,128)(2,1)S(1)}, bf16[256,160]{0,1:T(8,128)(2,1)}, u32[]{:S(2)}, u32[]{:S(2)}) collective-permute-start(bf16[256,160]{0,1:T(8,128)(2,1)S(1)} %get-tuple-element.122), channel_id=1, source_target_pairs={{0,3},{1,2},{2,1},{3,0},{4,7},{5,6},{6,5},{7,4},{8,11},{9,10},{10,... | collective-permute-start | bytes 245768 | tf_op jit(solution)/shard_map/ppermute | solution.py:41
  733.2 65.9 %collective-permute-start.86 = (f32[256,160]{0,1:T(8,128)S(1)}, f32[256,160]{0,1:T(8,128)S(1)}, u32[]{:S(2)}, u32[]{:S(2)}) collective-permute-start(f32[256,160]{0,1:T(8,128)S(1)} %convert_add_fusion.3), channel_id=1, source_target_pairs={{0,16},{16,0},{1,17},{17,1},{2,18},{18,2},{3,19},{19,3},{4,20},{20... | collective-permute-start | bytes 491528 | tf_op jit(solution)/shard_map/ppermute | solution.py:41
  783.1 53.3 %collective-permute-start.91 = (bf16[1024,256]{1,0:T(8,128)(2,1)}, bf16[1024,256]{1,0:T(8,128)(2,1)}, u32[]{:S(2)}, u32[]{:S(2)}) collective-permute-start(bf16[1024,256]{1,0:T(8,128)(2,1)} %reduce-scatter.14.cloned.1.call-done), channel_id=1, source_target_pairs={{0,16},{16,0},{1,17},{17,1},{2,18},{18,2},{3,19},{19,3},{4,20},{20... | collective-permute-start | bytes 1572872 | tf_op jit(solution)/shard_map/ppermute | solution.py:41
  795.9 43.4 %collective-permute-start.65 = (bf16[128,2048]{1,0:T(8,128)(2,1)}, bf16[128,2048]{1,0:T(8,128)(2,1)S(1)}, u32[]{:S(2)}, u32[]{:S(2)}) collective-permute-start(bf16[128,2048]{1,0:T(8,128)(2,1)} %get-tuple-element.98), channel_id=1, source_target_pairs={{0,4},{4,0},{8,12},{12,8},{1,5},{5,1},{9,13},{13,9},{2,6},{6,2},{1... | collective-permute-start | bytes 1572872 | tf_op jit(solution)/shard_map/ppermute | solution.py:41
  797.1 42.2 %collective-permute-start.67 = (bf16[128,2048]{1,0:T(8,128)(2,1)S(1)}, bf16[128,2048]{1,0:T(8,128)(2,1)S(1)}, u32[]{:S(2)}, u32[]{:S(2)}) collective-permute-start(bf16[128,2048]{1,0:T(8,128)(2,1)S(1)} %get-tuple-element.99), channel_id=1, source_target_pairs={{0,12},{4,8},{8,4},{12,0},{1,13},{5,9},{9,5},{13,1},{2,14},{6,10},... | collective-permute-start | bytes 1572872 | tf_op jit(solution)/shard_map/ppermute | solution.py:41
  798.3 41.0 %collective-permute-start.66 = (bf16[128,2048]{1,0:T(8,128)(2,1)S(1)}, bf16[128,2048]{1,0:T(8,128)(2,1)}, u32[]{:S(2)}, u32[]{:S(2)}) collective-permute-start(bf16[128,2048]{1,0:T(8,128)(2,1)S(1)} %get-tuple-element.100), channel_id=1, source_target_pairs={{0,8},{4,12},{8,0},{12,4},{1,9},{5,13},{9,1},{13,5},{2,10},{6,14},... | collective-permute-start | bytes 1572872 | tf_op jit(solution)/shard_map/ppermute | solution.py:41
  833.6 74.0 %collective-permute-start.78 = (bf16[256,1024]{1,0:T(8,128)(2,1)}, bf16[256,1024]{1,0:T(8,128)(2,1)S(1)}, u32[]{:S(2)}, u32[]{:S(2)}) collective-permute-start(bf16[256,1024]{1,0:T(8,128)(2,1)} %reduce-scatter.12.cloned.1.call-done), channel_id=1, source_target_pairs={{0,16},{16,0},{1,17},{17,1},{2,18},{18,2},{3,19},{19,3},{4,20},{20... | collective-permute-start | bytes 1572872 | tf_op jit(solution)/shard_map/ppermute | solution.py:41
  839.2 46.5 %collective-permute-start.93 = (bf16[2048,256]{1,0:T(8,128)(2,1)}, bf16[2048,256]{1,0:T(8,128)(2,1)}, u32[]{:S(2)}, u32[]{:S(2)}) collective-permute-start(bf16[2048,256]{1,0:T(8,128)(2,1)} %reduce-scatter.6.cloned.1.call-done), channel_id=1, source_target_pairs={{0,16},{16,0},{1,17},{17,1},{2,18},{18,2},{3,19},{19,3},{4,20},{20... | collective-permute-start | bytes 3145736 | tf_op jit(solution)/shard_map/ppermute | solution.py:41
  847.5 42.5 %collective-permute-start.92 = (bf16[256,4096]{1,0:T(8,128)(2,1)S(1)}, bf16[256,4096]{1,0:T(8,128)(2,1)}, u32[]{:S(2)}, u32[]{:S(2)}) collective-permute-start(bf16[256,4096]{1,0:T(8,128)(2,1)S(1)} %copy-done.41), channel_id=1, source_target_pairs={{0,16},{16,0},{1,17},{17,1},{2,18},{18,2},{3,19},{19,3},{4,20},{20... | collective-permute-start | bytes 6291464 | tf_op jit(solution)/shard_map/ppermute | solution.py:41
  848.7 18.8 %collective-permute-start.69 = (bf16[1,128,512]{2,1,0:T(8,128)(2,1)}, bf16[1,128,512]{2,1,0:T(8,128)(2,1)S(1)}, u32[]{:S(2)}, u32[]{:S(2)}) collective-permute-start(bf16[1,128,512]{2,1,0:T(8,128)(2,1)} %get-tuple-element.132), channel_id=1, source_target_pairs={{0,2},{1,3},{2,0},{3,1},{4,6},{5,7},{6,4},{7,5},{8,10},{9,11},{10,... | collective-permute-start | bytes 393224 | tf_op jit(solution)/shard_map/ppermute | solution.py:41
  848.8 15.8 %collective-permute-start.68 = (bf16[1,128,512]{2,1,0:T(8,128)(2,1)}, bf16[1,128,512]{2,1,0:T(8,128)(2,1)S(1)}, u32[]{:S(2)}, u32[]{:S(2)}) collective-permute-start(bf16[1,128,512]{2,1,0:T(8,128)(2,1)} %get-tuple-element.133), channel_id=1, source_target_pairs={{0,1},{1,0},{2,3},{3,2},{4,5},{5,4},{6,7},{7,6},{8,9},{9,8},{10,11... | collective-permute-start | bytes 393224 | tf_op jit(solution)/shard_map/ppermute | solution.py:41
  (167 other events, 2969.3 us)
Sparse Core Ops, SparseCore 0:
  10.2 109.6 all-gather.4
  122.1 60.6 all-gather.6
  184.4 153.4 all-gather.8
  339.3 80.7 all-gather.10
  444.2 85.2 reduce-scatter.5
  531.7 188.0 reduce-scatter.7
  722.1 61.0 reduce-scatter.13
  785.4 48.1 reduce-scatter.11
  836.5 57.8 reduce-scatter.9

commit v3 on v2

--- a/solution.py
+++ b/solution.py
@@ -63,6 +63,10 @@
     return joined
 
 
+def gather_blocks(values):
+    return gather_by_swaps(values[None], "col", 0)
+
+
 def scatter_by_swaps(values, axis_name, axis, dtype):
     size = lax.axis_size(axis_name)
     length = values.shape[axis] // size
@@ -79,26 +83,45 @@
     return total
 
 
+def by_swaps():
+    return lax.axis_size("row") == 4
+
+
+def block_order():
+    return lax.axis_index("row") if by_swaps() else jnp.int32(0)
+
+
 def row_gather(values):
-    if lax.axis_size("row") == 4:
-        return gather_by_swaps(values, "row", 0)
+    if by_swaps():
+        return jnp.concatenate(
+            [values] + [swap(values, "row", distance) for distance in range(1, 4)], axis=0
+        )
     return lax.all_gather(values, "row", axis=0, tiled=True)
 
 
 def row_scatter(values):
-    if lax.axis_size("row") == 4:
-        return scatter_by_swaps(values, "row", 0, jnp.bfloat16)
+    if by_swaps():
+        count = values.shape[0] // 4
+        total = values[:count]
+        for distance in range(1, 4):
+            block = low(values[distance * count : (distance + 1) * count])
+            total = total + swap(block, "row", distance).astype(jnp.float32)
+        return total
     return lax.psum_scatter(low(values), "row", scatter_dimension=0, tiled=True).astype(
         jnp.float32
     )
 
 
-def row_total(values):
-    if lax.axis_size("row") == 4:
-        total = values
+def row_total(values, local=None):
+    if by_swaps():
+        blocks = values.reshape((4, -1) + values.shape[1:])
+        total = (values if local is None else local).reshape(blocks.shape)
         for distance in range(1, 4):
-            total = total + swap(values, "row", distance)
-        return total
+            got = swap(values, "row", distance).reshape(blocks.shape)
+            total = total + jnp.concatenate(
+                [got[k ^ distance : (k ^ distance) + 1] for k in range(4)], axis=0
+            )
+        return total.reshape(values.shape)
     return lax.psum(values, "row")
 
 
@@ -129,28 +152,69 @@
     return lax.ppermute(split, ("row", "col"), block_moves())
 
 
-def to_feature_blocks(values):
+def to_feature_blocks(arrays, others):
     rows, cols = lax.axis_size("row"), lax.axis_size("col")
+    count, features = arrays[0].shape[0], arrays[0].shape[1] // cols
     if rows == cols:
-        count, features = values.shape[0], values.shape[1] // cols
-        pieces = jnp.stack([values[:, c * features : (c + 1) * features] for c in range(cols)])
-        pieces = exchange(exchange(pieces, "col"), "row")
-        return pieces.reshape(rows * count, features)
+        pieces = jnp.stack(
+            [
+                jnp.concatenate(
+                    [values[:, c * features : (c + 1) * features] for values in arrays]
+                )
+                for c in range(cols)
+            ]
+        )
+        pieces = lax.all_to_all(pieces, "col", split_axis=0, concat_axis=0)
+        pieces, others = lax.optimization_barrier((pieces, others))
+        pieces = exchange(pieces, "row")
+        return [
+            pieces[:, i * count : (i + 1) * count].reshape(rows * count, features)
+            for i in range(len(arrays))
+        ], others
     back = [(target, source) for source, target in block_moves()]
-    split = lax.ppermute(values, ("row", "col"), back)
-    return lax.all_to_all(split, "col", split_axis=1, concat_axis=0, tiled=True)
-
-
-def gather_weight(weight, axis):
-    half = weight.shape[axis] // lax.axis_size("dp")
-    part = lax.dynamic_slice_in_dim(weight, lax.axis_index("dp") * half, half, axis)
-    return lax.all_gather(low(part), ("col", "dp"), axis=axis, tiled=True)
-
-
-def scatter_gradient(gradient, axis, after=None):
-    if after is not None:
-        gradient, _ = lax.optimization_barrier((gradient, after))
-    return lax.psum_scatter(gradient, ("col", "dp"), scatter_dimension=axis, tiled=True)
+
+    def one(values):
+        split = lax.ppermute(values, ("row", "col"), back)
+        return lax.all_to_all(split, "col", split_axis=1, concat_axis=0, tiled=True)
+
+    return [one(values) for values in arrays], others
+
+
+def gather_weight(weight):
+    half = weight.shape[0] // lax.axis_size("dp")
+    part = lax.dynamic_slice_in_dim(weight, lax.axis_index("dp") * half, half, 0)
+    return lax.all_gather(low(part), ("col", "dp"), axis=0, tiled=True)
+
+
+def block_at(blocks, place):
+    return lax.dynamic_index_in_dim(blocks, place, 0, keepdims=False)
+
+
+def neighbours(outside, blocks, order, direction):
+    last = blocks.shape[0] - 1
+    edge = 0 if direction == -1 else last
+    got = []
+    for place in range(last + 1):
+        own = place ^ order
+        near = block_at(blocks, jnp.clip(own + direction, 0, last) ^ order)
+        got.append(jnp.where(own == edge, outside, near))
+    return jnp.stack(got)
+
+
+def feature_halves(values):
+    blocks, first = lax.axis_size("col"), lax.axis_index("dp") == 0
+    half = values.shape[1] // (2 * blocks)
+    parts = [values[:, i * half : (i + 1) * half] for i in range(2 * blocks)]
+    upper, lower = jnp.concatenate(parts[0::2], axis=1), jnp.concatenate(parts[1::2], axis=1)
+    return jnp.where(first, upper, lower), jnp.where(first, lower, upper)
+
+
+def add_pair(own, other):
+    return low(own + swap(other, "dp", 1).astype(jnp.float32))
+
+
+def scatter_gradient(gradient):
+    return lax.psum_scatter(gradient, "col", scatter_dimension=0, tiled=True)
 
 
 def both_halves(own, axis):
@@ -158,7 +222,7 @@
     first = lax.axis_index("dp") == 0
     return jnp.concatenate(
         [jnp.where(first, own, other), jnp.where(first, other, own)], axis=axis
-    ).astype(jnp.float32)
+    )
 
 
 def fold_rows(parts):
@@ -177,11 +241,12 @@
 
 
 class Tiling:
-    def __init__(self, tokens, channels, backward):
+    def __init__(self, order, tokens, channels, backward):
+        self.order = order
         groups = channels // LANES
         self.tokens, self.channels = tokens, channels
         self.per = min(8, groups)
-        self.block = min(128, tokens)
+        self.block = min(tokens // lax.axis_size("row") if by_swaps() else 128, tokens)
         self.blocks = tokens // self.block
         self.grid = (groups // self.per, self.blocks)
         self.width = self.per * LANES
@@ -194,26 +259,32 @@
     def narrow(self):
         def spec(i):
             return pl.BlockSpec(
-                (self.block, LANES), lambda g, b: (self.at(b), g * self.per + i)
+                (self.block, LANES), lambda g, b, order: (self.at(b) ^ order[0], g * self.per + i)
             )
 
         return [spec(i) for i in range(self.per)]
 
     def token_spec(self):
-        return pl.BlockSpec((self.block, self.width), lambda g, b: (self.at(b), g))
+        return pl.BlockSpec(
+            (self.block, self.width), lambda g, b, order: (self.at(b) ^ order[0], g)
+        )
 
     def wide_spec(self):
-        return pl.BlockSpec((self.block, STATE, LANES), lambda g, b: (self.at(b), 0, 0))
+        return pl.BlockSpec(
+            (self.block, STATE, LANES), lambda g, b, order: (self.at(b) ^ order[0], 0, 0)
+        )
 
     def state_spec(self):
-        return pl.BlockSpec((STATE, self.width), lambda g, b: (0, g))
+        return pl.BlockSpec((STATE, self.width), lambda g, b, order: (0, g))
 
     def history_spec(self):
-        return pl.BlockSpec((self.block, STATE, self.width), lambda g, b: (self.at(b), 0, g))
+        return pl.BlockSpec(
+            (self.block, STATE, self.width), lambda g, b, order: (self.at(b), 0, g)
+        )
 
     def part_spec(self):
         return pl.BlockSpec(
-            (1, self.block, STATE, LANES), lambda g, b: (g, self.at(b), 0, 0)
+            (1, self.block, LANES), lambda g, b, order: (g, self.at(b) ^ order[0], 0)
         )
 
     def load(self, ref):
@@ -228,19 +299,23 @@
             ref[8:16, lanes] = values[2 * g + 1]
 
     def call(self, kernel, name, in_specs, out_specs, out_shape, scratch=()):
-        return pl.pallas_call(
+        call = pl.pallas_call(
             kernel,
             out_shape=out_shape,
-            grid=self.grid,
-            in_specs=in_specs,
-            out_specs=out_specs,
-            scratch_shapes=list(scratch),
+            grid_spec=pltpu.PrefetchScalarGridSpec(
+                num_scalar_prefetch=1,
+                grid=self.grid,
+                in_specs=in_specs,
+                out_specs=out_specs,
+                scratch_shapes=list(scratch),
+            ),
             compiler_params=pltpu.CompilerParams(
                 dimension_semantics=("arbitrary", "arbitrary"),
                 vmem_limit_bytes=56 * 2**20,
             ),
             name=name,
         )
+        return lambda *operands: call(self.order.reshape(1), *operands)
 
 
 def pair(ref, token):
@@ -251,11 +326,11 @@
     return jax.ShapeDtypeStruct(shape, jnp.float32)
 
 
-def chunk_state(step, drive, wide, rate, backward):
-    t = Tiling(*step.shape, backward)
+def chunk_state(order, step, drive, wide, rate, backward):
+    t = Tiling(order, *step.shape, backward)
     per = t.per
 
-    def kernel(*refs):
+    def kernel(_, *refs):
         step_refs, drive_refs = refs[:per], refs[per : 2 * per]
         wide_ref, rate_ref, state_ref = refs[2 * per :]
 
@@ -296,11 +371,11 @@
     )(*[step] * per, *[drive] * per, wide, rate)
 
 
-def scan_forward(step, drive, in_wide, out_wide, rate, entry):
-    t = Tiling(*step.shape, False)
+def scan_forward(order, step, drive, in_wide, out_wide, rate, entry):
+    t = Tiling(order, *step.shape, False)
     per = t.per
 
-    def kernel(*refs):
+    def kernel(_, *refs):
         step_refs, drive_refs = refs[:per], refs[per : 2 * per]
         in_ref, out_ref, rate_ref, entry_ref, y_ref, before_ref, last_ref = refs[2 * per :]
 
@@ -349,19 +424,17 @@
     )(*[step] * per, *[drive] * per, in_wide, out_wide, rate, entry)
 
 
-def scan_backward(step, drive, back, in_wide, out_wide, rate, entry, before, last):
-    t = Tiling(*step.shape, True)
+def scan_backward(order, step, drive, back, in_wide, out_wide, rate, entry, before, last):
+    t = Tiling(order, *step.shape, True)
     per = t.per
 
-    def kernel(*refs):
+    def kernel(_, *refs):
         step_refs, drive_refs, back_refs = (refs[i * per : (i + 1) * per] for i in range(3))
         in_ref, out_ref, rate_ref, entry_ref, before_ref, last_ref = refs[
             3 * per : 3 * per + 6
         ]
-        rate_sum_ref, in_sum_ref, decay_ref, in_part_ref, out_part_ref = refs[
-            3 * per + 6 : 3 * per + 11
-        ]
-        carry_ref, state_ref = refs[3 * per + 11 :]
+        rate_sum_ref, in_sum_ref, decay_ref, coefficient_ref = refs[3 * per + 6 : 3 * per + 10]
+        carry_ref, state_ref, in_part_ref, out_part_ref = refs[3 * per + 10 :]
 
         @pl.when(pl.program_id(1) == 0)
         def _():
@@ -403,8 +476,9 @@
                     rate_sums[g][j] = by_rate[0] + by_rate[1]
                     in_sums[g][j] = by_in[0] + by_in[1]
                 for k in (0, 1):
-                    in_part_ref[0, token, 8 * k : 8 * k + 8, :] = in_part[k]
-                    out_part_ref[0, token, 8 * k : 8 * k + 8, :] = out_part[k]
+                    place = pl.multiple_of(token * STATE + k * ROWS, ROWS)
+                    in_part_ref[pl.ds(place, ROWS), :] = in_part[k]
+                    out_part_ref[pl.ds(place, ROWS), :] = out_part[k]
             for g in range(per):
                 rate_sum_ref[pl.ds(base, ROWS), t.lanes[g]] = fold_rows(rate_sums[g])
                 in_sum_ref[pl.ds(base, ROWS), t.lanes[g]] = fold_rows(in_sums[g])
@@ -420,8 +494,37 @@
         t.store(state_ref, state)
         t.store(decay_ref, decay)
 
-    parts = f32(t.grid[0], t.tokens, STATE, LANES)
-    rate_sum, in_sum, decay, in_part, out_part = t.call(
+        for part_ref in (in_part_ref, out_part_ref):
+            part = part_ref[...]
+            high = low(part)
+            ones = jnp.ones((LANES, LANES), jnp.bfloat16)
+            part_ref[...] = product(high, ones) + product(
+                low(part - high.astype(jnp.float32)), ones
+            )
+        row = lax.broadcasted_iota(jnp.int32, (ROWS, LANES), 0)
+        lane = lax.broadcasted_iota(jnp.int32, (ROWS, LANES), 1)
+
+        def gathered(i, _):
+            base = pl.multiple_of(i * ROWS, ROWS)
+            tokens = []
+            for j in range(ROWS):
+                total = None
+                for m, part_ref in ((0, in_part_ref), (1, out_part_ref)):
+                    for k in (0, 1):
+                        place = pl.multiple_of((base + j) * STATE + k * ROWS, ROWS)
+                        term = jnp.where(
+                            lane == row + (m * STATE + k * ROWS),
+                            part_ref[pl.ds(place, ROWS), :],
+                            0.0,
+                        )
+                        total = term if total is None else total + term
+                tokens.append(total)
+            coefficient_ref[0, pl.ds(base, ROWS), :] = fold_rows(tokens)
+            return _
+
+        lax.fori_loop(0, t.block // ROWS, gathered, 0)
+
+    rate_sum, in_sum, decay, coefficients = t.call(
         kernel,
         "scan_backward",
         t.narrow()
@@ -435,15 +538,15 @@
             t.history_spec(),
             t.state_spec(),
         ],
-        (t.token_spec(), t.token_spec(), t.state_spec(), t.part_spec(), t.part_spec()),
+        (t.token_spec(), t.token_spec(), t.state_spec(), t.part_spec()),
         (
             f32(t.tokens, t.channels),
             f32(t.tokens, t.channels),
             f32(STATE, t.channels),
-            parts,
-            parts,
+            f32(t.grid[0], t.tokens, LANES),
         ),
-        [pltpu.VMEM((STATE, t.width), jnp.float32)] * 2,
+        [pltpu.VMEM((STATE, t.width), jnp.float32)] * 2
+        + [pltpu.VMEM((t.block * STATE, LANES), jnp.float32)] * 2,
     )(
         *[step] * per,
         *[drive] * per,
@@ -455,7 +558,7 @@
         before,
         last,
     )
-    return rate_sum, in_sum, decay, jnp.sum(in_part, (0, 3)), jnp.sum(out_part, (0, 3))
+    return rate_sum, in_sum, decay, jnp.sum(coefficients, 0)[:, : 2 * STATE]
 
 
 def chunk_entry(state, step_total, rate, direction):
@@ -509,17 +612,19 @@
     out_grad,
 ):
     channels, units = in_value.shape[1], feed_gate.shape[1]
-    in_low = gather_weight(jnp.concatenate([in_value, in_gate], axis=1), 0)
-    mixer_low = gather_weight(mixer_out, 1)
-    feed_low = gather_weight(jnp.concatenate([feed_gate, feed_up], axis=1), 0)
-    feed_down_low = gather_weight(feed_down, 1)
-
-    inputs = to_whole_features(tokens).astype(jnp.float32)
-    out_back_low = to_whole_features(out_grad)
-    gains = gather_by_swaps(jnp.stack([mixer_norm, feed_norm]), "col", 1)
-    mixer_gain, feed_gain = gains[0:1], gains[1:2]
+    order = block_order()
+    rows, index = lax.axis_size("row"), lax.axis_index("dp")
+    first = gather_weight(jnp.concatenate([in_value, in_gate, mixer_out.T], axis=1))
+    in_low, mixer_low = first[:, : 2 * channels], first[:, 2 * channels :]
+    feed_low = gather_weight(jnp.concatenate([feed_gate, feed_up], axis=1))
+    feed_down_low = gather_weight(feed_down.T)
+
+    inputs = to_whole_features(tokens)
+    own_channels = conv_bias.shape[0]
+    gains = jnp.stack([mixer_norm, feed_norm]).reshape(-1, own_channels)
     packed = jnp.concatenate(
         [
+            gains,
             conv_weight.T,
             conv_bias[None],
             step_bias[None],
@@ -528,28 +633,47 @@
         ],
         axis=0,
     )
-    packed = gather_by_swaps(packed, "col", 1)
+    packed = gather_blocks(packed)
+    gain_rows = gains.shape[0]
+    gains = packed[:, :gain_rows].reshape(-1, 2, mixer_norm.shape[0])
+    mixer_gain = gains[:, 0].reshape(1, -1)
+    feed_gain = gains[:, 1].reshape(1, -1)
+    packed = jnp.swapaxes(packed[:, gain_rows:], 0, 1).reshape(-1, channels)
     taps = packed[:CONV]
     conv_bias_row, step_bias_row, skip_row = (
         packed[CONV + i : CONV + i + 1] for i in range(3)
     )
     decay_rate = -jnp.exp(packed[CONV + 3 :])
-    state_low = gather_by_swaps(low(state_proj), "col", 0)
-    step_weight = gather_by_swaps(low(step_proj), "col", 1)
+    projections = jnp.concatenate([low(step_proj), low(state_proj).T], axis=0)
+    projections, inputs = lax.optimization_barrier((projections, inputs))
+    half = projections.shape[0] // 2
+    projections = gather_blocks(
+        lax.dynamic_slice_in_dim(projections, index * half, half, 0)
+    )
+    projections = both_halves(projections, 1)
+    projections = jnp.swapaxes(projections, 0, 1).reshape(-1, channels)
+    step_weight, state_low = projections[:DT_RANK], projections[DT_RANK:]
+    inputs = inputs.astype(jnp.float32)
 
     scaled_first, inverse_first, normed_first = norm_forward(inputs, mixer_gain)
     normed_all = row_gather(normed_first)
+    count = normed_all.shape[0]
+    both_in = product(normed_all, in_low)
+    both_in, out_grad = lax.optimization_barrier((both_in, out_grad))
+    out_back_low = to_whole_features(out_grad)
     grad_all = row_gather(out_back_low)
-    both_in = product(normed_all, in_low)
     mixer_in, gate_in = both_in[:, :channels], both_in[:, channels:]
-    count = mixer_in.shape[0]
-    earlier = shift(mixer_in[-ROWS:], "col", 1)
-    padded = jnp.concatenate([earlier[ROWS - CONV + 1 :], mixer_in], axis=0)
+    mixer_in = mixer_in.reshape(rows, -1, channels)
+    length = mixer_in.shape[1]
+    tails = mixer_in[:, -ROWS:]
+    outside = shift(block_at(tails, (rows - 1) ^ order), "col", 1)
+    earlier = neighbours(outside, tails, order, -1)
+    padded = jnp.concatenate([earlier[:, ROWS - CONV + 1 :], mixer_in], axis=1)
     conv_out = conv_bias_row + sum(
-        padded[k : k + count] * taps[k : k + 1] for k in range(CONV)
-    )
+        padded[:, k : k + length] * taps[k : k + 1] for k in range(CONV)
+    ).reshape(count, channels)
     conv_act = low(sigmoid_linear(conv_out))
-    projected = row_total(product(conv_act, state_low))
+    projected = row_total(product(conv_act, state_low, contract_last))
     step_low = low(projected[:, :DT_RANK])
     in_wide = widen(projected[:, DT_RANK : DT_RANK + STATE])
     out_wide = widen(projected[:, DT_RANK + STATE :])
@@ -559,13 +683,15 @@
     drive = step_size * act_float
     rate = decay_rate * LOG2E
     step_total = jnp.sum(step_size, axis=0, keepdims=True)
-    handed = chunk_state(step_size, drive, in_wide, rate, False)
+    handed = chunk_state(order, step_size, drive, in_wide, rate, False)
     entry = chunk_entry(handed, step_total, rate, 1)
-    scanned, before, last = scan_forward(step_size, drive, in_wide, out_wide, rate, entry)
+    scanned, before, last = scan_forward(
+        order, step_size, drive, in_wide, out_wide, rate, entry
+    )
     scan_out = scanned + skip_row * act_float
     gate_act = sigmoid_linear(gate_in)
     gated = low(scan_out * gate_act)
-    middle = inputs + row_scatter(product(gated, mixer_low))
+    middle = inputs + row_scatter(product(gated, mixer_low, contract_last))
 
     scaled_second, inverse_second, normed_second = norm_forward(middle, feed_gain)
     normed_feed = row_gather(normed_second)
@@ -573,76 +699,142 @@
     gate_pre, up_pre = both_pre[:, :units], both_pre[:, units:]
     gate_swish = sigmoid_linear(gate_pre)
     hidden = low(gate_swish * up_pre)
-    feed_down_grad = low(product(hidden, grad_all, contract_first))
-    hidden, feed_down_grad = lax.optimization_barrier((hidden, feed_down_grad))
-    down_own = scatter_gradient(feed_down_grad, 1)
-    output = to_feature_blocks(low(middle + row_scatter(product(hidden, feed_down_low))))
-
-    hidden_back = product(grad_all, feed_down_low, contract_last)
+    grad_own, grad_other = feature_halves(grad_all)
+    down_grad = add_pair(
+        product(grad_own, hidden, contract_first),
+        low(product(grad_other, hidden, contract_first)),
+    )
+    feed_down_low, down_grad = lax.optimization_barrier((feed_down_low, down_grad))
+    down_own = scatter_gradient(down_grad)
+
+    hidden_back = product(grad_all, feed_down_low)
     gate_back = low(hidden_back * up_pre * sigmoid_slope(gate_pre))
     up_back = low(hidden_back * gate_swish)
     both_back = jnp.concatenate([gate_back, up_back], axis=1)
-    feed_grad = low(product(normed_feed, both_back, contract_first))
-    both_back, feed_grad = lax.optimization_barrier((both_back, feed_grad))
-    feed_own = scatter_gradient(feed_grad, 0)
-    normed_back = row_scatter(product(both_back, feed_low, contract_last))
+    feed_left, feed_right = feature_halves(normed_feed)
+    other_grad = low(product(feed_right, both_back, contract_first))
+    both_back, other_grad = lax.optimization_barrier((both_back, other_grad))
+    normed_back = product(both_back, feed_low, contract_last)
+    feed_grad = add_pair(product(feed_left, both_back, contract_first), other_grad)
+    normed_back, feed_grad = lax.optimization_barrier((normed_back, feed_grad))
+    feed_own = scatter_gradient(feed_grad)
+    normed_back = row_scatter(normed_back)
     middle_norm, feed_norm_part = norm_backward(
         normed_back, scaled_second, inverse_second, feed_gain
     )
     middle_back = out_back_low.astype(jnp.float32) + middle_norm
-    middle_all = row_gather(low(middle_back))
-
-    mixer_out_grad = low(product(gated, middle_all, contract_first))
-    middle_all, mixer_out_grad = lax.optimization_barrier((middle_all, mixer_out_grad))
-    mixer_own = scatter_gradient(mixer_out_grad, 1)
-    mixer_out_grad = both_halves(mixer_own, 1)
-    gated_back = product(middle_all, mixer_low, contract_last)
+    middle_low, down_own = lax.optimization_barrier((low(middle_back), down_own))
+    middle_all = row_gather(middle_low)
+
+    gated_back = product(middle_all, mixer_low)
     scan_back = gated_back * gate_act
     gate_in_back = low(gated_back * scan_out * sigmoid_slope(gate_in))
-    in_gate_grad = low(product(normed_all, gate_in_back, contract_first))
-    scan_back, in_gate_grad = lax.optimization_barrier((scan_back, in_gate_grad))
-    gate_own = scatter_gradient(in_gate_grad, 0)
-    in_gate_grad = both_halves(gate_own, 0)
-    handed_back = chunk_state(step_size, scan_back, out_wide, rate, True)
+    normed_own, normed_other = feature_halves(normed_all)
+    middle_own, middle_other = feature_halves(middle_all)
+    pair_own = jnp.concatenate(
+        [
+            product(middle_own, gated, contract_first),
+            product(normed_own, gate_in_back, contract_first),
+        ],
+        axis=1,
+    )
+    pair_other = jnp.concatenate(
+        [
+            low(product(middle_other, gated, contract_first)),
+            low(product(normed_other, gate_in_back, contract_first)),
+        ],
+        axis=1,
+    )
+    scan_back, hidden, pair_other = lax.optimization_barrier((scan_back, hidden, pair_other))
+    pair_grad = add_pair(pair_own, pair_other)
+    output = low(middle + row_scatter(product(hidden, feed_down_low, contract_last)))
+    handed_back = chunk_state(order, step_size, scan_back, out_wide, rate, True)
     entry_back = chunk_entry(handed_back, step_total, rate, -1)
-    rate_sum, in_sum, decay_sum, in_back, out_back = scan_backward(
-        step_size, drive, scan_back, in_wide, out_wide, rate, entry_back, before, last
+    rate_sum, in_sum, decay_sum, coefficient_back = scan_backward(
+        order,
+        step_size,
+        drive,
+        scan_back,
+        in_wide,
+        out_wide,
+        rate,
+        entry_back,
+        before,
+        last,
+    )
+    rate_sum, in_sum, coefficient_back, pair_grad, output = lax.optimization_barrier(
+        (rate_sum, in_sum, coefficient_back, pair_grad, output)
     )
     step_back = rate_sum * LN2 + act_float * in_sum
     act_scan = step_size * in_sum + skip_row * scan_back
     pre_back = step_back * jax.nn.sigmoid(step_pre)
     pre_low = low(pre_back)
     rank_back = product(pre_low, step_weight, contract_last)
-    proj_back = low(row_total(jnp.concatenate([rank_back, in_back, out_back], axis=1)))
-    act_back = act_scan + product(proj_back, state_low, contract_last)
+    partial = jnp.concatenate([rank_back, coefficient_back], axis=1)
+    local, pair_grad, feed_own = lax.optimization_barrier((partial, pair_grad, feed_own))
+    proj_back = low(row_total(partial, local))
+    pair_own = scatter_gradient(pair_grad)
+    act_back = act_scan + product(proj_back, state_low)
     conv_back = act_back * sigmoid_slope(conv_out)
-    later = shift(conv_back[:ROWS], "col", -1)
-    trailing = jnp.concatenate([conv_back, later[: CONV - 1]], axis=0)
+    conv_blocks = conv_back.reshape(rows, length, channels)
+    heads = conv_blocks[:, :ROWS]
+    outside = shift(block_at(heads, order), "col", -1)
+    later = neighbours(outside, heads, order, 1)
+    trailing = jnp.concatenate([conv_blocks, later[:, : CONV - 1]], axis=1)
     mixer_back = low(
         sum(
-            trailing[CONV - 1 - k : CONV - 1 - k + count] * taps[k : k + 1]
+            trailing[:, CONV - 1 - k : CONV - 1 - k + length] * taps[k : k + 1]
             for k in range(CONV)
         )
-    )
-    in_value_grad = low(product(normed_all, mixer_back, contract_first))
-    mixer_back, in_value_grad, down_own, feed_own = lax.optimization_barrier(
-        (mixer_back, in_value_grad, down_own, feed_own)
-    )
-    feed_down_grad = both_halves(down_own, 1)
-    feed_grad = both_halves(feed_own, 0)
-    in_value_grad = both_halves(scatter_gradient(in_value_grad, 0), 0)
+    ).reshape(count, channels)
     both_in_back = jnp.concatenate([mixer_back, gate_in_back], axis=1)
-    normed_first_back = row_scatter(product(both_in_back, in_low, contract_last))
+    normed_first_back = product(both_in_back, in_low, contract_last)
+    mixer_back, normed_first_back = lax.optimization_barrier((mixer_back, normed_first_back))
+    in_value_grad = add_pair(
+        product(normed_own, mixer_back, contract_first),
+        low(product(normed_other, mixer_back, contract_first)),
+    )
     input_norm, mixer_norm_part = norm_backward(
-        normed_first_back, scaled_first, inverse_first, mixer_gain
-    )
-    tokens_grad = to_feature_blocks(low(middle_back + input_norm)).astype(jnp.float32)
+        row_scatter(normed_first_back), scaled_first, inverse_first, mixer_gain
+    )
+    tokens_grad = low(middle_back + input_norm)
+
+    def whole(own, after):
+        own, _ = lax.optimization_barrier((own, after))
+        return both_halves(own, 0)
+
+    feed_grad = whole(feed_own, proj_back)
+    down_grad = whole(down_own, proj_back)
+    finished = (
+        feed_grad[:, :units].astype(jnp.float32),
+        feed_grad[:, units:].astype(jnp.float32),
+        down_grad.T.astype(jnp.float32),
+    )
+    gain_parts = jnp.concatenate([mixer_norm_part, feed_norm_part], axis=0)
+    in_value_grad, pair_own, tokens_grad, output, gain_parts, *finished = (
+        lax.optimization_barrier(
+            (in_value_grad, pair_own, tokens_grad, output, gain_parts) + finished
+        )
+    )
+    feed_gate_out, feed_up_out, feed_down_out = finished
+    value_own = scatter_gradient(in_value_grad)
+    pair_grad = both_halves(pair_own, 0)
+    finished = (
+        pair_grad[:, channels:].astype(jnp.float32),
+        pair_grad[:, :channels].T.astype(jnp.float32),
+    )
 
     def over_tokens(values):
         return jnp.sum(values, axis=0, keepdims=True)
 
+    gain_parts = gain_parts.reshape(2, lax.axis_size("col"), -1, own_channels)
+    gain_parts = jnp.swapaxes(gain_parts, 1, 2).reshape(gain_rows, channels)
     packed_grad = jnp.concatenate(
-        [over_tokens(conv_back * padded[k : k + count]) for k in range(CONV)]
+        [gain_parts]
+        + [
+            jnp.sum(conv_blocks * padded[:, k : k + length], axis=(0, 1))[None]
+            for k in range(CONV)
+        ]
         + [
             over_tokens(conv_back),
             over_tokens(pre_back),
@@ -651,38 +843,56 @@
         ],
         axis=0,
     )
-
-    def over_group(values, axis, dtype):
-        own = scatter_by_swaps(values, "col", axis, dtype)
+    projection_grad = jnp.concatenate(
+        [
+            product(step_low, pre_low, contract_first),
+            product(proj_back, conv_act, contract_first),
+        ],
+        axis=0,
+    )
+    (output, tokens_grad), (packed_grad, projection_grad) = to_feature_blocks(
+        (output, tokens_grad), (packed_grad, projection_grad)
+    )
+
+    def over_group(values, dtype):
+        own = scatter_by_swaps(values, "col", 1, dtype)
         return own + swap(own, "dp", 1)
 
-    packed_grad = over_group(packed_grad, 1, jnp.float32)
-    state_proj_grad = over_group(
-        product(conv_act, proj_back, contract_first), 0, jnp.bfloat16
-    )
-    step_proj_grad = over_group(product(step_low, pre_low, contract_first), 1, jnp.bfloat16)
-    gain_sums = scatter_by_swaps(
-        jnp.concatenate([mixer_norm_part, feed_norm_part], axis=0), "col", 1, jnp.float32
-    )
-    gain_sums = lax.psum(gain_sums, ("dp", "row"))
+    packed_grad = over_group(packed_grad, jnp.float32)
+    half = projection_grad.shape[0] // 2
+    mine, others = (
+        lax.dynamic_slice_in_dim(projection_grad, place * half, half, 0)
+        for place in (index, 1 - index)
+    )
+    mine = mine + swap(others, "dp", 1)
+    projection_grad = both_halves(scatter_by_swaps(mine, "col", 1, jnp.bfloat16), 0)
+    gain_sums = packed_grad[:gain_rows]
+    distance = 1
+    while distance < rows:
+        gain_sums = gain_sums + swap(gain_sums, "row", distance)
+        distance *= 2
+    gain_sums = gain_sums.reshape(2, -1)
+    packed_grad = packed_grad[gain_rows:]
+    value_own, *finished = lax.optimization_barrier((value_own,) + finished)
+    gate_out, mixer_out_grad = finished
     return (
         output,
-        tokens_grad,
+        tokens_grad.astype(jnp.float32),
         gain_sums[0],
-        in_value_grad,
-        in_gate_grad,
+        both_halves(value_own, 0).astype(jnp.float32),
+        gate_out,
         packed_grad[:CONV].T,
         packed_grad[CONV],
-        state_proj_grad,
-        step_proj_grad,
+        projection_grad[DT_RANK:].T,
+        projection_grad[:DT_RANK],
         packed_grad[CONV + 1],
         packed_grad[CONV + 3 :].T,
         packed_grad[CONV + 2],
         mixer_out_grad,
         gain_sums[1],
-        feed_grad[:, :units],
-        feed_grad[:, units:],
-        feed_down_grad,
+        feed_gate_out,
+        feed_up_out,
+        feed_down_out,
     )
 
 

time: 930 us -> 856 us (0.920)
  waiting for transfers between devices: 441 us -> 356 us
  starting transfers between devices: 119 us -> 140 us
  blocking collectives: 15 us -> 0 us
    all_gather x4 -> x3, waiting for transfers between devices: 143 us -> 82.4 us  [gather_weight(): return lax.all_gather(low(part), ('col', 'dp'), axis=0, tiled=True)]
    reduce_scatter x5 -> x4, waiting for transfers between devices: 83.5 us -> 26.1 us  [scatter_gradient(): return lax.psum_scatter(gradient, 'col', scatter_dimension=0, tiled=True)]
    all_to_all x0 -> x1, waiting for transfers between devices: none -> 31.7 us  [to_feature_blocks(): pieces = lax.all_to_all(pieces, 'col', split_axis=0, concat_axis=0)]
    unnamed x224 -> x295, local copies, waits for them, and re-layouts: 11 us -> 26.9 us
    psum x1 -> x0, blocking collectives: 15 us -> none  [body(): gain_sums = lax.psum(gain_sums, ('dp', 'row'))]
    ppermute x86 -> x71, starting transfers between devices: 104 us -> 116 us  [swap(): lax.ppermute(values, axis, [(i, i ^ distance) for i in range(lax.axis_siz...]
    convert_element_type x6 -> x14, other arithmetic: 12.8 us -> 24.7 us  [low(): return values.astype(jnp.bfloat16)]
    dot_general x19 -> x24, matrix products: 127 us -> 136 us  [product(): lax.dot_general(multiplicand, multiplier, dims, preferred_element_type=jn...]
  transfers between devices with their start and end apart: 103 -> 87, of which waited for: 47 -> 36; matrix products, arithmetic and copies ran while one was open for 24% -> 25% of each run, Pallas kernels for 7% -> 9%
where the time goes in v3:
time: 856 us; the launch traced here: 848 us
  waiting for transfers between devices  356 us (42%)
  starting transfers between devices  140 us (16%)
  matrix products  136 us (16%)
  Pallas kernels  73.9 us (9%)
  other arithmetic  72.3 us (8%)
  local copies, waits for them, and re-layouts  52.7 us (6%)
  between operations  17.2 us (2%)
    ppermute x71, waiting for transfers between devices, swap(): lax.ppermute(values, axis, [(i, i ^ distance) for i in range(lax.axis_siz...  194 us
    dot_general x24, matrix products, product(): lax.dot_general(multiplicand, multiplier, dims, preferred_element_type=jn...  136 us
    ppermute x71, starting transfers between devices, swap(): lax.ppermute(values, axis, [(i, i ^ distance) for i in range(lax.axis_siz...  116 us
    all_gather x3, waiting for transfers between devices, gather_weight(): return lax.all_gather(low(part), ('col', 'dp'), axis=0, tiled=True)  82.4 us
    pallas_call x4, Pallas kernels, call(): return lambda *operands: call(self.order.reshape(1), *operands)  73.9 us
    all_to_all x1, waiting for transfers between devices, to_feature_blocks(): pieces = lax.all_to_all(pieces, 'col', split_axis=0, concat_axis=0)  31.7 us
    unnamed x295, local copies, waits for them, and re-layouts  26.9 us
    reduce_scatter x4, waiting for transfers between devices, scatter_gradient(): return lax.psum_scatter(gradient, 'col', scatter_dimension=0, tiled=True)  26.1 us
  transfers between devices with their start and end apart: 87, of which 36 were waited for; matrix products, arithmetic and copies ran while one was open for 25% of the time, Pallas kernels for 9%

profile of v3, /device:TPU:1, one launch (start us, length us, event | category | flops | bytes accessed | tf_op | source)
XLA Modules:
  0.0 848.1 jit_solution(6969159138671906151)
XLA Ops:
  29.0 4.8 collective-permute-done.2
  37.7 5.8 collective-permute-done.3
  43.5 13.8 %collective-permute-done.4 = bf16[1,128,512]{2,1,0:T(8,128)(2,1)S(1)} collective-permute-done((bf16[1,128,512]{2,1,0:T(8,128)(2,1)S(1)}, bf16[1,128,512]{2,1,0:T(8,128)(2,1)S(1)}, u32[]{:S(2)}, u32[]{:S(2)}) %collective-permute-start.4) | collective-permute-done | bytes 131104 | tf_op jit(solution)/shard_map/ppermute | solution.py:41
  57.5 5.9 collective-permute-start.13
  65.9 15.6 %collective-permute-done.13 = bf16[1,144,256]{1,2,0:T(8,128)(2,1)S(1)} collective-permute-done((bf16[1,144,256]{1,2,0:T(8,128)(2,1)S(1)}, bf16[1,144,256]{1,2,0:T(8,128)(2,1)S(1)}, u32[]{:S(2)}, u32[]{:S(2)}) %collective-permute-start.13) | collective-permute-done | bytes 73760 | tf_op jit(solution)/shard_map/ppermute | solution.py:41
  81.6 16.1 %collective-permute-start.16 = (bf16[4,144,256]{1,2,0:T(8,128)(2,1)S(1)}, bf16[4,144,256]{1,2,0:T(8,128)(2,1)S(1)}, u32[]{:S(2)}, u32[]{:S(2)}) collective-permute-start(bf16[4,144,256]{1,2,0:T(8,128)(2,1)S(1)} %constant_dynamic-update-slice_fusion.9), channel_id=1, source_target_pairs={{0,16},{16,0},{1,17},{17,1},{2,18},{18,2},{3,19},{19,3},{4,20},{20... | collective-permute-start | bytes 884744 | tf_op jit(solution)/shard_map/ppermute | solution.py:41
  101.2 11.4 %collective-permute-done.11 = bf16[128,2048]{1,0:T(8,128)(2,1)S(1)} collective-permute-done((bf16[128,2048]{1,0:T(8,128)(2,1)S(1)}, bf16[128,2048]{1,0:T(8,128)(2,1)S(1)}, u32[]{:S(2)}, u32[]{:S(2)}) %collective-permute-start.11) | collective-permute-done | bytes 524320 | tf_op jit(solution)/shard_map/ppermute | solution.py:41
  112.6 11.5 %collective-permute-done.10 = bf16[128,2048]{1,0:T(8,128)(2,1)S(1)} collective-permute-done((bf16[128,2048]{1,0:T(8,128)(2,1)S(1)}, bf16[128,2048]{1,0:T(8,128)(2,1)S(1)}, u32[]{:S(2)}, u32[]{:S(2)}) %collective-permute-start.10) | collective-permute-done | bytes 524320 | tf_op jit(solution)/shard_map/ppermute | solution.py:41
  124.9 32.0 %all-gather.4.cloned.1.call-done = bf16[2048,3072]{0,1:T(8,128)(2,1)} async-done(((bf16[256,3072]{0,1:T(8,128)(2,1)}), bf16[2048,3072]{0,1:T(8,128)(2,1)}) %all-gather.4.cloned.1.call-update) | async-done | bytes 12582928 | tf_op jit(solution)/shard_map/all_gather | solution.py:186
  156.9 8.4 fusion.3
  186.9 7.2 collective-permute-done.23
  203.9 9.4 %chunk_state.1 = f32[16,1024]{1,0:T(8,128)} custom-call(s32[1]{0:T(128)} %bitcast.50._, f32[512,1024]{1,0:T(8,128)} %copy-done, f32[512,1024]{1,0:T(8,128)} %copy-done, f32[512,1024]{1,0:T(8,128)} %copy-done, f32[512,1024]{1,0:T(8,128)} %copy-done, f32[512,1024]{1,0:T(8,128)} %copy-done, f32[512,1024]{1,0:T(8,128)} %copy-done, f32[512,1024]{1,0:T(8,128)} %copy-done, ...), custom_call_target="tpu_custom_call" | custom-call | tf_op jit(solution)/shard_map/chunk_state/pallas_call | solution.py:318
  214.1 5.0 collective-permute-start.27
  223.8 7.5 collective-permute-done.26
  234.6 19.4 %scan_forward.1 = (f32[512,1024]{1,0:T(8,128)}, f32[512,16,1024]{2,1,0:T(8,128)}, f32[16,1024]{1,0:T(8,128)}) custom-call(s32[1]{0:T(128)} %bitcast.50._, f32[512,1024]{1,0:T(8,128)} %copy-done, f32[512,1024]{1,0:T(8,128)} %copy-done, f32[512,1024]{1,0:T(8,128)} %copy-done, f32[512,1024]{1,0:T(8,128)} %copy-done, f32[512,1024]{1,0:T(8,128)} %copy-done, ...), custom_call_target="tpu_custom_call" | custom-call | tf_op jit(solution)/shard_map/scan_forward/pallas_call | solution.py:318
  256.4 4.9 fusion.127
  276.8 14.3 %collective-permute-done.30 = bf16[128,2048]{1,0:T(8,128)(2,1)S(1)} collective-permute-done((bf16[128,2048]{1,0:T(8,128)(2,1)S(1)}, bf16[128,2048]{1,0:T(8,128)(2,1)S(1)}, u32[]{:S(2)}, u32[]{:S(2)}) %collective-permute-start.30) | collective-permute-done | bytes 524320 | tf_op jit(solution)/shard_map/ppermute | solution.py:41
  299.4 14.2 %collective-permute-done.33 = bf16[128,2048]{1,0:T(8,128)(2,1)S(1)} collective-permute-done((bf16[128,2048]{1,0:T(8,128)(2,1)S(1)}, bf16[128,2048]{1,0:T(8,128)(2,1)S(1)}, u32[]{:S(2)}, u32[]{:S(2)}) %collective-permute-start.33) | collective-permute-done | bytes 524320 | tf_op jit(solution)/shard_map/ppermute | solution.py:41
  318.2 14.3 %collective-permute-done.36 = bf16[128,2048]{1,0:T(8,128)(2,1)S(1)} collective-permute-done((bf16[128,2048]{1,0:T(8,128)(2,1)S(1)}, bf16[128,2048]{1,0:T(8,128)(2,1)S(1)}, u32[]{:S(2)}, u32[]{:S(2)}) %collective-permute-start.36) | collective-permute-done | bytes 524320 | tf_op jit(solution)/shard_map/ppermute | solution.py:41
  333.3 12.8 %fusion.105 = f32[512,4096]{1,0:T(8,128)S(1)} fusion(bf16[2048,4096]{1,0:T(8,128)(2,1)} %all-gather.8.cloned.1.call-done, bf16[128,2048]{1,0:T(8,128)(2,1)} %copy-done.46, bf16[128,2048]{1,0:T(8,128)(2,1)} %copy-done.48, bf16[128,2048]{1,0:T(8,128)(2,1)} %collective-permute-done.35, bf16[128,2048]{1,0:T(8,128)(2,1)S(1)} %multiply_convert_fusion.7), kind=kOutput, calls=%fused_computation.344 | convolution fusion | flops 8598323200 | bytes 27262976 | tf_op jit(solution)/shard_map/dot_general | solution.py:33
  359.2 4.8 add_convert_fusion.1
  364.1 50.3 %all-gather.6.cloned.1.call-done = bf16[2048,2048]{0,1:T(8,128)(2,1)} async-done(((bf16[256,2048]{0,1:T(8,128)(2,1)}), bf16[2048,2048]{0,1:T(8,128)(2,1)}) %all-gather.6.cloned.1.call-update) | async-done | bytes 8388624 | tf_op jit(solution)/shard_map/all_gather | solution.py:186
  414.4 13.9 %multiply_convert_fusion.1 = (bf16[512,2048]{1,0:T(8,128)(2,1)S(1)}, bf16[512,2048]{1,0:T(8,128)(2,1)S(1)}) fusion(f32[512,4096]{1,0:T(8,128)} %copy-done.13, bf16[2048,2048]{0,1:T(8,128)(2,1)} %all-gather.6.cloned.1.call-done, bf16[128,2048]{1,0:T(8,128)(2,1)S(1)} %copy-done.43, bf16[128,2048]{1,0:T(8,128)(2,1)} %copy-done.44, ...), kind=kOutput, calls=%fused_computation.24 | convolution fusion | flops 4323278848 | bytes 23068672 | tf_op jit(solution)/shard_map/dot_general | solution.py:33
  430.7 7.8 convolution_convert_fusion
  438.9 17.2 %fusion.130 = f32[512,2048]{1,0:T(8,128)} fusion(bf16[512,4096]{1,0:T(8,128)(2,1)} %pad_maximum_fusion, bf16[2048,4096]{1,0:T(8,128)(2,1)} %all-gather.8.cloned.1.call-done), kind=kOutput, calls=%fused_computation.368 | convolution fusion | flops 8589934592 | bytes 25165824 | tf_op jit(solution)/shard_map/dot_general | solution.py:33
  456.2 10.1 %add_convert_fusion = bf16[1024,4096]{1,0:T(8,128)(2,1)} fusion(bf16[1024,4096]{1,0:T(8,128)(2,1)} %collective-permute-done.39, bf16[512,4096]{1,0:T(8,128)(2,1)S(1)} %copy-done.17, pred[]{:T(512)S(6)} %eq.36, bf16[512,256]{1,0:T(8,128)(2,1)S(1)} %copy-done.79, bf16[512,256]{1,0:T(8,128)(2,1)S(1)} %copy-done.68, bf16[512,256]{1,0:T(8,128)(2,1)S(1)} %copy-done.69, ...), kind=kOutput, calls=%fused_computation | convolution fusion | flops 4316463104 | bytes 23068672 | tf_op jit(solution)/shard_map/dot_general | solution.py:33
  471.9 11.7 %collective-permute-done.42 = bf16[128,2048]{1,0:T(8,128)(2,1)S(1)} collective-permute-done((bf16[128,2048]{1,0:T(8,128)(2,1)S(1)}, bf16[128,2048]{1,0:T(8,128)(2,1)S(1)}, u32[]{:S(2)}, u32[]{:S(2)}) %collective-permute-start.42) | collective-permute-done | bytes 524320 | tf_op jit(solution)/shard_map/ppermute | solution.py:41
  483.7 11.7 %collective-permute-done.41 = bf16[128,2048]{1,0:T(8,128)(2,1)S(1)} collective-permute-done((bf16[128,2048]{1,0:T(8,128)(2,1)S(1)}, bf16[128,2048]{1,0:T(8,128)(2,1)S(1)}, u32[]{:S(2)}, u32[]{:S(2)}) %collective-permute-start.41) | collective-permute-done | bytes 524320 | tf_op jit(solution)/shard_map/ppermute | solution.py:41
  499.1 14.4 %reduce-scatter.5.cloned.1.call-done = bf16[256,2048]{1,0:T(8,128)(2,1)} async-done(((bf16[1024,2048]{1,0:T(8,128)(2,1)}), bf16[256,2048]{1,0:T(8,128)(2,1)}) %reduce-scatter.5.cloned.1.call-update) | async-done | bytes 1048592 | tf_op jit(solution)/shard_map/reduce_scatter | solution.py:217
  518.3 8.2 collective-permute-done.43
  526.6 13.8 %collective-permute-done.44 = bf16[128,2048]{1,0:T(8,128)(2,1)S(1)} collective-permute-done((bf16[128,2048]{1,0:T(8,128)(2,1)S(1)}, bf16[128,2048]{1,0:T(8,128)(2,1)S(1)}, u32[]{:S(2)}, u32[]{:S(2)}) %collective-permute-start.44) | collective-permute-done | bytes 524320 | tf_op jit(solution)/shard_map/ppermute | solution.py:41
  545.0 6.7 multiply_convert_fusion.3
  555.1 9.2 %chunk_state_back.1 = f32[16,1024]{1,0:T(8,128)} custom-call(s32[1]{0:T(128)} %bitcast.50._, f32[512,1024]{1,0:T(8,128)} %copy-done, f32[512,1024]{1,0:T(8,128)} %copy-done, f32[512,1024]{1,0:T(8,128)} %copy-done, f32[512,1024]{1,0:T(8,128)} %copy-done, f32[512,1024]{1,0:T(8,128)} %copy-done, f32[512,1024]{1,0:T(8,128)} %copy-done, f32[512,1024]{1,0:T(8,128)} %copy-done, ...), custom_call_target="tpu_custom_call" | custom-call | tf_op jit(solution)/shard_map/chunk_state_back/pallas_call | solution.py:318
  568.3 4.9 fusion.77
  573.2 9.5 %fusion.128 = (bf16[512,2048]{1,0:T(8,128)(2,1)S(1)}, f32[512,2048]{1,0:T(8,128)}) fusion(bf16[512,2048]{1,0:T(8,128)(2,1)S(1)} %copy-done.20, bf16[2048,2048]{0,1:T(8,128)(2,1)} %all-gather.6.cloned.1.call-done), kind=kOutput, calls=%fused_computation.366 | convolution fusion | flops 4296015872 | bytes 16777216 | tf_op jit(solution)/shard_map/dot_general | solution.py:33
  591.8 10.0 %collective-permute-done.48 = f32[17,1024]{1,0:T(8,128)S(1)} collective-permute-done((f32[17,1024]{1,0:T(8,128)S(1)}, f32[17,1024]{1,0:T(8,128)S(1)}, u32[]{:S(2)}, u32[]{:S(2)}) %collective-permute-start.48) | collective-permute-done | bytes 69664 | tf_op jit(solution)/shard_map/ppermute | solution.py:49
  602.5 35.9 %scan_backward.1 = (f32[512,1024]{1,0:T(8,128)}, f32[512,1024]{1,0:T(8,128)}, f32[16,1024]{1,0:T(8,128)}, f32[1,512,128]{2,1,0:T(8,128)}) custom-call(s32[1]{0:T(128)} %bitcast.50._, f32[512,1024]{1,0:T(8,128)} %copy-done, f32[512,1024]{1,0:T(8,128)} %copy-done, f32[512,1024]{1,0:T(8,128)} %copy-done, f32[512,1024]{1,0:T(8,128)} %copy-done, ...), custom_call_target="tpu_custom_call" | custom-call | tf_op jit(solution)/shard_map/scan_backward/pallas_call | solution.py:318
  641.2 5.6 fusion
  655.3 4.8 collective-permute-done.53
  661.6 6.4 collective-permute-done.55
  670.7 7.0 multiply_reduce_fusion.1
  688.3 7.1 fusion.1
  702.1 7.2 collective-permute-start.61
  712.6 7.4 collective-permute-start.57
  736.1 11.7 %reduce-scatter.9.cloned.1.call-done = bf16[256,2048]{1,0:T(8,128)(2,1)} async-done(((bf16[1024,2048]{1,0:T(8,128)(2,1)}), bf16[256,2048]{1,0:T(8,128)(2,1)}) %reduce-scatter.9.cloned.1.call-update) | async-done | bytes 1048592 | tf_op jit(solution)/shard_map/reduce_scatter | solution.py:217
  761.6 5.3 copy.73
  770.7 31.7 %all-to-all-done = bf16[4,256,512]{2,1,0:T(8,128)(2,1)} async-done(((bf16[4,256,512]{2,1,0:T(8,128)(2,1)}), bf16[4,256,512]{2,1,0:T(8,128)(2,1)}, u32[]{:S(2)}, u32[]{:S(2)}) %all-to-all-start) | async-done | bytes 1048608 | tf_op jit(solution)/shard_map/all_to_all | solution.py:167
  829.9 5.0 collective-permute-start.78
  (626 shorter events, 257.2 us)
Async XLA Ops:
  7.2 149.7 %all-gather.4.cloned.1.call-start = ((), (), s32[]{:S(2)}) async-start(), calls=%async_computation.5 | async-start | bytes 14155776 | tf_op jit(solution)/shard_map/all_gather | solution.py:186
  13.3 320.0 %all-gather.8.cloned.1.call-start = ((), (), s32[]{:S(2)}) async-start(), calls=%async_computation.7 | async-start | bytes 18874368 | tf_op jit(solution)/shard_map/all_gather | solution.py:186
  17.3 397.1 %all-gather.6.cloned.1.call-start = ((), (), s32[]{:S(2)}) async-start(), calls=%async_computation.6 | async-start | bytes 9437184 | tf_op jit(solution)/shard_map/all_gather | solution.py:186
  28.4 485.2 %reduce-scatter.5.cloned.1.call-start = ((), (), s32[]{:S(2)}) async-start(), calls=%async_computation.8 | async-start | bytes 5242880 | tf_op jit(solution)/shard_map/reduce_scatter | solution.py:217
  34.2 23.0 %collective-permute-start.4 = (bf16[1,128,512]{2,1,0:T(8,128)(2,1)S(1)}, bf16[1,128,512]{2,1,0:T(8,128)(2,1)S(1)}, u32[]{:S(2)}, u32[]{:S(2)}) collective-permute-start(bf16[1,128,512]{2,1,0:T(8,128)(2,1)S(1)} %get-tuple-element.267), channel_id=1, source_target_pairs={{0,2},{1,3},{2,0},{3,1},{4,6},{5,7},{6,4},{7,5},{8,10},{9,11},{10,... | collective-permute-start | bytes 393224 | tf_op jit(solution)/shard_map/ppermute | solution.py:41
  37.6 19.6 %collective-permute-start.5 = (bf16[1,128,512]{2,1,0:T(8,128)(2,1)S(1)}, bf16[1,128,512]{2,1,0:T(8,128)(2,1)S(1)}, u32[]{:S(2)}, u32[]{:S(2)}) collective-permute-start(bf16[1,128,512]{2,1,0:T(8,128)(2,1)S(1)} %get-tuple-element.266), channel_id=1, source_target_pairs={{0,3},{1,2},{2,1},{3,0},{4,7},{5,6},{6,5},{7,4},{8,11},{9,10},{10,... | collective-permute-start | bytes 393224 | tf_op jit(solution)/shard_map/ppermute | solution.py:41
  57.5 24.0 %collective-permute-start.13 = (bf16[1,144,256]{1,2,0:T(8,128)(2,1)S(1)}, bf16[1,144,256]{1,2,0:T(8,128)(2,1)S(1)}, u32[]{:S(2)}, u32[]{:S(2)}) collective-permute-start(bf16[1,144,256]{1,2,0:T(8,128)(2,1)S(1)} %bitcast.304), channel_id=1, source_target_pairs={{0,1},{1,0},{2,3},{3,2},{4,5},{5,4},{6,7},{7,6},{8,9},{9,8},{10,11... | collective-permute-start | bytes 221192 | tf_op jit(solution)/shard_map/ppermute | solution.py:41
  63.5 18.1 %collective-permute-start.14 = (bf16[1,144,256]{1,2,0:T(8,128)(2,1)S(1)}, bf16[1,144,256]{1,2,0:T(8,128)(2,1)S(1)}, u32[]{:S(2)}, u32[]{:S(2)}) collective-permute-start(bf16[1,144,256]{1,2,0:T(8,128)(2,1)S(1)} %bitcast.305), channel_id=1, source_target_pairs={{0,2},{1,3},{2,0},{3,1},{4,6},{5,7},{6,4},{7,5},{8,10},{9,11},{10,... | collective-permute-start | bytes 221192 | tf_op jit(solution)/shard_map/ppermute | solution.py:41
  63.5 18.1 %collective-permute-start.15 = (bf16[1,144,256]{1,2,0:T(8,128)(2,1)S(1)}, bf16[1,144,256]{1,2,0:T(8,128)(2,1)S(1)}, u32[]{:S(2)}, u32[]{:S(2)}) collective-permute-start(bf16[1,144,256]{1,2,0:T(8,128)(2,1)S(1)} %bitcast.306), channel_id=1, source_target_pairs={{0,3},{1,2},{2,1},{3,0},{4,7},{5,6},{6,5},{7,4},{8,11},{9,10},{10,... | collective-permute-start | bytes 221192 | tf_op jit(solution)/shard_map/ppermute | solution.py:41
  81.6 19.1 %collective-permute-start.16 = (bf16[4,144,256]{1,2,0:T(8,128)(2,1)S(1)}, bf16[4,144,256]{1,2,0:T(8,128)(2,1)S(1)}, u32[]{:S(2)}, u32[]{:S(2)}) collective-permute-start(bf16[4,144,256]{1,2,0:T(8,128)(2,1)S(1)} %constant_dynamic-update-slice_fusion.9), channel_id=1, source_target_pairs={{0,16},{16,0},{1,17},{17,1},{2,18},{18,2},{3,19},{19,3},{4,20},{20... | collective-permute-start | bytes 884744 | tf_op jit(solution)/shard_map/ppermute | solution.py:41
  97.9 14.7 %collective-permute-start.11 = (bf16[128,2048]{1,0:T(8,128)(2,1)S(1)}, bf16[128,2048]{1,0:T(8,128)(2,1)S(1)}, u32[]{:S(2)}, u32[]{:S(2)}) collective-permute-start(bf16[128,2048]{1,0:T(8,128)(2,1)S(1)} %fusion.36), channel_id=1, source_target_pairs={{0,12},{4,8},{8,4},{12,0},{1,13},{5,9},{9,5},{13,1},{2,14},{6,10},... | collective-permute-start | bytes 1572872 | tf_op jit(solution)/shard_map/ppermute | solution.py:41
  100.2 23.9 %collective-permute-start.10 = (bf16[128,2048]{1,0:T(8,128)(2,1)S(1)}, bf16[128,2048]{1,0:T(8,128)(2,1)S(1)}, u32[]{:S(2)}, u32[]{:S(2)}) collective-permute-start(bf16[128,2048]{1,0:T(8,128)(2,1)S(1)} %fusion.36), channel_id=1, source_target_pairs={{0,8},{4,12},{8,0},{12,4},{1,9},{5,13},{9,1},{13,5},{2,10},{6,14},... | collective-permute-start | bytes 1572872 | tf_op jit(solution)/shard_map/ppermute | solution.py:41
  100.4 24.5 %collective-permute-start.9 = (bf16[128,2048]{1,0:T(8,128)(2,1)S(1)}, bf16[128,2048]{1,0:T(8,128)(2,1)}, u32[]{:S(2)}, u32[]{:S(2)}) collective-permute-start(bf16[128,2048]{1,0:T(8,128)(2,1)S(1)} %fusion.36), channel_id=1, source_target_pairs={{0,4},{4,0},{8,12},{12,8},{1,5},{5,1},{9,13},{13,9},{2,6},{6,2},{1... | collective-permute-start | bytes 1572872 | tf_op jit(solution)/shard_map/ppermute | solution.py:41
  176.5 18.1 %collective-permute-start.17 = (f32[512,160]{0,1:T(8,128)S(1)}, f32[512,160]{0,1:T(8,128)S(1)}, u32[]{:S(2)}, u32[]{:S(2)}) collective-permute-start(f32[512,160]{0,1:T(8,128)S(1)} %fusion.129), channel_id=1, source_target_pairs={{0,4},{4,0},{8,12},{12,8},{1,5},{5,1},{9,13},{13,9},{2,6},{6,2},{1... | collective-permute-start | bytes 983048 | tf_op jit(solution)/shard_map/ppermute | solution.py:41
  181.5 14.7 %collective-permute-start.18 = (f32[512,160]{0,1:T(8,128)S(1)}, f32[512,160]{0,1:T(8,128)S(1)}, u32[]{:S(2)}, u32[]{:S(2)}) collective-permute-start(f32[512,160]{0,1:T(8,128)S(1)} %fusion.129), channel_id=1, source_target_pairs={{0,8},{4,12},{8,0},{12,4},{1,9},{5,13},{9,1},{13,5},{2,10},{6,14},... | collective-permute-start | bytes 983048 | tf_op jit(solution)/shard_map/ppermute | solution.py:41
  184.1 35.0 %collective-permute-start.24 = (bf16[1,128,512]{2,1,0:T(8,128)(2,1)}, bf16[1,128,512]{2,1,0:T(8,128)(2,1)S(1)}, u32[]{:S(2)}, u32[]{:S(2)}) collective-permute-start(bf16[1,128,512]{2,1,0:T(8,128)(2,1)} %get-tuple-element.255), channel_id=1, source_target_pairs={{0,2},{1,3},{2,0},{3,1},{4,6},{5,7},{6,4},{7,5},{8,10},{9,11},{10,... | collective-permute-start | bytes 393224 | tf_op jit(solution)/shard_map/ppermute | solution.py:41
  194.1 71.4 %collective-permute-start.25 = (bf16[1,128,512]{2,1,0:T(8,128)(2,1)}, bf16[1,128,512]{2,1,0:T(8,128)(2,1)S(1)}, u32[]{:S(2)}, u32[]{:S(2)}) collective-permute-start(bf16[1,128,512]{2,1,0:T(8,128)(2,1)} %get-tuple-element.254), channel_id=1, source_target_pairs={{0,3},{1,2},{2,1},{3,0},{4,7},{5,6},{6,5},{7,4},{8,11},{9,10},{10,... | collective-permute-start | bytes 393224 | tf_op jit(solution)/shard_map/ppermute | solution.py:41
  262.5 28.6 %collective-permute-start.30 = (bf16[128,2048]{1,0:T(8,128)(2,1)S(1)}, bf16[128,2048]{1,0:T(8,128)(2,1)S(1)}, u32[]{:S(2)}, u32[]{:S(2)}) collective-permute-start(bf16[128,2048]{1,0:T(8,128)(2,1)S(1)} %get-tuple-element.227), channel_id=1, source_target_pairs={{0,8},{4,12},{8,0},{12,4},{1,9},{5,13},{9,1},{13,5},{2,10},{6,14},... | collective-permute-start | bytes 1572872 | tf_op jit(solution)/shard_map/ppermute | solution.py:41
  265.5 25.6 %collective-permute-start.29 = (bf16[128,2048]{1,0:T(8,128)(2,1)S(1)}, bf16[128,2048]{1,0:T(8,128)(2,1)S(1)}, u32[]{:S(2)}, u32[]{:S(2)}) collective-permute-start(bf16[128,2048]{1,0:T(8,128)(2,1)S(1)} %get-tuple-element.225), channel_id=1, source_target_pairs={{0,4},{4,0},{8,12},{12,8},{1,5},{5,1},{9,13},{13,9},{2,6},{6,2},{1... | collective-permute-start | bytes 1572872 | tf_op jit(solution)/shard_map/ppermute | solution.py:41
  265.6 29.6 %collective-permute-start.34 = (bf16[128,2048]{1,0:T(8,128)(2,1)S(1)}, bf16[128,2048]{1,0:T(8,128)(2,1)S(1)}, u32[]{:S(2)}, u32[]{:S(2)}) collective-permute-start(bf16[128,2048]{1,0:T(8,128)(2,1)S(1)} %pad_maximum_fusion.24), channel_id=1, source_target_pairs={{0,12},{4,8},{8,4},{12,0},{1,13},{5,9},{9,5},{13,1},{2,14},{6,10},... | collective-permute-start | bytes 1572872 | tf_op jit(solution)/shard_map/ppermute | solution.py:41
  266.9 46.7 %collective-permute-start.33 = (bf16[128,2048]{1,0:T(8,128)(2,1)S(1)}, bf16[128,2048]{1,0:T(8,128)(2,1)S(1)}, u32[]{:S(2)}, u32[]{:S(2)}) collective-permute-start(bf16[128,2048]{1,0:T(8,128)(2,1)S(1)} %pad_maximum_fusion.24), channel_id=1, source_target_pairs={{0,8},{4,12},{8,0},{12,4},{1,9},{5,13},{9,1},{13,5},{2,10},{6,14},... | collective-permute-start | bytes 1572872 | tf_op jit(solution)/shard_map/ppermute | solution.py:41
  272.7 40.8 %collective-permute-start.32 = (bf16[128,2048]{1,0:T(8,128)(2,1)S(1)}, bf16[128,2048]{1,0:T(8,128)(2,1)S(1)}, u32[]{:S(2)}, u32[]{:S(2)}) collective-permute-start(bf16[128,2048]{1,0:T(8,128)(2,1)S(1)} %pad_maximum_fusion.24), channel_id=1, source_target_pairs={{0,4},{4,0},{8,12},{12,8},{1,5},{5,1},{9,13},{13,9},{2,6},{6,2},{1... | collective-permute-start | bytes 1572872 | tf_op jit(solution)/shard_map/ppermute | solution.py:41
  291.8 26.4 %collective-permute-start.37 = (bf16[128,2048]{1,0:T(8,128)(2,1)S(1)}, bf16[128,2048]{1,0:T(8,128)(2,1)S(1)}, u32[]{:S(2)}, u32[]{:S(2)}) collective-permute-start(bf16[128,2048]{1,0:T(8,128)(2,1)S(1)} %multiply_convert_fusion.7), channel_id=1, source_target_pairs={{0,12},{4,8},{8,4},{12,0},{1,13},{5,9},{9,5},{13,1},{2,14},{6,10},... | collective-permute-start | bytes 1572872 | tf_op jit(solution)/shard_map/ppermute | solution.py:41
  293.3 39.2 %collective-permute-start.36 = (bf16[128,2048]{1,0:T(8,128)(2,1)S(1)}, bf16[128,2048]{1,0:T(8,128)(2,1)S(1)}, u32[]{:S(2)}, u32[]{:S(2)}) collective-permute-start(bf16[128,2048]{1,0:T(8,128)(2,1)S(1)} %multiply_convert_fusion.7), channel_id=1, source_target_pairs={{0,8},{4,12},{8,0},{12,4},{1,9},{5,13},{9,1},{13,5},{2,10},{6,14},... | collective-permute-start | bytes 1572872 | tf_op jit(solution)/shard_map/ppermute | solution.py:41
  295.3 38.0 %collective-permute-start.35 = (bf16[128,2048]{1,0:T(8,128)(2,1)S(1)}, bf16[128,2048]{1,0:T(8,128)(2,1)}, u32[]{:S(2)}, u32[]{:S(2)}) collective-permute-start(bf16[128,2048]{1,0:T(8,128)(2,1)S(1)} %multiply_convert_fusion.7), channel_id=1, source_target_pairs={{0,4},{4,0},{8,12},{12,8},{1,5},{5,1},{9,13},{13,9},{2,6},{6,2},{1... | collective-permute-start | bytes 1572872 | tf_op jit(solution)/shard_map/ppermute | solution.py:41
  438.5 17.6 %collective-permute-start.39 = (bf16[1024,4096]{1,0:T(8,128)(2,1)}, bf16[1024,4096]{1,0:T(8,128)(2,1)}, u32[]{:S(2)}, u32[]{:S(2)}) collective-permute-start(bf16[1024,4096]{1,0:T(8,128)(2,1)} %convolution_convert_fusion), channel_id=1, source_target_pairs={{0,16},{16,0},{1,17},{17,1},{2,18},{18,2},{3,19},{19,3},{4,20},{20... | collective-permute-start | bytes 25165832 | tf_op jit(solution)/shard_map/ppermute | solution.py:41
  438.8 229.9 %reduce-scatter.7.cloned.1.call-start = ((), (), s32[]{:S(2)}) async-start(), calls=%async_computation.9 | async-start | bytes 10485760 | tf_op jit(solution)/shard_map/reduce_scatter | solution.py:217
  466.4 281.4 %reduce-scatter.9.cloned.1.call-start = ((), (), s32[]{:S(2)}) async-start(), calls=%async_computation.10 | async-start | bytes 5242880 | tf_op jit(solution)/shard_map/reduce_scatter | solution.py:217
  471.4 24.0 %collective-permute-start.41 = (bf16[128,2048]{1,0:T(8,128)(2,1)S(1)}, bf16[128,2048]{1,0:T(8,128)(2,1)S(1)}, u32[]{:S(2)}, u32[]{:S(2)}) collective-permute-start(bf16[128,2048]{1,0:T(8,128)(2,1)S(1)} %get-tuple-element.208), channel_id=1, source_target_pairs={{0,8},{4,12},{8,0},{12,4},{1,9},{5,13},{9,1},{13,5},{2,10},{6,14},... | collective-permute-start | bytes 1572872 | tf_op jit(solution)/shard_map/ppermute | solution.py:41
  471.7 23.7 %collective-permute-start.40 = (bf16[128,2048]{1,0:T(8,128)(2,1)S(1)}, bf16[128,2048]{1,0:T(8,128)(2,1)S(1)}, u32[]{:S(2)}, u32[]{:S(2)}) collective-permute-start(bf16[128,2048]{1,0:T(8,128)(2,1)S(1)} %get-tuple-element.206), channel_id=1, source_target_pairs={{0,4},{4,0},{8,12},{12,8},{1,5},{5,1},{9,13},{13,9},{2,6},{6,2},{1... | collective-permute-start | bytes 1572872 | tf_op jit(solution)/shard_map/ppermute | solution.py:41
  516.5 23.9 %collective-permute-start.44 = (bf16[128,2048]{1,0:T(8,128)(2,1)S(1)}, bf16[128,2048]{1,0:T(8,128)(2,1)S(1)}, u32[]{:S(2)}, u32[]{:S(2)}) collective-permute-start(bf16[128,2048]{1,0:T(8,128)(2,1)S(1)} %get-tuple-element.75), channel_id=1, source_target_pairs={{0,8},{4,12},{8,0},{12,4},{1,9},{5,13},{9,1},{13,5},{2,10},{6,14},... | collective-permute-start | bytes 1572872 | tf_op jit(solution)/shard_map/ppermute | solution.py:41
  518.0 22.5 %collective-permute-start.45 = (bf16[128,2048]{1,0:T(8,128)(2,1)S(1)}, bf16[128,2048]{1,0:T(8,128)(2,1)S(1)}, u32[]{:S(2)}, u32[]{:S(2)}) collective-permute-start(bf16[128,2048]{1,0:T(8,128)(2,1)S(1)} %get-tuple-element.75), channel_id=1, source_target_pairs={{0,12},{4,8},{8,4},{12,0},{1,13},{5,9},{9,5},{13,1},{2,14},{6,10},... | collective-permute-start | bytes 1572872 | tf_op jit(solution)/shard_map/ppermute | solution.py:41
  553.4 87.8 %collective-permute-start.49 = (bf16[1024,2048]{1,0:T(8,128)(2,1)S(1)}, bf16[1024,2048]{1,0:T(8,128)(2,1)}, u32[]{:S(2)}, u32[]{:S(2)}) collective-permute-start(bf16[1024,2048]{1,0:T(8,128)(2,1)S(1)} %pad_maximum_fusion.1), channel_id=1, source_target_pairs={{0,16},{16,0},{1,17},{17,1},{2,18},{18,2},{3,19},{19,3},{4,20},{20... | collective-permute-start | bytes 12582920 | tf_op jit(solution)/shard_map/ppermute | solution.py:41
  565.2 24.2 %collective-permute-start.47 = (f32[17,1024]{1,0:T(8,128)S(1)}, f32[17,1024]{1,0:T(8,128)S(1)}, u32[]{:S(2)}, u32[]{:S(2)}) collective-permute-start(f32[17,1024]{1,0:T(8,128)S(1)} %pad_maximum_fusion.40), channel_id=1, source_target_pairs={{2,0},{3,1},{6,4},{7,5},{10,8},{11,9},{14,12},{15,13},{18,16},{19,... | collective-permute-start | bytes 208904 | tf_op jit(solution)/shard_map/ppermute | solution.py:49
  566.6 23.9 %collective-permute-start.46 = (f32[17,1024]{1,0:T(8,128)S(1)}, f32[17,1024]{1,0:T(8,128)S(1)}, u32[]{:S(2)}, u32[]{:S(2)}) collective-permute-start(f32[17,1024]{1,0:T(8,128)S(1)} %pad_maximum_fusion.40), channel_id=1, source_target_pairs={{1,0},{2,1},{3,2},{5,4},{6,5},{7,6},{9,8},{10,9},{11,10},{13,12},{... | collective-permute-start | bytes 208904 | tf_op jit(solution)/shard_map/ppermute | solution.py:49
  587.9 50.6 %collective-permute-start.52 = (bf16[128,2048]{1,0:T(8,128)(2,1)}, bf16[128,2048]{1,0:T(8,128)(2,1)S(1)}, u32[]{:S(2)}, u32[]{:S(2)}) collective-permute-start(bf16[128,2048]{1,0:T(8,128)(2,1)} %get-tuple-element.188), channel_id=1, source_target_pairs={{0,12},{4,8},{8,4},{12,0},{1,13},{5,9},{9,5},{13,1},{2,14},{6,10},... | collective-permute-start | bytes 1572872 | tf_op jit(solution)/shard_map/ppermute | solution.py:41
  589.1 49.4 %collective-permute-start.51 = (bf16[128,2048]{1,0:T(8,128)(2,1)}, bf16[128,2048]{1,0:T(8,128)(2,1)S(1)}, u32[]{:S(2)}, u32[]{:S(2)}) collective-permute-start(bf16[128,2048]{1,0:T(8,128)(2,1)} %get-tuple-element.189), channel_id=1, source_target_pairs={{0,8},{4,12},{8,0},{12,4},{1,9},{5,13},{9,1},{13,5},{2,10},{6,14},... | collective-permute-start | bytes 1572872 | tf_op jit(solution)/shard_map/ppermute | solution.py:41
  589.4 49.1 %collective-permute-start.50 = (bf16[128,2048]{1,0:T(8,128)(2,1)S(1)}, bf16[128,2048]{1,0:T(8,128)(2,1)}, u32[]{:S(2)}, u32[]{:S(2)}) collective-permute-start(bf16[128,2048]{1,0:T(8,128)(2,1)S(1)} %get-tuple-element.187), channel_id=1, source_target_pairs={{0,4},{4,0},{8,12},{12,8},{1,5},{5,1},{9,13},{13,9},{2,6},{6,2},{1... | collective-permute-start | bytes 1572872 | tf_op jit(solution)/shard_map/ppermute | solution.py:41
  700.4 22.6 %collective-permute-start.59 = (bf16[128,2048]{1,0:T(8,128)(2,1)}, bf16[128,2048]{1,0:T(8,128)(2,1)}, u32[]{:S(2)}, u32[]{:S(2)}) collective-permute-start(bf16[128,2048]{1,0:T(8,128)(2,1)} %get-tuple-element.186), channel_id=1, source_target_pairs={{0,8},{4,12},{8,0},{12,4},{1,9},{5,13},{9,1},{13,5},{2,10},{6,14},... | collective-permute-start | bytes 1572872 | tf_op jit(solution)/shard_map/ppermute | solution.py:41
  700.7 22.3 %collective-permute-start.58 = (bf16[128,2048]{1,0:T(8,128)(2,1)}, bf16[128,2048]{1,0:T(8,128)(2,1)}, u32[]{:S(2)}, u32[]{:S(2)}) collective-permute-start(bf16[128,2048]{1,0:T(8,128)(2,1)} %get-tuple-element.184), channel_id=1, source_target_pairs={{0,4},{4,0},{8,12},{12,8},{1,5},{5,1},{9,13},{13,9},{2,6},{6,2},{1... | collective-permute-start | bytes 1572872 | tf_op jit(solution)/shard_map/ppermute | solution.py:41
  702.1 27.1 %collective-permute-start.61 = (bf16[256,4096]{1,0:T(8,128)(2,1)}, bf16[256,4096]{1,0:T(8,128)(2,1)S(1)}, u32[]{:S(2)}, u32[]{:S(2)}) collective-permute-start(bf16[256,4096]{1,0:T(8,128)(2,1)} %reduce-scatter.7.cloned.1.call-done), channel_id=1, source_target_pairs={{0,16},{16,0},{1,17},{17,1},{2,18},{18,2},{3,19},{19,3},{4,20},{20... | collective-permute-start | bytes 6291464 | tf_op jit(solution)/shard_map/ppermute | solution.py:41
  709.4 17.2 %collective-permute-start.62 = (bf16[256,2048]{1,0:T(8,128)(2,1)}, bf16[256,2048]{1,0:T(8,128)(2,1)S(1)}, u32[]{:S(2)}, u32[]{:S(2)}) collective-permute-start(bf16[256,2048]{1,0:T(8,128)(2,1)} %reduce-scatter.5.cloned.1.call-done), channel_id=1, source_target_pairs={{0,16},{16,0},{1,17},{17,1},{2,18},{18,2},{3,19},{19,3},{4,20},{20... | collective-permute-start | bytes 3145736 | tf_op jit(solution)/shard_map/ppermute | solution.py:41
  712.6 20.8 %collective-permute-start.57 = (bf16[1024,1024]{1,0:T(8,128)(2,1)S(1)}, bf16[1024,1024]{1,0:T(8,128)(2,1)S(1)}, u32[]{:S(2)}, u32[]{:S(2)}) collective-permute-start(bf16[1024,1024]{1,0:T(8,128)(2,1)S(1)} %convolution_convert_fusion.2), channel_id=1, source_target_pairs={{0,16},{16,0},{1,17},{17,1},{2,18},{18,2},{3,19},{19,3},{4,20},{20... | collective-permute-start | bytes 6291464 | tf_op jit(solution)/shard_map/ppermute | solution.py:41
  750.1 17.2 %collective-permute-start.72 = (bf16[256,2048]{1,0:T(8,128)(2,1)}, bf16[256,2048]{1,0:T(8,128)(2,1)}, u32[]{:S(2)}, u32[]{:S(2)}) collective-permute-start(bf16[256,2048]{1,0:T(8,128)(2,1)} %reduce-scatter.9.cloned.1.call-done), channel_id=1, source_target_pairs={{0,16},{16,0},{1,17},{17,1},{2,18},{18,2},{3,19},{19,3},{4,20},{20... | collective-permute-start | bytes 3145736 | tf_op jit(solution)/shard_map/ppermute | solution.py:41
  752.0 50.4 %all-to-all-start = ((bf16[4,256,512]{2,1,0:T(8,128)(2,1)}), bf16[4,256,512]{2,1,0:T(8,128)(2,1)}, u32[]{:S(2)}, u32[]{:S(2)}) async-start(bf16[4,256,512]{2,1,0:T(8,128)(2,1)} %pad_maximum_fusion.22), calls=%async_computation.3 | async-start | bytes 2097152 | tf_op jit(solution)/shard_map/all_to_all | solution.py:167
  756.4 78.6 %reduce-scatter.11.cloned.1.call-start = ((), (), s32[]{:S(2)}) async-start(), calls=%async_computation.11 | async-start | bytes 2621440 | tf_op jit(solution)/shard_map/reduce_scatter | solution.py:217
  807.4 16.3 %collective-permute-start.63 = (bf16[1,256,512]{2,1,0:T(8,128)(2,1)S(1)}, bf16[1,256,512]{2,1,0:T(8,128)(2,1)S(1)}, u32[]{:S(2)}, u32[]{:S(2)}) collective-permute-start(bf16[1,256,512]{2,1,0:T(8,128)(2,1)S(1)} %get-tuple-element.234), channel_id=1, source_target_pairs={{0,4},{4,0},{8,12},{12,8},{1,5},{5,1},{9,13},{13,9},{2,6},{6,2},{1... | collective-permute-start | bytes 786440 | tf_op jit(solution)/shard_map/ppermute | solution.py:41
  808.6 15.1 %collective-permute-start.64 = (bf16[1,256,512]{2,1,0:T(8,128)(2,1)S(1)}, bf16[1,256,512]{2,1,0:T(8,128)(2,1)S(1)}, u32[]{:S(2)}, u32[]{:S(2)}) collective-permute-start(bf16[1,256,512]{2,1,0:T(8,128)(2,1)S(1)} %get-tuple-element.233), channel_id=1, source_target_pairs={{0,8},{4,12},{8,0},{12,4},{1,9},{5,13},{9,1},{13,5},{2,10},{6,14},... | collective-permute-start | bytes 786440 | tf_op jit(solution)/shard_map/ppermute | solution.py:41
  (181 other events, 2546.7 us)
Sparse Core Ops, SparseCore 0:
  13.4 143.4 all-gather.3
  159.1 163.6 all-gather.7
  325.0 89.3 all-gather.5
  438.9 74.5 reduce-scatter.4
  515.9 151.0 reduce-scatter.6
  669.2 78.5 reduce-scatter.8
  760.1 57.3 reduce-scatter.10

commit v4 on v3

--- a/solution.py
+++ b/solution.py
@@ -561,15 +561,21 @@
     return rate_sum, in_sum, decay, jnp.sum(coefficients, 0)[:, : 2 * STATE]
 
 
-def chunk_entry(state, step_total, rate, direction):
-    packed = jnp.concatenate([state, step_total], axis=0)
+def neighbour_totals(step_total, direction):
+    return [
+        shift(step_total, "col", direction * distance)
+        for distance in range(1, lax.axis_size("col") - 1)
+    ]
+
+
+def chunk_entry(state, totals, rate, direction):
+    last = lax.axis_size("col") - 1
     entry = None
-    for distance in range(lax.axis_size("col") - 1, 0, -1):
-        got = shift(packed, "col", direction * distance)
-        if entry is None:
-            entry = got[:STATE]
-        else:
-            entry = got[:STATE] + jnp.exp2(got[STATE:] * rate) * entry
+    for distance in range(last, 0, -1):
+        got = shift(low(state), "col", direction * distance).astype(jnp.float32)
+        if entry is not None:
+            got = got + jnp.exp2(totals[distance - 1] * rate) * entry
+        entry = got
     return entry
 
 
@@ -683,8 +689,11 @@
     drive = step_size * act_float
     rate = decay_rate * LOG2E
     step_total = jnp.sum(step_size, axis=0, keepdims=True)
+    earlier_totals = neighbour_totals(step_total, 1)
+    later_totals = neighbour_totals(step_total, -1)
     handed = chunk_state(order, step_size, drive, in_wide, rate, False)
-    entry = chunk_entry(handed, step_total, rate, 1)
+    entry = chunk_entry(handed, earlier_totals, rate, 1)
+    entry, later_totals = lax.optimization_barrier((entry, later_totals))
     scanned, before, last = scan_forward(
         order, step_size, drive, in_wide, out_wide, rate, entry
     )
@@ -749,7 +758,7 @@
     pair_grad = add_pair(pair_own, pair_other)
     output = low(middle + row_scatter(product(hidden, feed_down_low, contract_last)))
     handed_back = chunk_state(order, step_size, scan_back, out_wide, rate, True)
-    entry_back = chunk_entry(handed_back, step_total, rate, -1)
+    entry_back = chunk_entry(handed_back, later_totals, rate, -1)
     rate_sum, in_sum, decay_sum, coefficient_back = scan_backward(
         order,
         step_size,
@@ -817,7 +826,6 @@
         )
     )
     feed_gate_out, feed_up_out, feed_down_out = finished
-    value_own = scatter_gradient(in_value_grad)
     pair_grad = both_halves(pair_own, 0)
     finished = (
         pair_grad[:, channels:].astype(jnp.float32),
@@ -850,22 +858,22 @@
         ],
         axis=0,
     )
-    (output, tokens_grad), (packed_grad, projection_grad) = to_feature_blocks(
-        (output, tokens_grad), (packed_grad, projection_grad)
-    )
-
-    def over_group(values, dtype):
-        own = scatter_by_swaps(values, "col", 1, dtype)
-        return own + swap(own, "dp", 1)
-
-    packed_grad = over_group(packed_grad, jnp.float32)
+    (output, tokens_grad), (packed_grad, projection_grad, in_value_grad) = to_feature_blocks(
+        (output, tokens_grad), (packed_grad, projection_grad, in_value_grad)
+    )
+    value_own = scatter_gradient(in_value_grad)
+
     half = projection_grad.shape[0] // 2
     mine, others = (
         lax.dynamic_slice_in_dim(projection_grad, place * half, half, 0)
         for place in (index, 1 - index)
     )
-    mine = mine + swap(others, "dp", 1)
-    projection_grad = both_halves(scatter_by_swaps(mine, "col", 1, jnp.bfloat16), 0)
+    small = jnp.concatenate(
+        [mine + swap(others, "dp", 1), packed_grad + swap(packed_grad, "dp", 1)], axis=0
+    )
+    small = scatter_by_swaps(small, "col", 1, jnp.bfloat16)
+    projection_grad = both_halves(small[:half], 0)
+    packed_grad = small[half:]
     gain_sums = packed_grad[:gain_rows]
     distance = 1
     while distance < rows:

time: 856 us -> 844 us (0.986)
  starting transfers between devices: 140 us -> 123 us
  waiting for transfers between devices: 356 us -> 368 us
    ppermute x71 -> x68, waiting for transfers between devices: 194 us -> 235 us  [swap(): lax.ppermute(values, axis, [(i, i ^ distance) for i in range(lax.axis_siz...]
    ppermute x71 -> x68, starting transfers between devices: 116 us -> 92.9 us  [swap(): lax.ppermute(values, axis, [(i, i ^ distance) for i in range(lax.axis_siz...]
    all_gather x3, waiting for transfers between devices: 82.4 us -> 63.2 us  [gather_weight(): return lax.all_gather(low(part), ('col', 'dp'), axis=0, tiled=True)]
    all_to_all x1, waiting for transfers between devices: 31.7 us -> 19.1 us  [to_feature_blocks(): pieces = lax.all_to_all(pieces, 'col', split_axis=0, concat_axis=0)]
    ppermute x8 -> x12, starting transfers between devices: 19.3 us -> 24.8 us  [shift(): return lax.ppermute(values, axis, pairs)]
    ppermute x8 -> x12, waiting for transfers between devices: 21.7 us -> 19.2 us  [shift(): return lax.ppermute(values, axis, pairs)]
    unnamed x295 -> x305, local copies, waits for them, and re-layouts: 26.9 us -> 24.6 us
    convert_element_type x14 -> x16, other arithmetic: 24.7 us -> 26.6 us  [low(): return values.astype(jnp.bfloat16)]
  transfers between devices with their start and end apart: 87 -> 88, of which waited for: 36 -> 41; matrix products, arithmetic and copies ran while one was open for 25% -> 25% of each run, Pallas kernels for 9% -> 9%
where the time goes in v4:
time: 844 us; the launch traced here: 836 us
  waiting for transfers between devices  368 us (44%)
  matrix products  132 us (16%)
  starting transfers between devices  123 us (15%)
  Pallas kernels  74.4 us (9%)
  other arithmetic  72.6 us (9%)
  local copies, waits for them, and re-layouts  48.7 us (6%)
  between operations  17.3 us (2%)
    ppermute x68, waiting for transfers between devices, swap(): lax.ppermute(values, axis, [(i, i ^ distance) for i in range(lax.axis_siz...  235 us
    dot_general x24, matrix products, product(): lax.dot_general(multiplicand, multiplier, dims, preferred_element_type=jn...  132 us
    ppermute x68, starting transfers between devices, swap(): lax.ppermute(values, axis, [(i, i ^ distance) for i in range(lax.axis_siz...  92.9 us
    pallas_call x4, Pallas kernels, call(): return lambda *operands: call(self.order.reshape(1), *operands)  74.4 us
    all_gather x3, waiting for transfers between devices, gather_weight(): return lax.all_gather(low(part), ('col', 'dp'), axis=0, tiled=True)  63.2 us
    reduce_scatter x4, waiting for transfers between devices, scatter_gradient(): return lax.psum_scatter(gradient, 'col', scatter_dimension=0, tiled=True)  31.8 us
    convert_element_type x16, other arithmetic, low(): return values.astype(jnp.bfloat16)  26.6 us
    ppermute x12, starting transfers between devices, shift(): return lax.ppermute(values, axis, pairs)  24.8 us
  transfers between devices with their start and end apart: 88, of which 41 were waited for; matrix products, arithmetic and copies ran while one was open for 25% of the time, Pallas kernels for 9%

profile of v4, /device:TPU:1, one launch (start us, length us, event | category | flops | bytes accessed | tf_op | source)
XLA Modules:
  0.0 836.3 jit_solution(4091626203131574738)
XLA Ops:
  37.7 5.8 collective-permute-done.3
  43.5 13.8 %collective-permute-done.4 = bf16[1,128,512]{2,1,0:T(8,128)(2,1)S(1)} collective-permute-done((bf16[1,128,512]{2,1,0:T(8,128)(2,1)S(1)}, bf16[1,128,512]{2,1,0:T(8,128)(2,1)S(1)}, u32[]{:S(2)}, u32[]{:S(2)}) %collective-permute-start.4) | collective-permute-done | bytes 131104 | tf_op jit(solution)/shard_map/ppermute | solution.py:41
  57.5 5.9 collective-permute-start.13
  65.9 15.6 %collective-permute-done.13 = bf16[1,144,256]{1,2,0:T(8,128)(2,1)S(1)} collective-permute-done((bf16[1,144,256]{1,2,0:T(8,128)(2,1)S(1)}, bf16[1,144,256]{1,2,0:T(8,128)(2,1)S(1)}, u32[]{:S(2)}, u32[]{:S(2)}) %collective-permute-start.13) | collective-permute-done | bytes 73760 | tf_op jit(solution)/shard_map/ppermute | solution.py:41
  81.6 16.1 %collective-permute-start.16 = (bf16[4,144,256]{1,2,0:T(8,128)(2,1)S(1)}, bf16[4,144,256]{1,2,0:T(8,128)(2,1)S(1)}, u32[]{:S(2)}, u32[]{:S(2)}) collective-permute-start(bf16[4,144,256]{1,2,0:T(8,128)(2,1)S(1)} %constant_dynamic-update-slice_fusion.9), channel_id=1, source_target_pairs={{0,16},{16,0},{1,17},{17,1},{2,18},{18,2},{3,19},{19,3},{4,20},{20... | collective-permute-start | bytes 884744 | tf_op jit(solution)/shard_map/ppermute | solution.py:41
  101.2 11.4 %collective-permute-done.11 = bf16[128,2048]{1,0:T(8,128)(2,1)S(1)} collective-permute-done((bf16[128,2048]{1,0:T(8,128)(2,1)S(1)}, bf16[128,2048]{1,0:T(8,128)(2,1)S(1)}, u32[]{:S(2)}, u32[]{:S(2)}) %collective-permute-start.11) | collective-permute-done | bytes 524320 | tf_op jit(solution)/shard_map/ppermute | solution.py:41
  112.6 11.5 %collective-permute-done.10 = bf16[128,2048]{1,0:T(8,128)(2,1)S(1)} collective-permute-done((bf16[128,2048]{1,0:T(8,128)(2,1)S(1)}, bf16[128,2048]{1,0:T(8,128)(2,1)S(1)}, u32[]{:S(2)}, u32[]{:S(2)}) %collective-permute-start.10) | collective-permute-done | bytes 524320 | tf_op jit(solution)/shard_map/ppermute | solution.py:41
  124.9 32.0 %all-gather.4.cloned.1.call-done = bf16[2048,3072]{0,1:T(8,128)(2,1)} async-done(((bf16[256,3072]{0,1:T(8,128)(2,1)}), bf16[2048,3072]{0,1:T(8,128)(2,1)}) %all-gather.4.cloned.1.call-update) | async-done | bytes 12582928 | tf_op jit(solution)/shard_map/all_gather | solution.py:186
  156.9 8.4 %fusion.3 = f32[512,2048]{1,0:T(8,128)S(1)} fusion(bf16[2048,3072]{0,1:T(8,128)(2,1)} %all-gather.4.cloned.1.call-done, bf16[128,2048]{1,0:T(8,128)(2,1)} %copy-done.36, bf16[128,2048]{1,0:T(8,128)(2,1)} %copy-done.37, bf16[128,2048]{1,0:T(8,128)(2,1)} %collective-permute-done.9, bf16[128,2048]{1,0:T(8,128)(2,1)S(1)} %fusion.36), kind=kOutput, calls=%fused_computation.9 | convolution fusion | flops 4303355904 | bytes 14680064 | tf_op jit(solution)/shard_map/dot_general | solution.py:33
  186.4 7.8 collective-permute-done.23
  208.1 9.4 %chunk_state.1 = f32[16,1024]{1,0:T(8,128)} custom-call(s32[1]{0:T(128)} %bitcast.50._, f32[512,1024]{1,0:T(8,128)} %copy-done, f32[512,1024]{1,0:T(8,128)} %copy-done, f32[512,1024]{1,0:T(8,128)} %copy-done, f32[512,1024]{1,0:T(8,128)} %copy-done, f32[512,1024]{1,0:T(8,128)} %copy-done, f32[512,1024]{1,0:T(8,128)} %copy-done, f32[512,1024]{1,0:T(8,128)} %copy-done, ...), custom_call_target="tpu_custom_call" | custom-call | tf_op jit(solution)/shard_map/chunk_state/pallas_call | solution.py:318
  218.3 5.6 collective-permute-start.30
  233.8 5.5 collective-permute-done.31
  239.3 6.0 collective-permute-done.32
  247.9 19.7 %scan_forward.1 = (f32[512,1024]{1,0:T(8,128)}, f32[512,16,1024]{2,1,0:T(8,128)}, f32[16,1024]{1,0:T(8,128)}) custom-call(s32[1]{0:T(128)} %bitcast.50._, f32[512,1024]{1,0:T(8,128)} %copy-done, f32[512,1024]{1,0:T(8,128)} %copy-done, f32[512,1024]{1,0:T(8,128)} %copy-done, f32[512,1024]{1,0:T(8,128)} %copy-done, f32[512,1024]{1,0:T(8,128)} %copy-done, ...), custom_call_target="tpu_custom_call" | custom-call | tf_op jit(solution)/shard_map/scan_forward/pallas_call | solution.py:318
  280.5 8.9 %collective-permute-done.35 = bf16[128,2048]{1,0:T(8,128)(2,1)S(1)} collective-permute-done((bf16[128,2048]{1,0:T(8,128)(2,1)S(1)}, bf16[128,2048]{1,0:T(8,128)(2,1)S(1)}, u32[]{:S(2)}, u32[]{:S(2)}) %collective-permute-start.35) | collective-permute-done | bytes 524320 | tf_op jit(solution)/shard_map/ppermute | solution.py:41
  290.6 11.5 %collective-permute-done.34 = bf16[128,2048]{1,0:T(8,128)(2,1)S(1)} collective-permute-done((bf16[128,2048]{1,0:T(8,128)(2,1)S(1)}, bf16[128,2048]{1,0:T(8,128)(2,1)S(1)}, u32[]{:S(2)}, u32[]{:S(2)}) %collective-permute-start.34) | collective-permute-done | bytes 524320 | tf_op jit(solution)/shard_map/ppermute | solution.py:41
  305.0 6.9 collective-permute-done.38
  313.1 11.3 %collective-permute-done.37 = bf16[128,2048]{1,0:T(8,128)(2,1)S(1)} collective-permute-done((bf16[128,2048]{1,0:T(8,128)(2,1)S(1)}, bf16[128,2048]{1,0:T(8,128)(2,1)S(1)}, u32[]{:S(2)}, u32[]{:S(2)}) %collective-permute-start.37) | collective-permute-done | bytes 524320 | tf_op jit(solution)/shard_map/ppermute | solution.py:41
  334.3 12.0 %collective-permute-done.40 = bf16[128,2048]{1,0:T(8,128)(2,1)S(1)} collective-permute-done((bf16[128,2048]{1,0:T(8,128)(2,1)S(1)}, bf16[128,2048]{1,0:T(8,128)(2,1)S(1)}, u32[]{:S(2)}, u32[]{:S(2)}) %collective-permute-start.40) | collective-permute-done | bytes 524320 | tf_op jit(solution)/shard_map/ppermute | solution.py:41
  347.1 12.5 %fusion.109 = f32[512,4096]{1,0:T(8,128)S(1)} fusion(bf16[2048,4096]{1,0:T(8,128)(2,1)} %all-gather.8.cloned.1.call-done, bf16[128,2048]{1,0:T(8,128)(2,1)} %copy-done.42, bf16[128,2048]{1,0:T(8,128)(2,1)} %copy-done.44, bf16[128,2048]{1,0:T(8,128)(2,1)} %collective-permute-done.39, bf16[128,2048]{1,0:T(8,128)(2,1)S(1)} %multiply_convert_fusion.7), kind=kOutput, calls=%fused_computation.346 | convolution fusion | flops 8598323200 | bytes 27262976 | tf_op jit(solution)/shard_map/dot_general | solution.py:33
  377.8 31.2 %all-gather.6.cloned.1.call-done = bf16[2048,2048]{0,1:T(8,128)(2,1)} async-done(((bf16[256,2048]{0,1:T(8,128)(2,1)}), bf16[2048,2048]{0,1:T(8,128)(2,1)}) %all-gather.6.cloned.1.call-update) | async-done | bytes 8388624 | tf_op jit(solution)/shard_map/all_gather | solution.py:186
  409.1 13.9 %multiply_convert_fusion.1 = (bf16[512,2048]{1,0:T(8,128)(2,1)S(1)}, bf16[512,2048]{1,0:T(8,128)(2,1)S(1)}) fusion(f32[512,4096]{1,0:T(8,128)} %copy-done.12, bf16[2048,2048]{0,1:T(8,128)(2,1)} %all-gather.6.cloned.1.call-done, bf16[128,2048]{1,0:T(8,128)(2,1)S(1)} %copy-done.39, bf16[128,2048]{1,0:T(8,128)(2,1)} %copy-done.40, ...), kind=kOutput, calls=%fused_computation.24 | convolution fusion | flops 4323278848 | bytes 23068672 | tf_op jit(solution)/shard_map/dot_general | solution.py:33
  425.3 7.8 convolution_convert_fusion
  433.6 17.4 %fusion.134 = f32[512,2048]{1,0:T(8,128)} fusion(bf16[512,4096]{1,0:T(8,128)(2,1)} %pad_maximum_fusion, bf16[2048,4096]{1,0:T(8,128)(2,1)} %all-gather.8.cloned.1.call-done), kind=kOutput, calls=%fused_computation.370 | convolution fusion | flops 8589934592 | bytes 25165824 | tf_op jit(solution)/shard_map/dot_general | solution.py:33
  451.0 10.1 %add_convert_fusion = bf16[1024,4096]{1,0:T(8,128)(2,1)} fusion(bf16[1024,4096]{1,0:T(8,128)(2,1)} %collective-permute-done.43, bf16[512,4096]{1,0:T(8,128)(2,1)S(1)} %copy-done.15, pred[]{:T(512)S(6)} %eq.36, bf16[512,256]{1,0:T(8,128)(2,1)S(1)} %copy-done.96, bf16[512,256]{1,0:T(8,128)(2,1)S(1)} %copy-done.85, bf16[512,256]{1,0:T(8,128)(2,1)S(1)} %copy-done.86, ...), kind=kOutput, calls=%fused_computation | convolution fusion | flops 4316463104 | bytes 23068672 | tf_op jit(solution)/shard_map/dot_general | solution.py:33
  466.7 11.7 %collective-permute-done.46 = bf16[128,2048]{1,0:T(8,128)(2,1)S(1)} collective-permute-done((bf16[128,2048]{1,0:T(8,128)(2,1)S(1)}, bf16[128,2048]{1,0:T(8,128)(2,1)S(1)}, u32[]{:S(2)}, u32[]{:S(2)}) %collective-permute-start.46) | collective-permute-done | bytes 524320 | tf_op jit(solution)/shard_map/ppermute | solution.py:41
  478.4 11.8 %collective-permute-done.45 = bf16[128,2048]{1,0:T(8,128)(2,1)S(1)} collective-permute-done((bf16[128,2048]{1,0:T(8,128)(2,1)S(1)}, bf16[128,2048]{1,0:T(8,128)(2,1)S(1)}, u32[]{:S(2)}, u32[]{:S(2)}) %collective-permute-start.45) | collective-permute-done | bytes 524320 | tf_op jit(solution)/shard_map/ppermute | solution.py:41
  493.9 14.3 %reduce-scatter.5.cloned.1.call-done = bf16[256,2048]{1,0:T(8,128)(2,1)} async-done(((bf16[1024,2048]{1,0:T(8,128)(2,1)}), bf16[256,2048]{1,0:T(8,128)(2,1)}) %reduce-scatter.5.cloned.1.call-update) | async-done | bytes 1048592 | tf_op jit(solution)/shard_map/reduce_scatter | solution.py:217
  513.0 8.1 collective-permute-done.47
  521.2 13.9 %collective-permute-done.48 = bf16[128,2048]{1,0:T(8,128)(2,1)S(1)} collective-permute-done((bf16[128,2048]{1,0:T(8,128)(2,1)S(1)}, bf16[128,2048]{1,0:T(8,128)(2,1)S(1)}, u32[]{:S(2)}, u32[]{:S(2)}) %collective-permute-start.48) | collective-permute-done | bytes 524320 | tf_op jit(solution)/shard_map/ppermute | solution.py:41
  539.6 6.7 multiply_convert_fusion.3
  549.8 9.2 %chunk_state_back.1 = f32[16,1024]{1,0:T(8,128)} custom-call(s32[1]{0:T(128)} %bitcast.50._, f32[512,1024]{1,0:T(8,128)} %copy-done, f32[512,1024]{1,0:T(8,128)} %copy-done, f32[512,1024]{1,0:T(8,128)} %copy-done, f32[512,1024]{1,0:T(8,128)} %copy-done, f32[512,1024]{1,0:T(8,128)} %copy-done, f32[512,1024]{1,0:T(8,128)} %copy-done, f32[512,1024]{1,0:T(8,128)} %copy-done, ...), custom_call_target="tpu_custom_call" | custom-call | tf_op jit(solution)/shard_map/chunk_state_back/pallas_call | solution.py:318
  564.1 10.5 %fusion.132 = (bf16[512,2048]{1,0:T(8,128)(2,1)S(1)}, f32[512,2048]{1,0:T(8,128)}) fusion(bf16[512,2048]{1,0:T(8,128)(2,1)} %copy-done.17, bf16[2048,2048]{0,1:T(8,128)(2,1)} %all-gather.6.cloned.1.call-done), kind=kOutput, calls=%fused_computation.368 | convolution fusion | flops 4296015872 | bytes 16777216 | tf_op jit(solution)/shard_map/dot_general | solution.py:33
  586.9 36.2 %scan_backward.1 = (f32[512,1024]{1,0:T(8,128)}, f32[512,1024]{1,0:T(8,128)}, f32[16,1024]{1,0:T(8,128)}, f32[1,512,128]{2,1,0:T(8,128)}) custom-call(s32[1]{0:T(128)} %bitcast.50._, f32[512,1024]{1,0:T(8,128)} %copy-done, f32[512,1024]{1,0:T(8,128)} %copy-done, f32[512,1024]{1,0:T(8,128)} %copy-done, f32[512,1024]{1,0:T(8,128)} %copy-done, ...), custom_call_target="tpu_custom_call" | custom-call | tf_op jit(solution)/shard_map/scan_backward/pallas_call | solution.py:318
  626.1 5.7 fusion
  640.2 5.5 collective-permute-done.57
  647.2 6.3 collective-permute-done.59
  658.8 7.0 multiply_reduce_fusion.1
  668.7 7.0 collective-permute-done.60
  679.2 7.0 fusion.1
  692.0 9.1 %collective-permute-done.64 = bf16[128,2048]{1,0:T(8,128)(2,1)S(1)} collective-permute-done((bf16[128,2048]{1,0:T(8,128)(2,1)S(1)}, bf16[128,2048]{1,0:T(8,128)(2,1)S(1)}, u32[]{:S(2)}, u32[]{:S(2)}) %collective-permute-start.64) | collective-permute-done | bytes 524320 | tf_op jit(solution)/shard_map/ppermute | solution.py:41
  702.8 10.2 %collective-permute-done.63 = bf16[128,2048]{1,0:T(8,128)(2,1)S(1)} collective-permute-done((bf16[128,2048]{1,0:T(8,128)(2,1)S(1)}, bf16[128,2048]{1,0:T(8,128)(2,1)S(1)}, u32[]{:S(2)}, u32[]{:S(2)}) %collective-permute-start.63) | collective-permute-done | bytes 524320 | tf_op jit(solution)/shard_map/ppermute | solution.py:41
  724.2 14.5 %reduce-scatter.9.cloned.1.call-done = bf16[256,2048]{1,0:T(8,128)(2,1)} async-done(((bf16[1024,2048]{1,0:T(8,128)(2,1)}), bf16[256,2048]{1,0:T(8,128)(2,1)}) %reduce-scatter.9.cloned.1.call-update) | async-done | bytes 1048592 | tf_op jit(solution)/shard_map/reduce_scatter | solution.py:217
  753.3 19.1 %all-to-all-done = bf16[4,256,512]{2,1,0:T(8,128)(2,1)} async-done(((bf16[4,256,512]{2,1,0:T(8,128)(2,1)}), bf16[4,256,512]{2,1,0:T(8,128)(2,1)}, u32[]{:S(2)}, u32[]{:S(2)}) %all-to-all-start) | async-done | bytes 1048608 | tf_op jit(solution)/shard_map/all_to_all | solution.py:167
  772.4 5.3 copy.73
  788.7 5.7 collective-permute-done.69
  803.4 9.3 %collective-permute-done.73 = bf16[171,256]{1,0:T(8,128)(2,1)S(1)} collective-permute-done((bf16[171,256]{1,0:T(8,128)(2,1)S(1)}, bf16[171,256]{1,0:T(8,128)(2,1)S(1)}, u32[]{:S(2)}, u32[]{:S(2)}) %collective-permute-start.73) | collective-permute-done | bytes 87584 | tf_op jit(solution)/shard_map/ppermute | solution.py:41
  (637 shorter events, 267.0 us)
Async XLA Ops:
  7.2 149.7 %all-gather.4.cloned.1.call-start = ((), (), s32[]{:S(2)}) async-start(), calls=%async_computation.5 | async-start | bytes 14155776 | tf_op jit(solution)/shard_map/all_gather | solution.py:186
  13.3 333.8 %all-gather.8.cloned.1.call-start = ((), (), s32[]{:S(2)}) async-start(), calls=%async_computation.7 | async-start | bytes 18874368 | tf_op jit(solution)/shard_map/all_gather | solution.py:186
  17.3 391.8 %all-gather.6.cloned.1.call-start = ((), (), s32[]{:S(2)}) async-start(), calls=%async_computation.6 | async-start | bytes 9437184 | tf_op jit(solution)/shard_map/all_gather | solution.py:186
  28.4 479.8 %reduce-scatter.5.cloned.1.call-start = ((), (), s32[]{:S(2)}) async-start(), calls=%async_computation.8 | async-start | bytes 5242880 | tf_op jit(solution)/shard_map/reduce_scatter | solution.py:217
  34.2 23.0 %collective-permute-start.4 = (bf16[1,128,512]{2,1,0:T(8,128)(2,1)S(1)}, bf16[1,128,512]{2,1,0:T(8,128)(2,1)S(1)}, u32[]{:S(2)}, u32[]{:S(2)}) collective-permute-start(bf16[1,128,512]{2,1,0:T(8,128)(2,1)S(1)} %get-tuple-element.275), channel_id=1, source_target_pairs={{0,2},{1,3},{2,0},{3,1},{4,6},{5,7},{6,4},{7,5},{8,10},{9,11},{10,... | collective-permute-start | bytes 393224 | tf_op jit(solution)/shard_map/ppermute | solution.py:41
  37.6 19.6 %collective-permute-start.5 = (bf16[1,128,512]{2,1,0:T(8,128)(2,1)S(1)}, bf16[1,128,512]{2,1,0:T(8,128)(2,1)S(1)}, u32[]{:S(2)}, u32[]{:S(2)}) collective-permute-start(bf16[1,128,512]{2,1,0:T(8,128)(2,1)S(1)} %get-tuple-element.274), channel_id=1, source_target_pairs={{0,3},{1,2},{2,1},{3,0},{4,7},{5,6},{6,5},{7,4},{8,11},{9,10},{10,... | collective-permute-start | bytes 393224 | tf_op jit(solution)/shard_map/ppermute | solution.py:41
  57.5 24.0 %collective-permute-start.13 = (bf16[1,144,256]{1,2,0:T(8,128)(2,1)S(1)}, bf16[1,144,256]{1,2,0:T(8,128)(2,1)S(1)}, u32[]{:S(2)}, u32[]{:S(2)}) collective-permute-start(bf16[1,144,256]{1,2,0:T(8,128)(2,1)S(1)} %bitcast.304), channel_id=1, source_target_pairs={{0,1},{1,0},{2,3},{3,2},{4,5},{5,4},{6,7},{7,6},{8,9},{9,8},{10,11... | collective-permute-start | bytes 221192 | tf_op jit(solution)/shard_map/ppermute | solution.py:41
  63.5 18.1 %collective-permute-start.14 = (bf16[1,144,256]{1,2,0:T(8,128)(2,1)S(1)}, bf16[1,144,256]{1,2,0:T(8,128)(2,1)S(1)}, u32[]{:S(2)}, u32[]{:S(2)}) collective-permute-start(bf16[1,144,256]{1,2,0:T(8,128)(2,1)S(1)} %bitcast.305), channel_id=1, source_target_pairs={{0,2},{1,3},{2,0},{3,1},{4,6},{5,7},{6,4},{7,5},{8,10},{9,11},{10,... | collective-permute-start | bytes 221192 | tf_op jit(solution)/shard_map/ppermute | solution.py:41
  63.5 18.1 %collective-permute-start.15 = (bf16[1,144,256]{1,2,0:T(8,128)(2,1)S(1)}, bf16[1,144,256]{1,2,0:T(8,128)(2,1)S(1)}, u32[]{:S(2)}, u32[]{:S(2)}) collective-permute-start(bf16[1,144,256]{1,2,0:T(8,128)(2,1)S(1)} %bitcast.306), channel_id=1, source_target_pairs={{0,3},{1,2},{2,1},{3,0},{4,7},{5,6},{6,5},{7,4},{8,11},{9,10},{10,... | collective-permute-start | bytes 221192 | tf_op jit(solution)/shard_map/ppermute | solution.py:41
  81.6 19.1 %collective-permute-start.16 = (bf16[4,144,256]{1,2,0:T(8,128)(2,1)S(1)}, bf16[4,144,256]{1,2,0:T(8,128)(2,1)S(1)}, u32[]{:S(2)}, u32[]{:S(2)}) collective-permute-start(bf16[4,144,256]{1,2,0:T(8,128)(2,1)S(1)} %constant_dynamic-update-slice_fusion.9), channel_id=1, source_target_pairs={{0,16},{16,0},{1,17},{17,1},{2,18},{18,2},{3,19},{19,3},{4,20},{20... | collective-permute-start | bytes 884744 | tf_op jit(solution)/shard_map/ppermute | solution.py:41
  100.2 23.9 %collective-permute-start.10 = (bf16[128,2048]{1,0:T(8,128)(2,1)S(1)}, bf16[128,2048]{1,0:T(8,128)(2,1)S(1)}, u32[]{:S(2)}, u32[]{:S(2)}) collective-permute-start(bf16[128,2048]{1,0:T(8,128)(2,1)S(1)} %fusion.36), channel_id=1, source_target_pairs={{0,8},{4,12},{8,0},{12,4},{1,9},{5,13},{9,1},{13,5},{2,10},{6,14},... | collective-permute-start | bytes 1572872 | tf_op jit(solution)/shard_map/ppermute | solution.py:41
  100.4 24.5 %collective-permute-start.9 = (bf16[128,2048]{1,0:T(8,128)(2,1)S(1)}, bf16[128,2048]{1,0:T(8,128)(2,1)}, u32[]{:S(2)}, u32[]{:S(2)}) collective-permute-start(bf16[128,2048]{1,0:T(8,128)(2,1)S(1)} %fusion.36), channel_id=1, source_target_pairs={{0,4},{4,0},{8,12},{12,8},{1,5},{5,1},{9,13},{13,9},{2,6},{6,2},{1... | collective-permute-start | bytes 1572872 | tf_op jit(solution)/shard_map/ppermute | solution.py:41
  176.5 21.1 %collective-permute-start.17 = (f32[512,160]{0,1:T(8,128)S(1)}, f32[512,160]{0,1:T(8,128)S(1)}, u32[]{:S(2)}, u32[]{:S(2)}) collective-permute-start(f32[512,160]{0,1:T(8,128)S(1)} %fusion.133), channel_id=1, source_target_pairs={{0,4},{4,0},{8,12},{12,8},{1,5},{5,1},{9,13},{13,9},{2,6},{6,2},{1... | collective-permute-start | bytes 983048 | tf_op jit(solution)/shard_map/ppermute | solution.py:41
  180.2 17.3 %collective-permute-start.24 = (bf16[1,128,512]{2,1,0:T(8,128)(2,1)S(1)}, bf16[1,128,512]{2,1,0:T(8,128)(2,1)S(1)}, u32[]{:S(2)}, u32[]{:S(2)}) collective-permute-start(bf16[1,128,512]{2,1,0:T(8,128)(2,1)S(1)} %get-tuple-element.263), channel_id=1, source_target_pairs={{0,2},{1,3},{2,0},{3,1},{4,6},{5,7},{6,4},{7,5},{8,10},{9,11},{10,... | collective-permute-start | bytes 393224 | tf_op jit(solution)/shard_map/ppermute | solution.py:41
  194.2 83.7 %collective-permute-start.25 = (bf16[1,128,512]{2,1,0:T(8,128)(2,1)S(1)}, bf16[1,128,512]{2,1,0:T(8,128)(2,1)S(1)}, u32[]{:S(2)}, u32[]{:S(2)}) collective-permute-start(bf16[1,128,512]{2,1,0:T(8,128)(2,1)S(1)} %get-tuple-element.262), channel_id=1, source_target_pairs={{0,3},{1,2},{2,1},{3,0},{4,7},{5,6},{6,5},{7,4},{8,11},{9,10},{10,... | collective-permute-start | bytes 393224 | tf_op jit(solution)/shard_map/ppermute | solution.py:41
  202.1 25.5 %collective-permute-start.29 = (f32[1,1024]{1,0:T(1,128)S(1)}, f32[1,1024]{1,0:T(1,128)S(1)}, u32[]{:S(2)}, u32[]{:S(2)}) collective-permute-start(f32[1,1024]{1,0:T(1,128)S(1)} %bitcast.362), channel_id=1, source_target_pairs={{0,2},{1,3},{4,6},{5,7},{8,10},{9,11},{12,14},{13,15},{16,18},{17,... | collective-permute-start | bytes 12296 | tf_op jit(solution)/shard_map/ppermute | solution.py:49
  275.3 26.8 %collective-permute-start.34 = (bf16[128,2048]{1,0:T(8,128)(2,1)S(1)}, bf16[128,2048]{1,0:T(8,128)(2,1)S(1)}, u32[]{:S(2)}, u32[]{:S(2)}) collective-permute-start(bf16[128,2048]{1,0:T(8,128)(2,1)S(1)} %get-tuple-element.235), channel_id=1, source_target_pairs={{0,8},{4,12},{8,0},{12,4},{1,9},{5,13},{9,1},{13,5},{2,10},{6,14},... | collective-permute-start | bytes 1572872 | tf_op jit(solution)/shard_map/ppermute | solution.py:41
  277.6 24.5 %collective-permute-start.33 = (bf16[128,2048]{1,0:T(8,128)(2,1)S(1)}, bf16[128,2048]{1,0:T(8,128)(2,1)S(1)}, u32[]{:S(2)}, u32[]{:S(2)}) collective-permute-start(bf16[128,2048]{1,0:T(8,128)(2,1)S(1)} %get-tuple-element.233), channel_id=1, source_target_pairs={{0,4},{4,0},{8,12},{12,8},{1,5},{5,1},{9,13},{13,9},{2,6},{6,2},{1... | collective-permute-start | bytes 1572872 | tf_op jit(solution)/shard_map/ppermute | solution.py:41
  278.0 33.9 %collective-permute-start.38 = (bf16[128,2048]{1,0:T(8,128)(2,1)S(1)}, bf16[128,2048]{1,0:T(8,128)(2,1)S(1)}, u32[]{:S(2)}, u32[]{:S(2)}) collective-permute-start(bf16[128,2048]{1,0:T(8,128)(2,1)S(1)} %pad_maximum_fusion.24), channel_id=1, source_target_pairs={{0,12},{4,8},{8,4},{12,0},{1,13},{5,9},{9,5},{13,1},{2,14},{6,10},... | collective-permute-start | bytes 1572872 | tf_op jit(solution)/shard_map/ppermute | solution.py:41
  279.0 45.4 %collective-permute-start.37 = (bf16[128,2048]{1,0:T(8,128)(2,1)S(1)}, bf16[128,2048]{1,0:T(8,128)(2,1)S(1)}, u32[]{:S(2)}, u32[]{:S(2)}) collective-permute-start(bf16[128,2048]{1,0:T(8,128)(2,1)S(1)} %pad_maximum_fusion.24), channel_id=1, source_target_pairs={{0,8},{4,12},{8,0},{12,4},{1,9},{5,13},{9,1},{13,5},{2,10},{6,14},... | collective-permute-start | bytes 1572872 | tf_op jit(solution)/shard_map/ppermute | solution.py:41
  289.4 35.0 %collective-permute-start.36 = (bf16[128,2048]{1,0:T(8,128)(2,1)S(1)}, bf16[128,2048]{1,0:T(8,128)(2,1)S(1)}, u32[]{:S(2)}, u32[]{:S(2)}) collective-permute-start(bf16[128,2048]{1,0:T(8,128)(2,1)S(1)} %pad_maximum_fusion.24), channel_id=1, source_target_pairs={{0,4},{4,0},{8,12},{12,8},{1,5},{5,1},{9,13},{13,9},{2,6},{6,2},{1... | collective-permute-start | bytes 1572872 | tf_op jit(solution)/shard_map/ppermute | solution.py:41
  302.8 31.5 %collective-permute-start.41 = (bf16[128,2048]{1,0:T(8,128)(2,1)S(1)}, bf16[128,2048]{1,0:T(8,128)(2,1)S(1)}, u32[]{:S(2)}, u32[]{:S(2)}) collective-permute-start(bf16[128,2048]{1,0:T(8,128)(2,1)S(1)} %multiply_convert_fusion.7), channel_id=1, source_target_pairs={{0,12},{4,8},{8,4},{12,0},{1,13},{5,9},{9,5},{13,1},{2,14},{6,10},... | collective-permute-start | bytes 1572872 | tf_op jit(solution)/shard_map/ppermute | solution.py:41
  305.0 41.3 %collective-permute-start.40 = (bf16[128,2048]{1,0:T(8,128)(2,1)S(1)}, bf16[128,2048]{1,0:T(8,128)(2,1)S(1)}, u32[]{:S(2)}, u32[]{:S(2)}) collective-permute-start(bf16[128,2048]{1,0:T(8,128)(2,1)S(1)} %multiply_convert_fusion.7), channel_id=1, source_target_pairs={{0,8},{4,12},{8,0},{12,4},{1,9},{5,13},{9,1},{13,5},{2,10},{6,14},... | collective-permute-start | bytes 1572872 | tf_op jit(solution)/shard_map/ppermute | solution.py:41
  311.9 35.2 %collective-permute-start.39 = (bf16[128,2048]{1,0:T(8,128)(2,1)S(1)}, bf16[128,2048]{1,0:T(8,128)(2,1)}, u32[]{:S(2)}, u32[]{:S(2)}) collective-permute-start(bf16[128,2048]{1,0:T(8,128)(2,1)S(1)} %multiply_convert_fusion.7), channel_id=1, source_target_pairs={{0,4},{4,0},{8,12},{12,8},{1,5},{5,1},{9,13},{13,9},{2,6},{6,2},{1... | collective-permute-start | bytes 1572872 | tf_op jit(solution)/shard_map/ppermute | solution.py:41
  433.2 17.7 %collective-permute-start.43 = (bf16[1024,4096]{1,0:T(8,128)(2,1)}, bf16[1024,4096]{1,0:T(8,128)(2,1)}, u32[]{:S(2)}, u32[]{:S(2)}) collective-permute-start(bf16[1024,4096]{1,0:T(8,128)(2,1)} %convolution_convert_fusion), channel_id=1, source_target_pairs={{0,16},{16,0},{1,17},{17,1},{2,18},{18,2},{3,19},{19,3},{4,20},{20... | collective-permute-start | bytes 25165832 | tf_op jit(solution)/shard_map/ppermute | solution.py:41
  433.4 223.9 %reduce-scatter.7.cloned.1.call-start = ((), (), s32[]{:S(2)}) async-start(), calls=%async_computation.9 | async-start | bytes 10485760 | tf_op jit(solution)/shard_map/reduce_scatter | solution.py:217
  461.1 277.5 %reduce-scatter.9.cloned.1.call-start = ((), (), s32[]{:S(2)}) async-start(), calls=%async_computation.10 | async-start | bytes 5242880 | tf_op jit(solution)/shard_map/reduce_scatter | solution.py:217
  466.2 24.0 %collective-permute-start.45 = (bf16[128,2048]{1,0:T(8,128)(2,1)S(1)}, bf16[128,2048]{1,0:T(8,128)(2,1)S(1)}, u32[]{:S(2)}, u32[]{:S(2)}) collective-permute-start(bf16[128,2048]{1,0:T(8,128)(2,1)S(1)} %get-tuple-element.216), channel_id=1, source_target_pairs={{0,8},{4,12},{8,0},{12,4},{1,9},{5,13},{9,1},{13,5},{2,10},{6,14},... | collective-permute-start | bytes 1572872 | tf_op jit(solution)/shard_map/ppermute | solution.py:41
  466.5 23.7 %collective-permute-start.44 = (bf16[128,2048]{1,0:T(8,128)(2,1)S(1)}, bf16[128,2048]{1,0:T(8,128)(2,1)S(1)}, u32[]{:S(2)}, u32[]{:S(2)}) collective-permute-start(bf16[128,2048]{1,0:T(8,128)(2,1)S(1)} %get-tuple-element.214), channel_id=1, source_target_pairs={{0,4},{4,0},{8,12},{12,8},{1,5},{5,1},{9,13},{13,9},{2,6},{6,2},{1... | collective-permute-start | bytes 1572872 | tf_op jit(solution)/shard_map/ppermute | solution.py:41
  511.1 23.9 %collective-permute-start.48 = (bf16[128,2048]{1,0:T(8,128)(2,1)S(1)}, bf16[128,2048]{1,0:T(8,128)(2,1)S(1)}, u32[]{:S(2)}, u32[]{:S(2)}) collective-permute-start(bf16[128,2048]{1,0:T(8,128)(2,1)S(1)} %get-tuple-element.80), channel_id=1, source_target_pairs={{0,8},{4,12},{8,0},{12,4},{1,9},{5,13},{9,1},{13,5},{2,10},{6,14},... | collective-permute-start | bytes 1572872 | tf_op jit(solution)/shard_map/ppermute | solution.py:41
  512.6 22.5 %collective-permute-start.49 = (bf16[128,2048]{1,0:T(8,128)(2,1)S(1)}, bf16[128,2048]{1,0:T(8,128)(2,1)S(1)}, u32[]{:S(2)}, u32[]{:S(2)}) collective-permute-start(bf16[128,2048]{1,0:T(8,128)(2,1)S(1)} %get-tuple-element.80), channel_id=1, source_target_pairs={{0,12},{4,8},{8,4},{12,0},{1,13},{5,9},{9,5},{13,1},{2,14},{6,10},... | collective-permute-start | bytes 1572872 | tf_op jit(solution)/shard_map/ppermute | solution.py:41
  548.0 78.1 %collective-permute-start.53 = (bf16[1024,2048]{1,0:T(8,128)(2,1)S(1)}, bf16[1024,2048]{1,0:T(8,128)(2,1)}, u32[]{:S(2)}, u32[]{:S(2)}) collective-permute-start(bf16[1024,2048]{1,0:T(8,128)(2,1)S(1)} %pad_maximum_fusion.1), channel_id=1, source_target_pairs={{0,16},{16,0},{1,17},{17,1},{2,18},{18,2},{3,19},{19,3},{4,20},{20... | collective-permute-start | bytes 12582920 | tf_op jit(solution)/shard_map/ppermute | solution.py:41
  559.8 21.6 %collective-permute-start.52 = (bf16[16,1024]{1,0:T(8,128)(2,1)S(1)}, bf16[16,1024]{1,0:T(8,128)(2,1)S(1)}, u32[]{:S(2)}, u32[]{:S(2)}) collective-permute-start(bf16[16,1024]{1,0:T(8,128)(2,1)S(1)} %convert_element_type.276), channel_id=1, source_target_pairs={{3,0},{7,4},{11,8},{15,12},{19,16},{23,20},{27,24},{31,28}} | collective-permute-start | bytes 98312 | tf_op jit(solution)/shard_map/ppermute | solution.py:49
  561.1 20.6 %collective-permute-start.51 = (bf16[16,1024]{1,0:T(8,128)(2,1)S(1)}, bf16[16,1024]{1,0:T(8,128)(2,1)S(1)}, u32[]{:S(2)}, u32[]{:S(2)}) collective-permute-start(bf16[16,1024]{1,0:T(8,128)(2,1)S(1)} %convert_element_type.276), channel_id=1, source_target_pairs={{2,0},{3,1},{6,4},{7,5},{10,8},{11,9},{14,12},{15,13},{18,16},{19,... | collective-permute-start | bytes 98312 | tf_op jit(solution)/shard_map/ppermute | solution.py:49
  562.4 23.8 %collective-permute-start.50 = (bf16[16,1024]{1,0:T(8,128)(2,1)S(1)}, bf16[16,1024]{1,0:T(8,128)(2,1)S(1)}, u32[]{:S(2)}, u32[]{:S(2)}) collective-permute-start(bf16[16,1024]{1,0:T(8,128)(2,1)S(1)} %convert_element_type.276), channel_id=1, source_target_pairs={{1,0},{2,1},{3,2},{5,4},{6,5},{7,6},{9,8},{10,9},{11,10},{13,12},{... | collective-permute-start | bytes 98312 | tf_op jit(solution)/shard_map/ppermute | solution.py:49
  580.2 42.8 %collective-permute-start.56 = (bf16[128,2048]{1,0:T(8,128)(2,1)}, bf16[128,2048]{1,0:T(8,128)(2,1)}, u32[]{:S(2)}, u32[]{:S(2)}) collective-permute-start(bf16[128,2048]{1,0:T(8,128)(2,1)} %get-tuple-element.196), channel_id=1, source_target_pairs={{0,12},{4,8},{8,4},{12,0},{1,13},{5,9},{9,5},{13,1},{2,14},{6,10},... | collective-permute-start | bytes 1572872 | tf_op jit(solution)/shard_map/ppermute | solution.py:41
  581.5 41.6 %collective-permute-start.55 = (bf16[128,2048]{1,0:T(8,128)(2,1)}, bf16[128,2048]{1,0:T(8,128)(2,1)}, u32[]{:S(2)}, u32[]{:S(2)}) collective-permute-start(bf16[128,2048]{1,0:T(8,128)(2,1)} %get-tuple-element.197), channel_id=1, source_target_pairs={{0,8},{4,12},{8,0},{12,4},{1,9},{5,13},{9,1},{13,5},{2,10},{6,14},... | collective-permute-start | bytes 1572872 | tf_op jit(solution)/shard_map/ppermute | solution.py:41
  581.7 41.3 %collective-permute-start.54 = (bf16[128,2048]{1,0:T(8,128)(2,1)S(1)}, bf16[128,2048]{1,0:T(8,128)(2,1)}, u32[]{:S(2)}, u32[]{:S(2)}) collective-permute-start(bf16[128,2048]{1,0:T(8,128)(2,1)S(1)} %get-tuple-element.195), channel_id=1, source_target_pairs={{0,4},{4,0},{8,12},{12,8},{1,5},{5,1},{9,13},{13,9},{2,6},{6,2},{1... | collective-permute-start | bytes 1572872 | tf_op jit(solution)/shard_map/ppermute | solution.py:41
  688.9 24.0 %collective-permute-start.63 = (bf16[128,2048]{1,0:T(8,128)(2,1)S(1)}, bf16[128,2048]{1,0:T(8,128)(2,1)S(1)}, u32[]{:S(2)}, u32[]{:S(2)}) collective-permute-start(bf16[128,2048]{1,0:T(8,128)(2,1)S(1)} %get-tuple-element.194), channel_id=1, source_target_pairs={{0,8},{4,12},{8,0},{12,4},{1,9},{5,13},{9,1},{13,5},{2,10},{6,14},... | collective-permute-start | bytes 1572872 | tf_op jit(solution)/shard_map/ppermute | solution.py:41
  689.2 23.7 %collective-permute-start.62 = (bf16[128,2048]{1,0:T(8,128)(2,1)S(1)}, bf16[128,2048]{1,0:T(8,128)(2,1)S(1)}, u32[]{:S(2)}, u32[]{:S(2)}) collective-permute-start(bf16[128,2048]{1,0:T(8,128)(2,1)S(1)} %get-tuple-element.192), channel_id=1, source_target_pairs={{0,4},{4,0},{8,12},{12,8},{1,5},{5,1},{9,13},{13,9},{2,6},{6,2},{1... | collective-permute-start | bytes 1572872 | tf_op jit(solution)/shard_map/ppermute | solution.py:41
  689.5 28.0 %collective-permute-start.65 = (bf16[256,4096]{1,0:T(8,128)(2,1)S(1)}, bf16[256,4096]{1,0:T(8,128)(2,1)S(1)}, u32[]{:S(2)}, u32[]{:S(2)}) collective-permute-start(bf16[256,4096]{1,0:T(8,128)(2,1)S(1)} %copy-done.19), channel_id=1, source_target_pairs={{0,16},{16,0},{1,17},{17,1},{2,18},{18,2},{3,19},{19,3},{4,20},{20... | collective-permute-start | bytes 6291464 | tf_op jit(solution)/shard_map/ppermute | solution.py:41
  690.6 24.2 %collective-permute-start.66 = (bf16[256,2048]{1,0:T(8,128)(2,1)S(1)}, bf16[256,2048]{1,0:T(8,128)(2,1)S(1)}, u32[]{:S(2)}, u32[]{:S(2)}) collective-permute-start(bf16[256,2048]{1,0:T(8,128)(2,1)S(1)} %copy-done.26), channel_id=1, source_target_pairs={{0,16},{16,0},{1,17},{17,1},{2,18},{18,2},{3,19},{19,3},{4,20},{20... | collective-permute-start | bytes 3145736 | tf_op jit(solution)/shard_map/ppermute | solution.py:41
  701.2 20.3 %collective-permute-start.61 = (bf16[1024,1024]{1,0:T(8,128)(2,1)S(1)}, bf16[1024,1024]{1,0:T(8,128)(2,1)S(1)}, u32[]{:S(2)}, u32[]{:S(2)}) collective-permute-start(bf16[1024,1024]{1,0:T(8,128)(2,1)S(1)} %convolution_convert_fusion.2), channel_id=1, source_target_pairs={{0,16},{16,0},{1,17},{17,1},{2,18},{18,2},{3,19},{19,3},{4,20},{20... | collective-permute-start | bytes 6291464 | tf_op jit(solution)/shard_map/ppermute | solution.py:41
  742.1 30.2 %all-to-all-start = ((bf16[4,256,512]{2,1,0:T(8,128)(2,1)}), bf16[4,256,512]{2,1,0:T(8,128)(2,1)}, u32[]{:S(2)}, u32[]{:S(2)}) async-start(bf16[4,256,512]{2,1,0:T(8,128)(2,1)} %pad_maximum_fusion.22), calls=%async_computation.3 | async-start | bytes 2097152 | tf_op jit(solution)/shard_map/all_to_all | solution.py:167
  746.4 75.1 %reduce-scatter.11.cloned.1.call-start = ((), (), s32[]{:S(2)}) async-start(), calls=%async_computation.11 | async-start | bytes 2621440 | tf_op jit(solution)/shard_map/reduce_scatter | solution.py:217
  752.1 25.6 %collective-permute-start.77 = (bf16[256,2048]{1,0:T(8,128)(2,1)}, bf16[256,2048]{1,0:T(8,128)(2,1)S(1)}, u32[]{:S(2)}, u32[]{:S(2)}) collective-permute-start(bf16[256,2048]{1,0:T(8,128)(2,1)} %reduce-scatter.9.cloned.1.call-done), channel_id=1, source_target_pairs={{0,16},{16,0},{1,17},{17,1},{2,18},{18,2},{3,19},{19,3},{4,20},{20... | collective-permute-start | bytes 3145736 | tf_op jit(solution)/shard_map/ppermute | solution.py:41
  795.5 17.2 %collective-permute-start.73 = (bf16[171,256]{1,0:T(8,128)(2,1)S(1)}, bf16[171,256]{1,0:T(8,128)(2,1)S(1)}, u32[]{:S(2)}, u32[]{:S(2)}) collective-permute-start(bf16[171,256]{1,0:T(8,128)(2,1)S(1)} %get-tuple-element.248), channel_id=1, source_target_pairs={{0,2},{1,3},{2,0},{3,1},{4,6},{5,7},{6,4},{7,5},{8,10},{9,11},{10,... | collective-permute-start | bytes 262664 | tf_op jit(solution)/shard_map/ppermute | solution.py:41
  795.6 17.1 %collective-permute-start.72 = (bf16[171,256]{1,0:T(8,128)(2,1)S(1)}, bf16[171,256]{1,0:T(8,128)(2,1)S(1)}, u32[]{:S(2)}, u32[]{:S(2)}) collective-permute-start(bf16[171,256]{1,0:T(8,128)(2,1)S(1)} %get-tuple-element.247), channel_id=1, source_target_pairs={{0,1},{1,0},{2,3},{3,2},{4,5},{5,4},{6,7},{7,6},{8,9},{9,8},{10,11... | collective-permute-start | bytes 262664 | tf_op jit(solution)/shard_map/ppermute | solution.py:41
  (187 other events, 2589.2 us)
Sparse Core Ops, SparseCore 0:
  13.4 143.4 all-gather.3
  159.1 163.9 all-gather.7
  325.2 83.7 all-gather.5
  433.6 74.5 reduce-scatter.4
  510.5 146.8 reduce-scatter.6
  660.2 78.3 reduce-scatter.8
  772.5 48.5 reduce-scatter.10

commit v5 on v4

--- a/solution.py
+++ b/solution.py
@@ -146,7 +146,7 @@
     if rows == cols:
         count, features = values.shape
         pieces = values.reshape(rows, count // rows, features)
-        pieces = exchange(exchange(pieces, "row"), "col")
+        pieces = lax.all_to_all(exchange(pieces, "row"), "col", split_axis=0, concat_axis=0)
         return jnp.concatenate([pieces[c] for c in range(cols)], axis=1)
     split = lax.all_to_all(values, "col", split_axis=0, concat_axis=1, tiled=True)
     return lax.ppermute(split, ("row", "col"), block_moves())

time: 844 us -> 844 us (level)
  waiting for transfers between devices: 368 us -> 348 us
    ppermute x68 -> x62, waiting for transfers between devices: 235 us -> 195 us  [swap(): lax.ppermute(values, axis, [(i, i ^ distance) for i in range(lax.axis_siz...]
    all_to_all x0 -> x2, waiting for transfers between devices: none -> 27.4 us  [to_whole_features(): lax.all_to_all(exchange(pieces, 'row'), 'col', split_axis=0, concat_axis=0)]
    ppermute x68 -> x62, starting transfers between devices: 92.9 us -> 90.5 us  [swap(): lax.ppermute(values, axis, [(i, i ^ distance) for i in range(lax.axis_siz...]
    unnamed x305 -> x315, local copies, waits for them, and re-layouts: 24.6 us -> 25.3 us
  transfers between devices with their start and end apart: 88 -> 84, of which waited for: 41 -> 40; matrix products, arithmetic and copies ran while one was open for 25% -> 26% of each run, Pallas kernels for 9% -> 9%
where the time goes in v5:
time: 844 us; the launch traced here: 836 us
  waiting for transfers between devices  348 us (41%)
  matrix products  134 us (16%)
  starting transfers between devices  131 us (16%)
  other arithmetic  74.8 us (9%)
  Pallas kernels  74.3 us (9%)
  local copies, waits for them, and re-layouts  56.7 us (7%)
  between operations  17.3 us (2%)
    ppermute x62, waiting for transfers between devices, swap(): lax.ppermute(values, axis, [(i, i ^ distance) for i in range(lax.axis_siz...  195 us
    dot_general x24, matrix products, product(): lax.dot_general(multiplicand, multiplier, dims, preferred_element_type=jn...  134 us
    ppermute x62, starting transfers between devices, swap(): lax.ppermute(values, axis, [(i, i ^ distance) for i in range(lax.axis_siz...  90.5 us
    pallas_call x4, Pallas kernels, call(): return lambda *operands: call(self.order.reshape(1), *operands)  74.3 us
    all_gather x3, waiting for transfers between devices, gather_weight(): return lax.all_gather(low(part), ('col', 'dp'), axis=0, tiled=True)  62.3 us
    reduce_scatter x4, waiting for transfers between devices, scatter_gradient(): return lax.psum_scatter(gradient, 'col', scatter_dimension=0, tiled=True)  31.7 us
    all_to_all x2, waiting for transfers between devices, to_whole_features(): lax.all_to_all(exchange(pieces, 'row'), 'col', split_axis=0, concat_axis=0)  27.4 us
    ppermute x12, starting transfers between devices, shift(): return lax.ppermute(values, axis, pairs)  27.1 us
  transfers between devices with their start and end apart: 84, of which 40 were waited for; matrix products, arithmetic and copies ran while one was open for 26% of the time, Pallas kernels for 9%

profile of v5, /device:TPU:1, one launch (start us, length us, event | category | flops | bytes accessed | tf_op | source)
XLA Modules:
  0.0 836.4 jit_solution(12579082026361754493)
XLA Ops:
  35.5 4.5 all-to-all-start
  40.2 22.4 %all-to-all-done = bf16[4,128,512]{2,1,0:T(8,128)(2,1)S(1)} async-done(((bf16[4,128,512]{2,1,0:T(8,128)(2,1)}), bf16[4,128,512]{2,1,0:T(8,128)(2,1)S(1)}, u32[]{:S(2)}, u32[]{:S(2)}) %all-to-all-start) | async-done | bytes 524320 | tf_op jit(solution)/shard_map/all_to_all | solution.py:149
  66.7 15.0 %collective-permute-done.10 = bf16[1,144,256]{1,2,0:T(8,128)(2,1)S(1)} collective-permute-done((bf16[1,144,256]{1,2,0:T(8,128)(2,1)S(1)}, bf16[1,144,256]{1,2,0:T(8,128)(2,1)S(1)}, u32[]{:S(2)}, u32[]{:S(2)}) %collective-permute-start.10) | collective-permute-done | bytes 73760 | tf_op jit(solution)/shard_map/ppermute | solution.py:41
  81.8 15.8 %collective-permute-start.13 = (bf16[4,144,256]{1,2,0:T(8,128)(2,1)S(1)}, bf16[4,144,256]{1,2,0:T(8,128)(2,1)S(1)}, u32[]{:S(2)}, u32[]{:S(2)}) collective-permute-start(bf16[4,144,256]{1,2,0:T(8,128)(2,1)S(1)} %constant_dynamic-update-slice_fusion.6), channel_id=1, source_target_pairs={{0,16},{16,0},{1,17},{17,1},{2,18},{18,2},{3,19},{19,3},{4,20},{20... | collective-permute-start | bytes 884744 | tf_op jit(solution)/shard_map/ppermute | solution.py:41
  101.1 11.4 %collective-permute-done.8 = bf16[128,2048]{1,0:T(8,128)(2,1)S(1)} collective-permute-done((bf16[128,2048]{1,0:T(8,128)(2,1)S(1)}, bf16[128,2048]{1,0:T(8,128)(2,1)S(1)}, u32[]{:S(2)}, u32[]{:S(2)}) %collective-permute-start.8) | collective-permute-done | bytes 524320 | tf_op jit(solution)/shard_map/ppermute | solution.py:41
  112.5 10.4 %collective-permute-done.7 = bf16[128,2048]{1,0:T(8,128)(2,1)S(1)} collective-permute-done((bf16[128,2048]{1,0:T(8,128)(2,1)S(1)}, bf16[128,2048]{1,0:T(8,128)(2,1)S(1)}, u32[]{:S(2)}, u32[]{:S(2)}) %collective-permute-start.7) | collective-permute-done | bytes 524320 | tf_op jit(solution)/shard_map/ppermute | solution.py:41
  123.7 33.4 %all-gather.4.cloned.1.call-done = bf16[2048,3072]{0,1:T(8,128)(2,1)} async-done(((bf16[256,3072]{0,1:T(8,128)(2,1)}), bf16[2048,3072]{0,1:T(8,128)(2,1)}) %all-gather.4.cloned.1.call-update) | async-done | bytes 12582928 | tf_op jit(solution)/shard_map/all_gather | solution.py:186
  157.1 8.4 %fusion.3 = f32[512,2048]{1,0:T(8,128)S(1)} fusion(bf16[2048,3072]{0,1:T(8,128)(2,1)} %all-gather.4.cloned.1.call-done, bf16[128,2048]{1,0:T(8,128)(2,1)} %copy-done.40, bf16[128,2048]{1,0:T(8,128)(2,1)} %copy-done.41, bf16[128,2048]{1,0:T(8,128)(2,1)} %collective-permute-done.6, bf16[128,2048]{1,0:T(8,128)(2,1)S(1)} %fusion.36), kind=kOutput, calls=%fused_computation.9 | convolution fusion | flops 4303355904 | bytes 14680064 | tf_op jit(solution)/shard_map/dot_general | solution.py:33
  189.3 6.5 collective-permute-done.16
  198.6 9.8 %collective-permute-start.23 = (f32[1,1024]{1,0:T(1,128)S(1)}, f32[1,1024]{1,0:T(1,128)S(1)}, u32[]{:S(2)}, u32[]{:S(2)}) collective-permute-start(f32[1,1024]{1,0:T(1,128)S(1)} %bitcast.362), channel_id=1, source_target_pairs={{0,2},{1,3},{4,6},{5,7},{8,10},{9,11},{12,14},{13,15},{16,18},{17,... | collective-permute-start | bytes 12296 | tf_op jit(solution)/shard_map/ppermute | solution.py:49
  213.2 9.4 %chunk_state.1 = f32[16,1024]{1,0:T(8,128)} custom-call(s32[1]{0:T(128)} %bitcast.50._, f32[512,1024]{1,0:T(8,128)} %copy-done, f32[512,1024]{1,0:T(8,128)} %copy-done, f32[512,1024]{1,0:T(8,128)} %copy-done, f32[512,1024]{1,0:T(8,128)} %copy-done, f32[512,1024]{1,0:T(8,128)} %copy-done, f32[512,1024]{1,0:T(8,128)} %copy-done, f32[512,1024]{1,0:T(8,128)} %copy-done, ...), custom_call_target="tpu_custom_call" | custom-call | tf_op jit(solution)/shard_map/chunk_state/pallas_call | solution.py:318
  240.4 19.6 %scan_forward.1 = (f32[512,1024]{1,0:T(8,128)}, f32[512,16,1024]{2,1,0:T(8,128)}, f32[16,1024]{1,0:T(8,128)}) custom-call(s32[1]{0:T(128)} %bitcast.50._, f32[512,1024]{1,0:T(8,128)} %copy-done, f32[512,1024]{1,0:T(8,128)} %copy-done, f32[512,1024]{1,0:T(8,128)} %copy-done, f32[512,1024]{1,0:T(8,128)} %copy-done, f32[512,1024]{1,0:T(8,128)} %copy-done, ...), custom_call_target="tpu_custom_call" | custom-call | tf_op jit(solution)/shard_map/scan_forward/pallas_call | solution.py:318
  262.3 6.9 fusion.131
  279.9 11.6 %collective-permute-done.28 = bf16[128,2048]{1,0:T(8,128)(2,1)S(1)} collective-permute-done((bf16[128,2048]{1,0:T(8,128)(2,1)}, bf16[128,2048]{1,0:T(8,128)(2,1)S(1)}, u32[]{:S(2)}, u32[]{:S(2)}) %collective-permute-start.28) | collective-permute-done | bytes 524320 | tf_op jit(solution)/shard_map/ppermute | solution.py:41
  295.0 5.1 all-to-all-done.1
  322.9 14.4 %collective-permute-done.34 = bf16[128,2048]{1,0:T(8,128)(2,1)S(1)} collective-permute-done((bf16[128,2048]{1,0:T(8,128)(2,1)S(1)}, bf16[128,2048]{1,0:T(8,128)(2,1)S(1)}, u32[]{:S(2)}, u32[]{:S(2)}) %collective-permute-start.34) | collective-permute-done | bytes 524320 | tf_op jit(solution)/shard_map/ppermute | solution.py:41
  338.2 12.2 %fusion.109 = f32[512,4096]{1,0:T(8,128)S(1)} fusion(bf16[2048,4096]{1,0:T(8,128)(2,1)} %all-gather.8.cloned.1.call-done, bf16[128,2048]{1,0:T(8,128)(2,1)} %copy-done.46, bf16[128,2048]{1,0:T(8,128)(2,1)} %copy-done.48, bf16[128,2048]{1,0:T(8,128)(2,1)} %collective-permute-done.33, bf16[128,2048]{1,0:T(8,128)(2,1)S(1)} %multiply_convert_fusion.7), kind=kOutput, calls=%fused_computation.332 | convolution fusion | flops 8598323200 | bytes 27262976 | tf_op jit(solution)/shard_map/dot_general | solution.py:33
  356.3 11.9 %collective-permute-start.36 = (bf16[1024,2048]{1,0:T(8,128)(2,1)S(1)}, bf16[1024,2048]{1,0:T(8,128)(2,1)S(1)}, u32[]{:S(2)}, u32[]{:S(2)}) collective-permute-start(bf16[1024,2048]{1,0:T(8,128)(2,1)S(1)} %convolution_convert_fusion.1), channel_id=1, source_target_pairs={{0,16},{16,0},{1,17},{17,1},{2,18},{18,2},{3,19},{19,3},{4,20},{20... | collective-permute-start | bytes 12582920 | tf_op jit(solution)/shard_map/ppermute | solution.py:41
  375.1 4.8 add_convert_fusion.1
  379.9 28.9 %all-gather.6.cloned.1.call-done = bf16[2048,2048]{0,1:T(8,128)(2,1)} async-done(((bf16[256,2048]{0,1:T(8,128)(2,1)}), bf16[2048,2048]{0,1:T(8,128)(2,1)}) %all-gather.6.cloned.1.call-update) | async-done | bytes 8388624 | tf_op jit(solution)/shard_map/all_gather | solution.py:186
  408.8 14.1 %multiply_convert_fusion.1 = (bf16[512,2048]{1,0:T(8,128)(2,1)S(1)}, bf16[512,2048]{1,0:T(8,128)(2,1)S(1)}) fusion(f32[512,4096]{1,0:T(8,128)} %copy-done.12, bf16[2048,2048]{0,1:T(8,128)(2,1)} %all-gather.6.cloned.1.call-done, bf16[128,2048]{1,0:T(8,128)(2,1)S(1)} %copy-done.43, bf16[128,2048]{1,0:T(8,128)(2,1)} %copy-done.44, ...), kind=kOutput, calls=%fused_computation.24 | convolution fusion | flops 4323278848 | bytes 23068672 | tf_op jit(solution)/shard_map/dot_general | solution.py:33
  425.3 7.7 convolution_convert_fusion
  433.4 17.7 %fusion.134 = f32[512,2048]{1,0:T(8,128)} fusion(bf16[512,4096]{1,0:T(8,128)(2,1)} %pad_maximum_fusion, bf16[2048,4096]{1,0:T(8,128)(2,1)} %all-gather.8.cloned.1.call-done), kind=kOutput, calls=%fused_computation.356 | convolution fusion | flops 8589934592 | bytes 25165824 | tf_op jit(solution)/shard_map/dot_general | solution.py:33
  451.1 10.1 %add_convert_fusion = bf16[1024,4096]{1,0:T(8,128)(2,1)} fusion(bf16[1024,4096]{1,0:T(8,128)(2,1)} %collective-permute-done.37, bf16[512,4096]{1,0:T(8,128)(2,1)S(1)} %copy-done.15, pred[]{:T(512)S(6)} %eq.36, bf16[512,256]{1,0:T(8,128)(2,1)S(1)} %copy-done.100, bf16[512,256]{1,0:T(8,128)(2,1)S(1)} %copy-done.89, bf16[512,256]{1,0:T(8,128)(2,1)S(1)} %copy-done.90, ...), kind=kOutput, calls=%fused_computation | convolution fusion | flops 4316463104 | bytes 23068672 | tf_op jit(solution)/shard_map/dot_general | solution.py:33
  466.8 11.6 %collective-permute-done.40 = bf16[128,2048]{1,0:T(8,128)(2,1)S(1)} collective-permute-done((bf16[128,2048]{1,0:T(8,128)(2,1)S(1)}, bf16[128,2048]{1,0:T(8,128)(2,1)S(1)}, u32[]{:S(2)}, u32[]{:S(2)}) %collective-permute-start.40) | collective-permute-done | bytes 524320 | tf_op jit(solution)/shard_map/ppermute | solution.py:41
  478.4 11.8 %collective-permute-done.39 = bf16[128,2048]{1,0:T(8,128)(2,1)S(1)} collective-permute-done((bf16[128,2048]{1,0:T(8,128)(2,1)S(1)}, bf16[128,2048]{1,0:T(8,128)(2,1)S(1)}, u32[]{:S(2)}, u32[]{:S(2)}) %collective-permute-start.39) | collective-permute-done | bytes 524320 | tf_op jit(solution)/shard_map/ppermute | solution.py:41
  494.0 14.0 %reduce-scatter.5.cloned.1.call-done = bf16[256,2048]{1,0:T(8,128)(2,1)} async-done(((bf16[1024,2048]{1,0:T(8,128)(2,1)}), bf16[256,2048]{1,0:T(8,128)(2,1)}) %reduce-scatter.5.cloned.1.call-update) | async-done | bytes 1048592 | tf_op jit(solution)/shard_map/reduce_scatter | solution.py:217
  512.8 8.2 collective-permute-done.41
  521.0 13.8 %collective-permute-done.42 = bf16[128,2048]{1,0:T(8,128)(2,1)S(1)} collective-permute-done((bf16[128,2048]{1,0:T(8,128)(2,1)S(1)}, bf16[128,2048]{1,0:T(8,128)(2,1)S(1)}, u32[]{:S(2)}, u32[]{:S(2)}) %collective-permute-start.42) | collective-permute-done | bytes 524320 | tf_op jit(solution)/shard_map/ppermute | solution.py:41
  539.4 6.7 multiply_convert_fusion.3
  549.6 9.2 %chunk_state_back.1 = f32[16,1024]{1,0:T(8,128)} custom-call(s32[1]{0:T(128)} %bitcast.50._, f32[512,1024]{1,0:T(8,128)} %copy-done, f32[512,1024]{1,0:T(8,128)} %copy-done, f32[512,1024]{1,0:T(8,128)} %copy-done, f32[512,1024]{1,0:T(8,128)} %copy-done, f32[512,1024]{1,0:T(8,128)} %copy-done, f32[512,1024]{1,0:T(8,128)} %copy-done, f32[512,1024]{1,0:T(8,128)} %copy-done, ...), custom_call_target="tpu_custom_call" | custom-call | tf_op jit(solution)/shard_map/chunk_state_back/pallas_call | solution.py:318
  563.8 10.5 %fusion.132 = (bf16[512,2048]{1,0:T(8,128)(2,1)S(1)}, f32[512,2048]{1,0:T(8,128)}) fusion(bf16[512,2048]{1,0:T(8,128)(2,1)} %copy-done.17, bf16[2048,2048]{0,1:T(8,128)(2,1)} %all-gather.6.cloned.1.call-done), kind=kOutput, calls=%fused_computation.354 | convolution fusion | flops 4296015872 | bytes 16777216 | tf_op jit(solution)/shard_map/dot_general | solution.py:33
  586.5 36.2 %scan_backward.1 = (f32[512,1024]{1,0:T(8,128)}, f32[512,1024]{1,0:T(8,128)}, f32[16,1024]{1,0:T(8,128)}, f32[1,512,128]{2,1,0:T(8,128)}) custom-call(s32[1]{0:T(128)} %bitcast.50._, f32[512,1024]{1,0:T(8,128)} %copy-done, f32[512,1024]{1,0:T(8,128)} %copy-done, f32[512,1024]{1,0:T(8,128)} %copy-done, f32[512,1024]{1,0:T(8,128)} %copy-done, ...), custom_call_target="tpu_custom_call" | custom-call | tf_op jit(solution)/shard_map/scan_backward/pallas_call | solution.py:318
  625.7 5.7 fusion
  632.1 4.5 fusion.112
  639.8 5.5 collective-permute-done.51
  646.8 6.4 collective-permute-done.53
  658.6 7.0 multiply_reduce_fusion.1
  668.6 6.9 collective-permute-done.54
  679.0 7.0 fusion.1
  691.9 9.1 %collective-permute-done.58 = bf16[128,2048]{1,0:T(8,128)(2,1)S(1)} collective-permute-done((bf16[128,2048]{1,0:T(8,128)(2,1)S(1)}, bf16[128,2048]{1,0:T(8,128)(2,1)S(1)}, u32[]{:S(2)}, u32[]{:S(2)}) %collective-permute-start.58) | collective-permute-done | bytes 524320 | tf_op jit(solution)/shard_map/ppermute | solution.py:41
  702.6 10.2 %collective-permute-done.57 = bf16[128,2048]{1,0:T(8,128)(2,1)S(1)} collective-permute-done((bf16[128,2048]{1,0:T(8,128)(2,1)S(1)}, bf16[128,2048]{1,0:T(8,128)(2,1)S(1)}, u32[]{:S(2)}, u32[]{:S(2)}) %collective-permute-start.57) | collective-permute-done | bytes 524320 | tf_op jit(solution)/shard_map/ppermute | solution.py:41
  724.0 14.5 %reduce-scatter.9.cloned.1.call-done = bf16[256,2048]{1,0:T(8,128)(2,1)} async-done(((bf16[1024,2048]{1,0:T(8,128)(2,1)}), bf16[256,2048]{1,0:T(8,128)(2,1)}) %reduce-scatter.9.cloned.1.call-update) | async-done | bytes 1048592 | tf_op jit(solution)/shard_map/reduce_scatter | solution.py:217
  753.2 19.0 %all-to-all-done.2 = bf16[4,256,512]{2,1,0:T(8,128)(2,1)} async-done(((bf16[4,256,512]{2,1,0:T(8,128)(2,1)}), bf16[4,256,512]{2,1,0:T(8,128)(2,1)}, u32[]{:S(2)}, u32[]{:S(2)}) %all-to-all-start.2) | async-done | bytes 1048608 | tf_op jit(solution)/shard_map/all_to_all | solution.py:167
  772.2 5.3 copy.73
  788.5 5.6 collective-permute-done.63
  803.1 9.5 %collective-permute-done.67 = bf16[171,256]{1,0:T(8,128)(2,1)S(1)} collective-permute-done((bf16[171,256]{1,0:T(8,128)(2,1)S(1)}, bf16[171,256]{1,0:T(8,128)(2,1)S(1)}, u32[]{:S(2)}, u32[]{:S(2)}) %collective-permute-start.67) | collective-permute-done | bytes 87584 | tf_op jit(solution)/shard_map/ppermute | solution.py:41
  816.8 4.6 collective-permute-start.73
  (629 shorter events, 264.2 us)
Async XLA Ops:
  7.2 150.0 %all-gather.4.cloned.1.call-start = ((), (), s32[]{:S(2)}) async-start(), calls=%async_computation.7 | async-start | bytes 14155776 | tf_op jit(solution)/shard_map/all_gather | solution.py:186
  13.3 324.9 %all-gather.8.cloned.1.call-start = ((), (), s32[]{:S(2)}) async-start(), calls=%async_computation.9 | async-start | bytes 18874368 | tf_op jit(solution)/shard_map/all_gather | solution.py:186
  17.4 391.4 %all-gather.6.cloned.1.call-start = ((), (), s32[]{:S(2)}) async-start(), calls=%async_computation.8 | async-start | bytes 9437184 | tf_op jit(solution)/shard_map/all_gather | solution.py:186
  22.7 17.3 %collective-permute-start.5 = (f32[1,27,256]{2,1,0:T(8,128)S(1)}, f32[1,27,256]{2,1,0:T(8,128)S(1)}, u32[]{:S(2)}, u32[]{:S(2)}) collective-permute-start(f32[1,27,256]{2,1,0:T(8,128)S(1)} %bitcast.317), channel_id=1, source_target_pairs={{0,3},{1,2},{2,1},{3,0},{4,7},{5,6},{6,5},{7,4},{8,11},{9,10},{10,... | collective-permute-start | bytes 82952 | tf_op jit(solution)/shard_map/ppermute | solution.py:41
  35.5 27.0 %all-to-all-start = ((bf16[4,128,512]{2,1,0:T(8,128)(2,1)}), bf16[4,128,512]{2,1,0:T(8,128)(2,1)S(1)}, u32[]{:S(2)}, u32[]{:S(2)}) async-start(bf16[4,128,512]{2,1,0:T(8,128)(2,1)} %constant_dynamic-update-slice_fusion.14), calls=%async_computation | async-start | bytes 1048576 | tf_op jit(solution)/shard_map/all_to_all | solution.py:149
  62.8 18.9 %collective-permute-start.10 = (bf16[1,144,256]{1,2,0:T(8,128)(2,1)S(1)}, bf16[1,144,256]{1,2,0:T(8,128)(2,1)S(1)}, u32[]{:S(2)}, u32[]{:S(2)}) collective-permute-start(bf16[1,144,256]{1,2,0:T(8,128)(2,1)S(1)} %bitcast.304), channel_id=1, source_target_pairs={{0,1},{1,0},{2,3},{3,2},{4,5},{5,4},{6,7},{7,6},{8,9},{9,8},{10,11... | collective-permute-start | bytes 221192 | tf_op jit(solution)/shard_map/ppermute | solution.py:41
  62.9 18.9 %collective-permute-start.11 = (bf16[1,144,256]{1,2,0:T(8,128)(2,1)S(1)}, bf16[1,144,256]{1,2,0:T(8,128)(2,1)S(1)}, u32[]{:S(2)}, u32[]{:S(2)}) collective-permute-start(bf16[1,144,256]{1,2,0:T(8,128)(2,1)S(1)} %bitcast.305), channel_id=1, source_target_pairs={{0,2},{1,3},{2,0},{3,1},{4,6},{5,7},{6,4},{7,5},{8,10},{9,11},{10,... | collective-permute-start | bytes 221192 | tf_op jit(solution)/shard_map/ppermute | solution.py:41
  62.9 18.8 %collective-permute-start.12 = (bf16[1,144,256]{1,2,0:T(8,128)(2,1)S(1)}, bf16[1,144,256]{1,2,0:T(8,128)(2,1)S(1)}, u32[]{:S(2)}, u32[]{:S(2)}) collective-permute-start(bf16[1,144,256]{1,2,0:T(8,128)(2,1)S(1)} %bitcast.306), channel_id=1, source_target_pairs={{0,3},{1,2},{2,1},{3,0},{4,7},{5,6},{6,5},{7,4},{8,11},{9,10},{10,... | collective-permute-start | bytes 221192 | tf_op jit(solution)/shard_map/ppermute | solution.py:41
  81.8 18.9 %collective-permute-start.13 = (bf16[4,144,256]{1,2,0:T(8,128)(2,1)S(1)}, bf16[4,144,256]{1,2,0:T(8,128)(2,1)S(1)}, u32[]{:S(2)}, u32[]{:S(2)}) collective-permute-start(bf16[4,144,256]{1,2,0:T(8,128)(2,1)S(1)} %constant_dynamic-update-slice_fusion.6), channel_id=1, source_target_pairs={{0,16},{16,0},{1,17},{17,1},{2,18},{18,2},{3,19},{19,3},{4,20},{20... | collective-permute-start | bytes 884744 | tf_op jit(solution)/shard_map/ppermute | solution.py:41
  97.9 14.7 %collective-permute-start.8 = (bf16[128,2048]{1,0:T(8,128)(2,1)S(1)}, bf16[128,2048]{1,0:T(8,128)(2,1)S(1)}, u32[]{:S(2)}, u32[]{:S(2)}) collective-permute-start(bf16[128,2048]{1,0:T(8,128)(2,1)S(1)} %fusion.36), channel_id=1, source_target_pairs={{0,12},{4,8},{8,4},{12,0},{1,13},{5,9},{9,5},{13,1},{2,14},{6,10},... | collective-permute-start | bytes 1572872 | tf_op jit(solution)/shard_map/ppermute | solution.py:41
  97.9 24.9 %collective-permute-start.7 = (bf16[128,2048]{1,0:T(8,128)(2,1)S(1)}, bf16[128,2048]{1,0:T(8,128)(2,1)S(1)}, u32[]{:S(2)}, u32[]{:S(2)}) collective-permute-start(bf16[128,2048]{1,0:T(8,128)(2,1)S(1)} %fusion.36), channel_id=1, source_target_pairs={{0,8},{4,12},{8,0},{12,4},{1,9},{5,13},{9,1},{13,5},{2,10},{6,14},... | collective-permute-start | bytes 1572872 | tf_op jit(solution)/shard_map/ppermute | solution.py:41
  98.0 25.7 %collective-permute-start.6 = (bf16[128,2048]{1,0:T(8,128)(2,1)S(1)}, bf16[128,2048]{1,0:T(8,128)(2,1)}, u32[]{:S(2)}, u32[]{:S(2)}) collective-permute-start(bf16[128,2048]{1,0:T(8,128)(2,1)S(1)} %fusion.36), channel_id=1, source_target_pairs={{0,4},{4,0},{8,12},{12,8},{1,5},{5,1},{9,13},{13,9},{2,6},{6,2},{1... | collective-permute-start | bytes 1572872 | tf_op jit(solution)/shard_map/ppermute | solution.py:41
  178.7 94.3 %collective-permute-start.19 = (bf16[1,128,512]{2,1,0:T(8,128)(2,1)}, bf16[1,128,512]{2,1,0:T(8,128)(2,1)S(1)}, u32[]{:S(2)}, u32[]{:S(2)}) collective-permute-start(bf16[1,128,512]{2,1,0:T(8,128)(2,1)} %get-tuple-element.262), channel_id=1, source_target_pairs={{0,12},{4,8},{8,4},{12,0},{1,13},{5,9},{9,5},{13,1},{2,14},{6,10},... | collective-permute-start | bytes 393224 | tf_op jit(solution)/shard_map/ppermute | solution.py:41
  181.2 14.6 %collective-permute-start.16 = (f32[512,160]{0,1:T(8,128)S(1)}, f32[512,160]{0,1:T(8,128)S(1)}, u32[]{:S(2)}, u32[]{:S(2)}) collective-permute-start(f32[512,160]{0,1:T(8,128)S(1)} %fusion.133), channel_id=1, source_target_pairs={{0,12},{4,8},{8,4},{12,0},{1,13},{5,9},{9,5},{13,1},{2,14},{6,10},... | collective-permute-start | bytes 983048 | tf_op jit(solution)/shard_map/ppermute | solution.py:41
  198.6 28.9 %collective-permute-start.23 = (f32[1,1024]{1,0:T(1,128)S(1)}, f32[1,1024]{1,0:T(1,128)S(1)}, u32[]{:S(2)}, u32[]{:S(2)}) collective-permute-start(f32[1,1024]{1,0:T(1,128)S(1)} %bitcast.362), channel_id=1, source_target_pairs={{0,2},{1,3},{4,6},{5,7},{8,10},{9,11},{12,14},{13,15},{16,18},{17,... | collective-permute-start | bytes 12296 | tf_op jit(solution)/shard_map/ppermute | solution.py:49
  271.6 19.9 %collective-permute-start.28 = (bf16[128,2048]{1,0:T(8,128)(2,1)}, bf16[128,2048]{1,0:T(8,128)(2,1)S(1)}, u32[]{:S(2)}, u32[]{:S(2)}) collective-permute-start(bf16[128,2048]{1,0:T(8,128)(2,1)} %get-tuple-element.235), channel_id=1, source_target_pairs={{0,8},{4,12},{8,0},{12,4},{1,9},{5,13},{9,1},{13,5},{2,10},{6,14},... | collective-permute-start | bytes 1572872 | tf_op jit(solution)/shard_map/ppermute | solution.py:41
  272.7 18.8 %collective-permute-start.27 = (bf16[128,2048]{1,0:T(8,128)(2,1)}, bf16[128,2048]{1,0:T(8,128)(2,1)}, u32[]{:S(2)}, u32[]{:S(2)}) collective-permute-start(bf16[128,2048]{1,0:T(8,128)(2,1)} %get-tuple-element.233), channel_id=1, source_target_pairs={{0,4},{4,0},{8,12},{12,8},{1,5},{5,1},{9,13},{13,9},{2,6},{6,2},{1... | collective-permute-start | bytes 1572872 | tf_op jit(solution)/shard_map/ppermute | solution.py:41
  273.7 26.4 %all-to-all-start.1 = ((bf16[4,128,512]{2,1,0:T(8,128)(2,1)}), bf16[4,128,512]{2,1,0:T(8,128)(2,1)S(1)}, u32[]{:S(2)}, u32[]{:S(2)}) async-start(bf16[4,128,512]{2,1,0:T(8,128)(2,1)} %constant_dynamic-update-slice_fusion.3), calls=%async_computation.1 | async-start | bytes 1048576 | tf_op jit(solution)/shard_map/all_to_all | solution.py:149
  277.1 230.9 %reduce-scatter.5.cloned.1.call-start = ((), (), s32[]{:S(2)}) async-start(), calls=%async_computation.10 | async-start | bytes 5242880 | tf_op jit(solution)/shard_map/reduce_scatter | solution.py:217
  303.1 19.9 %collective-permute-start.35 = (bf16[128,2048]{1,0:T(8,128)(2,1)S(1)}, bf16[128,2048]{1,0:T(8,128)(2,1)S(1)}, u32[]{:S(2)}, u32[]{:S(2)}) collective-permute-start(bf16[128,2048]{1,0:T(8,128)(2,1)S(1)} %multiply_convert_fusion.7), channel_id=1, source_target_pairs={{0,12},{4,8},{8,4},{12,0},{1,13},{5,9},{9,5},{13,1},{2,14},{6,10},... | collective-permute-start | bytes 1572872 | tf_op jit(solution)/shard_map/ppermute | solution.py:41
  305.2 32.2 %collective-permute-start.34 = (bf16[128,2048]{1,0:T(8,128)(2,1)S(1)}, bf16[128,2048]{1,0:T(8,128)(2,1)S(1)}, u32[]{:S(2)}, u32[]{:S(2)}) collective-permute-start(bf16[128,2048]{1,0:T(8,128)(2,1)S(1)} %multiply_convert_fusion.7), channel_id=1, source_target_pairs={{0,8},{4,12},{8,0},{12,4},{1,9},{5,13},{9,1},{13,5},{2,10},{6,14},... | collective-permute-start | bytes 1572872 | tf_op jit(solution)/shard_map/ppermute | solution.py:41
  309.6 28.6 %collective-permute-start.33 = (bf16[128,2048]{1,0:T(8,128)(2,1)S(1)}, bf16[128,2048]{1,0:T(8,128)(2,1)}, u32[]{:S(2)}, u32[]{:S(2)}) collective-permute-start(bf16[128,2048]{1,0:T(8,128)(2,1)S(1)} %multiply_convert_fusion.7), channel_id=1, source_target_pairs={{0,4},{4,0},{8,12},{12,8},{1,5},{5,1},{9,13},{13,9},{2,6},{6,2},{1... | collective-permute-start | bytes 1572872 | tf_op jit(solution)/shard_map/ppermute | solution.py:41
  356.3 18.7 %collective-permute-start.36 = (bf16[1024,2048]{1,0:T(8,128)(2,1)S(1)}, bf16[1024,2048]{1,0:T(8,128)(2,1)S(1)}, u32[]{:S(2)}, u32[]{:S(2)}) collective-permute-start(bf16[1024,2048]{1,0:T(8,128)(2,1)S(1)} %convolution_convert_fusion.1), channel_id=1, source_target_pairs={{0,16},{16,0},{1,17},{17,1},{2,18},{18,2},{3,19},{19,3},{4,20},{20... | collective-permute-start | bytes 12582920 | tf_op jit(solution)/shard_map/ppermute | solution.py:41
  433.0 18.1 %collective-permute-start.37 = (bf16[1024,4096]{1,0:T(8,128)(2,1)}, bf16[1024,4096]{1,0:T(8,128)(2,1)}, u32[]{:S(2)}, u32[]{:S(2)}) collective-permute-start(bf16[1024,4096]{1,0:T(8,128)(2,1)} %convolution_convert_fusion), channel_id=1, source_target_pairs={{0,16},{16,0},{1,17},{17,1},{2,18},{18,2},{3,19},{19,3},{4,20},{20... | collective-permute-start | bytes 25165832 | tf_op jit(solution)/shard_map/ppermute | solution.py:41
  433.3 223.9 %reduce-scatter.7.cloned.1.call-start = ((), (), s32[]{:S(2)}) async-start(), calls=%async_computation.11 | async-start | bytes 10485760 | tf_op jit(solution)/shard_map/reduce_scatter | solution.py:217
  461.3 277.2 %reduce-scatter.9.cloned.1.call-start = ((), (), s32[]{:S(2)}) async-start(), calls=%async_computation.12 | async-start | bytes 5242880 | tf_op jit(solution)/shard_map/reduce_scatter | solution.py:217
  466.3 24.0 %collective-permute-start.39 = (bf16[128,2048]{1,0:T(8,128)(2,1)S(1)}, bf16[128,2048]{1,0:T(8,128)(2,1)S(1)}, u32[]{:S(2)}, u32[]{:S(2)}) collective-permute-start(bf16[128,2048]{1,0:T(8,128)(2,1)S(1)} %get-tuple-element.216), channel_id=1, source_target_pairs={{0,8},{4,12},{8,0},{12,4},{1,9},{5,13},{9,1},{13,5},{2,10},{6,14},... | collective-permute-start | bytes 1572872 | tf_op jit(solution)/shard_map/ppermute | solution.py:41
  466.5 23.7 %collective-permute-start.38 = (bf16[128,2048]{1,0:T(8,128)(2,1)S(1)}, bf16[128,2048]{1,0:T(8,128)(2,1)S(1)}, u32[]{:S(2)}, u32[]{:S(2)}) collective-permute-start(bf16[128,2048]{1,0:T(8,128)(2,1)S(1)} %get-tuple-element.214), channel_id=1, source_target_pairs={{0,4},{4,0},{8,12},{12,8},{1,5},{5,1},{9,13},{13,9},{2,6},{6,2},{1... | collective-permute-start | bytes 1572872 | tf_op jit(solution)/shard_map/ppermute | solution.py:41
  510.9 23.9 %collective-permute-start.42 = (bf16[128,2048]{1,0:T(8,128)(2,1)S(1)}, bf16[128,2048]{1,0:T(8,128)(2,1)S(1)}, u32[]{:S(2)}, u32[]{:S(2)}) collective-permute-start(bf16[128,2048]{1,0:T(8,128)(2,1)S(1)} %get-tuple-element.80), channel_id=1, source_target_pairs={{0,8},{4,12},{8,0},{12,4},{1,9},{5,13},{9,1},{13,5},{2,10},{6,14},... | collective-permute-start | bytes 1572872 | tf_op jit(solution)/shard_map/ppermute | solution.py:41
  512.4 22.5 %collective-permute-start.43 = (bf16[128,2048]{1,0:T(8,128)(2,1)S(1)}, bf16[128,2048]{1,0:T(8,128)(2,1)S(1)}, u32[]{:S(2)}, u32[]{:S(2)}) collective-permute-start(bf16[128,2048]{1,0:T(8,128)(2,1)S(1)} %get-tuple-element.80), channel_id=1, source_target_pairs={{0,12},{4,8},{8,4},{12,0},{1,13},{5,9},{9,5},{13,1},{2,14},{6,10},... | collective-permute-start | bytes 1572872 | tf_op jit(solution)/shard_map/ppermute | solution.py:41
  547.8 77.9 %collective-permute-start.47 = (bf16[1024,2048]{1,0:T(8,128)(2,1)S(1)}, bf16[1024,2048]{1,0:T(8,128)(2,1)}, u32[]{:S(2)}, u32[]{:S(2)}) collective-permute-start(bf16[1024,2048]{1,0:T(8,128)(2,1)S(1)} %pad_maximum_fusion.1), channel_id=1, source_target_pairs={{0,16},{16,0},{1,17},{17,1},{2,18},{18,2},{3,19},{19,3},{4,20},{20... | collective-permute-start | bytes 12582920 | tf_op jit(solution)/shard_map/ppermute | solution.py:41
  559.7 21.5 %collective-permute-start.46 = (bf16[16,1024]{1,0:T(8,128)(2,1)S(1)}, bf16[16,1024]{1,0:T(8,128)(2,1)S(1)}, u32[]{:S(2)}, u32[]{:S(2)}) collective-permute-start(bf16[16,1024]{1,0:T(8,128)(2,1)S(1)} %convert_element_type.276), channel_id=1, source_target_pairs={{3,0},{7,4},{11,8},{15,12},{19,16},{23,20},{27,24},{31,28}} | collective-permute-start | bytes 98312 | tf_op jit(solution)/shard_map/ppermute | solution.py:49
  560.9 20.5 %collective-permute-start.45 = (bf16[16,1024]{1,0:T(8,128)(2,1)S(1)}, bf16[16,1024]{1,0:T(8,128)(2,1)S(1)}, u32[]{:S(2)}, u32[]{:S(2)}) collective-permute-start(bf16[16,1024]{1,0:T(8,128)(2,1)S(1)} %convert_element_type.276), channel_id=1, source_target_pairs={{2,0},{3,1},{6,4},{7,5},{10,8},{11,9},{14,12},{15,13},{18,16},{19,... | collective-permute-start | bytes 98312 | tf_op jit(solution)/shard_map/ppermute | solution.py:49
  562.2 23.6 %collective-permute-start.44 = (bf16[16,1024]{1,0:T(8,128)(2,1)S(1)}, bf16[16,1024]{1,0:T(8,128)(2,1)S(1)}, u32[]{:S(2)}, u32[]{:S(2)}) collective-permute-start(bf16[16,1024]{1,0:T(8,128)(2,1)S(1)} %convert_element_type.276), channel_id=1, source_target_pairs={{1,0},{2,1},{3,2},{5,4},{6,5},{7,6},{9,8},{10,9},{11,10},{13,12},{... | collective-permute-start | bytes 98312 | tf_op jit(solution)/shard_map/ppermute | solution.py:49
  579.8 42.8 %collective-permute-start.50 = (bf16[128,2048]{1,0:T(8,128)(2,1)}, bf16[128,2048]{1,0:T(8,128)(2,1)}, u32[]{:S(2)}, u32[]{:S(2)}) collective-permute-start(bf16[128,2048]{1,0:T(8,128)(2,1)} %get-tuple-element.196), channel_id=1, source_target_pairs={{0,12},{4,8},{8,4},{12,0},{1,13},{5,9},{9,5},{13,1},{2,14},{6,10},... | collective-permute-start | bytes 1572872 | tf_op jit(solution)/shard_map/ppermute | solution.py:41
  581.1 41.6 %collective-permute-start.49 = (bf16[128,2048]{1,0:T(8,128)(2,1)}, bf16[128,2048]{1,0:T(8,128)(2,1)}, u32[]{:S(2)}, u32[]{:S(2)}) collective-permute-start(bf16[128,2048]{1,0:T(8,128)(2,1)} %get-tuple-element.197), channel_id=1, source_target_pairs={{0,8},{4,12},{8,0},{12,4},{1,9},{5,13},{9,1},{13,5},{2,10},{6,14},... | collective-permute-start | bytes 1572872 | tf_op jit(solution)/shard_map/ppermute | solution.py:41
  581.4 41.3 %collective-permute-start.48 = (bf16[128,2048]{1,0:T(8,128)(2,1)S(1)}, bf16[128,2048]{1,0:T(8,128)(2,1)}, u32[]{:S(2)}, u32[]{:S(2)}) collective-permute-start(bf16[128,2048]{1,0:T(8,128)(2,1)S(1)} %get-tuple-element.195), channel_id=1, source_target_pairs={{0,4},{4,0},{8,12},{12,8},{1,5},{5,1},{9,13},{13,9},{2,6},{6,2},{1... | collective-permute-start | bytes 1572872 | tf_op jit(solution)/shard_map/ppermute | solution.py:41
  638.8 14.4 %collective-permute-start.53 = (f32[512,160]{0,1:T(8,128)S(1)}, f32[512,160]{0,1:T(8,128)S(1)}, u32[]{:S(2)}, u32[]{:S(2)}) collective-permute-start(f32[512,160]{0,1:T(8,128)S(1)} %pad_maximum_fusion.25), channel_id=1, source_target_pairs={{0,12},{4,8},{8,4},{12,0},{1,13},{5,9},{9,5},{13,1},{2,14},{6,10},... | collective-permute-start | bytes 983048 | tf_op jit(solution)/shard_map/ppermute | solution.py:41
  688.8 24.0 %collective-permute-start.57 = (bf16[128,2048]{1,0:T(8,128)(2,1)S(1)}, bf16[128,2048]{1,0:T(8,128)(2,1)S(1)}, u32[]{:S(2)}, u32[]{:S(2)}) collective-permute-start(bf16[128,2048]{1,0:T(8,128)(2,1)S(1)} %get-tuple-element.194), channel_id=1, source_target_pairs={{0,8},{4,12},{8,0},{12,4},{1,9},{5,13},{9,1},{13,5},{2,10},{6,14},... | collective-permute-start | bytes 1572872 | tf_op jit(solution)/shard_map/ppermute | solution.py:41
  689.0 23.7 %collective-permute-start.56 = (bf16[128,2048]{1,0:T(8,128)(2,1)S(1)}, bf16[128,2048]{1,0:T(8,128)(2,1)S(1)}, u32[]{:S(2)}, u32[]{:S(2)}) collective-permute-start(bf16[128,2048]{1,0:T(8,128)(2,1)S(1)} %get-tuple-element.192), channel_id=1, source_target_pairs={{0,4},{4,0},{8,12},{12,8},{1,5},{5,1},{9,13},{13,9},{2,6},{6,2},{1... | collective-permute-start | bytes 1572872 | tf_op jit(solution)/shard_map/ppermute | solution.py:41
  689.3 27.9 %collective-permute-start.59 = (bf16[256,4096]{1,0:T(8,128)(2,1)S(1)}, bf16[256,4096]{1,0:T(8,128)(2,1)S(1)}, u32[]{:S(2)}, u32[]{:S(2)}) collective-permute-start(bf16[256,4096]{1,0:T(8,128)(2,1)S(1)} %copy-done.19), channel_id=1, source_target_pairs={{0,16},{16,0},{1,17},{17,1},{2,18},{18,2},{3,19},{19,3},{4,20},{20... | collective-permute-start | bytes 6291464 | tf_op jit(solution)/shard_map/ppermute | solution.py:41
  690.4 24.2 %collective-permute-start.60 = (bf16[256,2048]{1,0:T(8,128)(2,1)S(1)}, bf16[256,2048]{1,0:T(8,128)(2,1)S(1)}, u32[]{:S(2)}, u32[]{:S(2)}) collective-permute-start(bf16[256,2048]{1,0:T(8,128)(2,1)S(1)} %copy-done.28), channel_id=1, source_target_pairs={{0,16},{16,0},{1,17},{17,1},{2,18},{18,2},{3,19},{19,3},{4,20},{20... | collective-permute-start | bytes 3145736 | tf_op jit(solution)/shard_map/ppermute | solution.py:41
  701.0 20.3 %collective-permute-start.55 = (bf16[1024,1024]{1,0:T(8,128)(2,1)S(1)}, bf16[1024,1024]{1,0:T(8,128)(2,1)S(1)}, u32[]{:S(2)}, u32[]{:S(2)}) collective-permute-start(bf16[1024,1024]{1,0:T(8,128)(2,1)S(1)} %convolution_convert_fusion.2), channel_id=1, source_target_pairs={{0,16},{16,0},{1,17},{17,1},{2,18},{18,2},{3,19},{19,3},{4,20},{20... | collective-permute-start | bytes 6291464 | tf_op jit(solution)/shard_map/ppermute | solution.py:41
  741.9 30.2 %all-to-all-start.2 = ((bf16[4,256,512]{2,1,0:T(8,128)(2,1)}), bf16[4,256,512]{2,1,0:T(8,128)(2,1)}, u32[]{:S(2)}, u32[]{:S(2)}) async-start(bf16[4,256,512]{2,1,0:T(8,128)(2,1)} %pad_maximum_fusion.22), calls=%async_computation.5 | async-start | bytes 2097152 | tf_op jit(solution)/shard_map/all_to_all | solution.py:167
  746.2 75.1 %reduce-scatter.11.cloned.1.call-start = ((), (), s32[]{:S(2)}) async-start(), calls=%async_computation.13 | async-start | bytes 2621440 | tf_op jit(solution)/shard_map/reduce_scatter | solution.py:217
  752.0 25.5 %collective-permute-start.71 = (bf16[256,2048]{1,0:T(8,128)(2,1)}, bf16[256,2048]{1,0:T(8,128)(2,1)S(1)}, u32[]{:S(2)}, u32[]{:S(2)}) collective-permute-start(bf16[256,2048]{1,0:T(8,128)(2,1)} %reduce-scatter.9.cloned.1.call-done), channel_id=1, source_target_pairs={{0,16},{16,0},{1,17},{17,1},{2,18},{18,2},{3,19},{19,3},{4,20},{20... | collective-permute-start | bytes 3145736 | tf_op jit(solution)/shard_map/ppermute | solution.py:41
  795.3 17.3 %collective-permute-start.67 = (bf16[171,256]{1,0:T(8,128)(2,1)S(1)}, bf16[171,256]{1,0:T(8,128)(2,1)S(1)}, u32[]{:S(2)}, u32[]{:S(2)}) collective-permute-start(bf16[171,256]{1,0:T(8,128)(2,1)S(1)} %get-tuple-element.248), channel_id=1, source_target_pairs={{0,2},{1,3},{2,0},{3,1},{4,6},{5,7},{6,4},{7,5},{8,10},{9,11},{10,... | collective-permute-start | bytes 262664 | tf_op jit(solution)/shard_map/ppermute | solution.py:41
  795.3 17.3 %collective-permute-start.66 = (bf16[171,256]{1,0:T(8,128)(2,1)S(1)}, bf16[171,256]{1,0:T(8,128)(2,1)S(1)}, u32[]{:S(2)}, u32[]{:S(2)}) collective-permute-start(bf16[171,256]{1,0:T(8,128)(2,1)S(1)} %get-tuple-element.247), channel_id=1, source_target_pairs={{0,1},{1,0},{2,3},{3,2},{4,5},{5,4},{6,7},{7,6},{8,9},{9,8},{10,11... | collective-permute-start | bytes 262664 | tf_op jit(solution)/shard_map/ppermute | solution.py:41
  (188 other events, 2713.3 us)
Sparse Core Ops, SparseCore 0:
  13.4 143.6 all-gather.3
  158.7 163.7 all-gather.7
  324.7 84.0 all-gather.5
  433.4 74.5 reduce-scatter.4
  510.3 146.8 reduce-scatter.6
  660.0 78.3 reduce-scatter.8
  772.3 48.5 reduce-scatter.10
